TPU v7x, 128 devices: a whole 4x4x4 slice. The times are simulated.
128 devices in a mesh: req: 16 (over x, y), mlp: 8 (over z, core).
Axes of the slice: x: 4, y: 4, z: 4, core: 2. Of those that a mesh axis runs over, the one named last changes fastest.
Arguments:
- tokens: bfloat16 [4096, 2048], P(('req', 'mlp')), may hold values from -6 to 6
- cached_states: float32 [256, 8, 256, 512], P('req', 'mlp'), may hold values from -12 to 12
- prompt_lengths: int32 [256], P('req'), may hold values from 1 to 4096, as said below
- accepted: int32 [256], P('req'), may hold values from 1 to 16, as said below
- owner_slot: int32 [256], P('req'), may hold values from 0 to 255, as said below
- w_query: bfloat16 [2048, 2048], P(None, 'mlp'), may hold values from -0.125 to 0.125
- w_key: bfloat16 [2048, 2048], P(None, 'mlp'), may hold values from -0.125 to 0.125
- w_value: bfloat16 [2048, 4096], P(None, 'mlp'), may hold values from -0.125 to 0.125
- w_gate_ret: bfloat16 [2048, 4096], P(None, 'mlp'), may hold values from -0.125 to 0.125
- w_out: bfloat16 [4096, 2048], P('mlp'), may hold values from -0.09375 to 0.09375
- w_gate: bfloat16 [2048, 4096], P('req', 'mlp'), may hold values from -0.125 to 0.125
- w_up: bfloat16 [2048, 4096], P('req', 'mlp'), may hold values from -0.125 to 0.125
- w_down: bfloat16 [4096, 2048], P('mlp', 'req'), may hold values from -0.09375 to 0.09375
Outputs:
- mixed: bfloat16 [4096, 2048], P(('req', 'mlp'))
- new_states: float32 [256, 8, 256, 512], P('req', 'mlp')
Inputs may be any that keep to these rules, and one draw needn't show every extreme that they name: `prompt_lengths`: request r belongs to tenant k = (4 r) // 256, so the four tenants hold consecutive ranges of 64 requests; its prompt length is drawn evenly from 1 to 4^(k + 3). `accepted`: number of leading drafts of request r that are kept, drawn evenly for each request. A permutation of the requests; for request r on req block i = r // 16, owner_slot[r] = j * 16 + i + c with owner block j and 0 <= c < 1, and each pair (j, c) occurs exactly once within a block.
All inputs are finite; a program needn't handle non-finite values.
Results may differ from a plain program's by a relative error of at most 0.017.
Values may be sent and summed in bfloat16 or wider, within the bound.
No kernel may reach another device: no remote copies, remote signals or barrier semaphores. Data moves between devices by JAX's collectives and lax.ppermute only.
A program may use at most 128 MiB of HBM per device.

v0:
```python
import math

import jax
import jax.numpy as jnp
from jax import lax
from jax.sharding import PartitionSpec as P

DRAFT = 16


epsilon = 1e-05


def layer_norm(inputs):
    average = jnp.mean(inputs, axis=-1, keepdims=True)
    centred = inputs - average
    variance = jnp.mean(centred * centred, axis=-1, keepdims=True)
    return centred * lax.rsqrt(variance + epsilon)


def decays(head_count, first_head):
    head_index = jnp.arange(head_count, dtype=jnp.float32) + first_head
    return 1.0 - jnp.exp2(-5.0 - head_index)


def rotate(inputs, positions):
    half_width = inputs.shape[-1] // 2
    frequencies = jnp.exp(
        -math.log(10000.0) * jnp.arange(half_width, dtype=jnp.float32) / half_width
    )
    angles = positions[:, :, None] * frequencies[None, None, :]
    cosine_part = jnp.cos(angles)[:, :, None, :]
    sine_part = jnp.sin(angles)[:, :, None, :]
    front_half = inputs[..., :half_width]
    back_half = inputs[..., half_width:]
    return jnp.concatenate(
        [
            front_half * cosine_part - back_half * sine_part,
            front_half * sine_part + back_half * cosine_part,
        ],
        axis=-1,
    )


def state_weights(states, accepted, gammas, draft_count):
    draft_pos = jnp.arange(draft_count, dtype=jnp.float32)
    accepted_f = accepted.astype(jnp.float32)
    exponent = accepted_f[:, None, None] - 1.0 - draft_pos[None, None, :]
    draft_weights = jnp.where(
        exponent >= 0, jnp.power(gammas[None, :, None], jnp.maximum(exponent, 0.0)), 0.0
    )
    old_part = jnp.power(gammas[None, :], accepted_f[:, None])[:, :, None, None] * states
    return (old_part, draft_weights)


def fold_update(key_rows, values, draft_weights):
    scaled = key_rows.astype(jnp.float32) * jnp.transpose(draft_weights, (0, 2, 1))[..., None]
    return jnp.einsum(
        "rshd,rshv->rhdv", scaled, values.astype(jnp.float32), precision=lax.Precision.HIGHEST
    )


def retain_outputs(queries, key_rows, values, states, gammas):
    draft_count = queries.shape[1]
    draft_pos = jnp.arange(draft_count, dtype=jnp.float32)
    distance = draft_pos[:, None] - draft_pos[None, :]
    decay_mask = jnp.where(
        distance[None] >= 0, jnp.power(gammas[:, None, None], jnp.maximum(distance, 0.0)[None]), 0.0
    )
    scores = jnp.einsum("rthd,rshd->rhts", queries, key_rows, preferred_element_type=jnp.float32)
    weights = (scores * decay_mask[None]).astype(jnp.bfloat16)
    within = jnp.einsum("rhts,rshv->rthv", weights, values, preferred_element_type=jnp.float32)
    carried = jnp.einsum(
        "rthd,rhdv->rthv", queries.astype(jnp.float32), states, precision=lax.Precision.HIGHEST
    )
    carried = carried * jnp.power(gammas[None, None, :, None], draft_pos[None, :, None, None] + 1.0)
    return within + carried


def per_device(
    tokens,
    cached_states,
    prompt_lengths,
    accepted,
    owner_slot,
    w_query,
    w_key,
    w_value,
    w_gate_ret,
    w_out,
    w_gate,
    w_up,
    w_down,
):
    requests = cached_states.shape[0]
    heads_here = cached_states.shape[1]
    key_width = cached_states.shape[2]
    value_width = cached_states.shape[3]
    draft_count = DRAFT
    per_peer = requests // lax.axis_size("req")
    first_head = (lax.axis_index("mlp") * heads_here).astype(jnp.float32)
    gammas = decays(heads_here, first_head)
    target_pos = owner_slot // requests * per_peer + owner_slot % per_peer
    local_ids = jnp.arange(requests, dtype=jnp.int32)
    send_order = jnp.sum(
        jnp.where(target_pos[None, :] == local_ids[:, None], local_ids[None, :], 0), axis=1
    )
    old_part, draft_weights = state_weights(cached_states, accepted, gammas, draft_count)
    group_rows = lax.all_gather(tokens, "mlp", axis=0, tiled=True)
    row_count = group_rows.shape[0]
    normed = layer_norm(group_rows.astype(jnp.float32)).astype(jnp.bfloat16)
    queries = jnp.dot(normed, w_query, preferred_element_type=jnp.float32).reshape(
        requests, draft_count, heads_here, key_width
    )
    key_rows = (
        jnp.dot(normed, w_key, preferred_element_type=jnp.float32) * (1.0 / math.sqrt(key_width))
    ).reshape(requests, draft_count, heads_here, key_width)
    values = (
        jnp.dot(normed, w_value, preferred_element_type=jnp.float32)
        .astype(jnp.bfloat16)
        .reshape(requests, draft_count, heads_here, value_width)
    )
    gate_ret = jnp.dot(normed, w_gate_ret, preferred_element_type=jnp.float32).reshape(
        requests, draft_count, heads_here, value_width
    )
    positions = (
        prompt_lengths[:, None] + jnp.arange(draft_count, dtype=jnp.int32)[None, :]
    ).astype(jnp.float32)
    rotated_q = rotate(queries, positions).astype(jnp.bfloat16)
    rotated_k = rotate(key_rows, positions).astype(jnp.bfloat16)
    fresh = old_part + fold_update(rotated_k, values, draft_weights)
    new_states = lax.all_to_all(
        jnp.take(fresh, send_order, axis=0).astype(jnp.bfloat16),
        "req",
        split_axis=0,
        concat_axis=0,
        tiled=True,
    ).astype(jnp.float32)
    outputs = retain_outputs(rotated_q, rotated_k, values, cached_states, gammas)
    joined = (
        (layer_norm(outputs) * jax.nn.silu(gate_ret))
        .astype(jnp.bfloat16)
        .reshape(row_count, heads_here * value_width)
    )
    partials = jnp.dot(joined, w_out, preferred_element_type=jnp.float32)
    share = tokens.shape[0]
    summed = lax.psum(partials.astype(jnp.bfloat16), "mlp").astype(jnp.float32)
    residual = group_rows.astype(jnp.float32) + summed
    hidden_in = layer_norm(residual).astype(jnp.bfloat16)
    residual_share = lax.dynamic_slice_in_dim(residual, lax.axis_index("mlp") * share, share, 0)
    gate_sum = jnp.dot(
        hidden_in,
        lax.all_gather(w_gate, "req", axis=0, tiled=True),
        preferred_element_type=jnp.float32,
    )
    up_sum = jnp.dot(
        hidden_in,
        lax.all_gather(w_up, "req", axis=0, tiled=True),
        preferred_element_type=jnp.float32,
    )
    hidden = (jax.nn.silu(gate_sum) * up_sum).astype(jnp.bfloat16)
    down_terms = jnp.dot(
        hidden,
        lax.all_gather(w_down, "req", axis=1, tiled=True),
        preferred_element_type=jnp.float32,
    )
    mixed = (
        residual_share
        + lax.psum_scatter(
            down_terms.astype(jnp.bfloat16), "mlp", scatter_dimension=0, tiled=True
        ).astype(jnp.float32)
    ).astype(jnp.bfloat16)
    return (mixed, new_states)


def solution(mesh):
    return jax.shard_map(
        per_device,
        mesh=mesh,
        in_specs=(
            P(("req", "mlp"), None),
            P("req", "mlp", None, None),
            P("req"),
            P("req"),
            P("req"),
            P(None, "mlp"),
            P(None, "mlp"),
            P(None, "mlp"),
            P(None, "mlp"),
            P("mlp", None),
            P("req", "mlp"),
            P("req", "mlp"),
            P("mlp", "req"),
        ),
        out_specs=(P(("req", "mlp"), None), P("req", "mlp", None, None)),
        check_vma=False,
    )
```

profile of v0, /device:TPU:28, one launch (start us, length us, event | category | flops | bytes accessed | tf_op | source)
XLA Modules:
  0.0 292.3 jit_solution(9923239641830720972)
XLA Ops:
  8.0 0.0 copy-start
  8.0 0.0 copy-start.13
  8.0 0.0 all-gather.5.cloned.1.call-start
  8.1 0.7 all-gather.5.cloned.1.call-update
  8.8 0.0 all-reduce.2.cloned.1.call-start
  8.9 1.3 convert_add_fusion.1
  10.2 0.7 add_convert_fusion.1
  10.9 0.7 power_select_fusion
  11.6 24.6 %all-gather.5.cloned.1.call-done = bf16[256,2048]{1,0:T(8,128)(2,1)} async-done(((bf16[32,2048]{1,0:T(8,128)(2,1)}), bf16[256,2048]{1,0:T(8,128)(2,1)}) %all-gather.5.cloned.1.call-update) | async-done | bytes 1048592 | tf_op jit(solution)/shard_map/all_gather | solution.py:109
  36.2 1.6 convert_reduce_fusion
  37.9 0.0 copy-start.8
  37.9 2.0 fusion.7
  39.8 0.0 copy-done.13
  39.8 0.0 copy-start.10
  39.9 1.7 fusion.62
  41.6 2.0 convolution_multiply_fusion.1
  43.6 0.6 fusion.46
  44.2 0.0 copy-start.5
  44.2 0.0 copy-start.6
  44.3 0.6 copy-done.5
  44.9 0.0 copy-done.6
  44.9 0.0 copy-done.1
  44.9 3.7 %fusion.14 = f32[16,1,512,16]{2,3,0,1:T(8,128)} fusion(f32[16,1,256,512]{3,2,1,0:T(8,128)S(1)} %copy-done.1, f32[16]{0:T(128)S(1)} %add_power_fusion, bf16[16,16,128]{2,1,0:T(8,128)(2,1)S(1)} %get-tuple-element.10, bf16[16,16,128]{2,1,0:T(8,128)(2,1)S(1)} %get-tuple-element.11), kind=kOutput, calls=%fused_computation.25 | convolution fusion | flops 403046400 | bytes 9044032 | tf_op jit(solution)/shard_map/rthd,rhdv->rthv/dot_general | solution.py:73
  48.6 0.0 copy-done.8
  48.6 0.0 copy-done.10
  48.6 0.0 copy-done.2
  48.6 0.0 copy-done.12
  48.6 0.8 convolution_convert_fusion.2
  49.3 2.2 fusion.65
  51.6 1.2 multiply_reduce_fusion.1
  52.8 0.0 copy-start.3
  52.8 2.4 fusion.59
  55.3 0.0 copy-done.3
  55.3 0.2 multiply_convert_fusion.1
  55.5 0.0 copy-start.14
  55.6 1.7 convolution_convert_fusion.1
  57.3 0.0 all-reduce.2.cloned.1.call-update
  57.3 0.0 all-gather.7.cloned.1.call-start
  57.3 0.5 all-gather.7.cloned.1.call-update
  57.9 0.0 all-gather.9.cloned.1.call-start
  57.9 0.5 all-gather.9.cloned.1.call-update
  58.5 0.0 all-gather.11.cloned.1.call-start
  58.5 0.5 all-gather.11.cloned.1.call-update
  59.1 0.1 select_reduce_fusion
  59.2 0.5 compare_and_fusion
  59.7 8.5 %fusion.1 = bf16[16,256,512]{2,1,0:T(8,128)(2,1)} fusion(f32[16,1,256,512]{3,2,1,0:T(8,128)} %param.14, f32[16]{0:T(128)S(1)} %copy-done.9, bf16[16,16,512]{2,1,0:T(8,128)(2,1)S(1)} %bitcast.68, f32[16,16]{1,0:T(8,128)S(1)} %copy-done.7, bf16[16,16,128]{2,1,0:T(8,128)(2,1)S(1)} %get-tuple-element.7, bf16[16,16,128]{2,1,0:T(8,128)(2,1)S(1)} %get-tuple-element.6), kind=kOutput, calls=%fused_computation.4 | convolution fusion | flops 409272320 | bytes 12977216 | tf_op jit(solution)/shard_map/rshd,rshv->rhdv/dot_general | solution.py:58
  68.3 5.1 %gather_fusion = bf16[16,256,512]{2,1,0:T(8,128)(2,1)} fusion(bf16[16,256,512]{2,1,0:T(8,128)(2,1)} %fusion.1, s32[1024]{0:T(1024)S(1)} %pad_clamp_fusion), kind=kCustom, calls=%fused_computation | custom fusion | bytes 8388672 | tf_op jit(solution)/shard_map/jit(_take)/gather | solution.py:133
  73.3 5.5 %fusion.4 = bf16[16,1,256,512]{3,2,1,0:T(8,128)(2,1)} fusion(bf16[16,256,512]{2,1,0:T(8,128)(2,1)} %gather_fusion, pred[16]{0:T(512)(128)(4,1)S(1)} %copy-done.11), kind=kLoop, calls=%fused_computation.8 | loop fusion | flops 2097152 | bytes 8388624 | tf_op jit(solution)/shard_map/convert_element_type | solution.py:133
  78.8 7.2 %all-to-all-start = ((bf16[16,1,256,512]{3,2,1,0:T(8,128)(2,1)}), bf16[16,1,256,512]{3,2,1,0:T(8,128)(2,1)}, u32[]{:S(2)}, u32[]{:S(2)}) async-start(bf16[16,1,256,512]{3,2,1,0:T(8,128)(2,1)} %fusion.4), calls=%async_computation.1 | async-start | bytes 8388608 | tf_op jit(solution)/shard_map/all_to_all | solution.py:132
  86.0 0.2 reduce-scatter.2.cloned.1.call-start
  86.3 34.8 %all-reduce.2.cloned.1.call-done = bf16[256,2048]{1,0:T(8,128)(2,1)} async-done(((bf16[256,2048]{1,0:T(8,128)(2,1)}), bf16[256,2048]{1,0:T(8,128)(2,1)}) %all-reduce.2.cloned.1.call-update) | async-done | bytes 1048592 | tf_op jit(solution)/shard_map/psum | solution.py:147
  121.1 2.9 convert_add_fusion
  124.0 0.0 copy-done.4
  124.0 0.5 multiply_reduce_fusion
  124.6 21.7 %all-gather.7.cloned.1.call-done = bf16[2048,512]{1,0:T(8,128)(2,1)} async-done(((bf16[128,512]{1,0:T(8,128)(2,1)}), bf16[2048,512]{1,0:T(8,128)(2,1)}) %all-gather.7.cloned.1.call-update) | async-done | bytes 2097168 | tf_op jit(solution)/shard_map/all_gather | solution.py:153
  146.2 3.5 %fusion.58 = f32[256,512]{1,0:T(8,128)} fusion(bf16[2048,512]{1,0:T(8,128)(2,1)} %all-gather.7.cloned.1.call-done, f32[256]{0:T(256)S(1)} %add_rsqrt_fusion.1, f32[256]{0:T(256)S(1)} %broadcast_multiply_fusion.1, bf16[256,2048]{1,0:T(8,128)(2,1)} %all-reduce.2.cloned.1.call-done, bf16[256,2048]{1,0:T(8,128)(2,1)S(1)} %copy-done.2), kind=kOutput, calls=%fused_computation.101 | convolution fusion | flops 540016640 | bytes 4720640 | tf_op jit(solution)/shard_map/dot_general | solution.py:151
  149.7 46.3 %all-gather.9.cloned.1.call-done = bf16[2048,512]{1,0:T(8,128)(2,1)} async-done(((bf16[128,512]{1,0:T(8,128)(2,1)}), bf16[2048,512]{1,0:T(8,128)(2,1)}) %all-gather.9.cloned.1.call-update) | async-done | bytes 2097168 | tf_op jit(solution)/shard_map/all_gather | solution.py:158
  196.1 48.4 %all-gather.11.cloned.1.call-done = bf16[512,2048]{1,0:T(8,128)(2,1)} async-done(((bf16[512,128]{1,0:T(8,128)(2,1)}), bf16[512,2048]{1,0:T(8,128)(2,1)}) %all-gather.11.cloned.1.call-update) | async-done | bytes 2097168 | tf_op jit(solution)/shard_map/all_gather | solution.py:164
  244.5 5.2 %convolution_convert_fusion = bf16[256,2048]{1,0:T(8,128)(2,1)} fusion(bf16[512,2048]{1,0:T(8,128)(2,1)} %all-gather.11.cloned.1.call-done, bf16[2048,512]{1,0:T(8,128)(2,1)} %all-gather.9.cloned.1.call-done, f32[256,512]{1,0:T(8,128)} %fusion.58, f32[256]{0:T(256)S(1)} %add_rsqrt_fusion.1, f32[256]{0:T(256)S(1)} %broadcast_multiply_fusion.1, ...), kind=kOutput, calls=%fused_computation.12 | convolution fusion | flops 1078198272 | bytes 7866368 | tf_op jit(solution)/shard_map/dot_general | solution.py:162
  249.7 0.0 reduce-scatter.2.cloned.1.call-update
  249.7 0.0 all-to-all-done
  249.8 6.7 %convert_element_type.101 = f32[16,1,256,512]{3,2,1,0:T(8,128)} convert(bf16[16,1,256,512]{3,2,1,0:T(8,128)(2,1)} %all-to-all-done) | non-fusion elementwise | flops 2097152 | bytes 12582912 | tf_op jit(solution)/shard_map/convert_element_type | solution.py:138
  256.5 26.8 %reduce-scatter.2.cloned.1.call-done = bf16[32,2048]{1,0:T(8,128)(2,1)} async-done(((bf16[256,2048]{1,0:T(8,128)(2,1)}), bf16[32,2048]{1,0:T(8,128)(2,1)}) %reduce-scatter.2.cloned.1.call-update) | async-done | bytes 131088 | tf_op jit(solution)/shard_map/reduce_scatter | solution.py:169
  283.3 1.7 add_convert_fusion
  (23 shorter events, 0.1 us)
Async XLA Ops:
  8.0 47.5 %copy-start = (bf16[512,2048]{1,0:T(8,128)(2,1)S(1)}, bf16[512,2048]{1,0:T(8,128)(2,1)}, u32[]{:S(2)}) copy-start(bf16[512,2048]{1,0:T(8,128)(2,1)} %param.22) | copy-start | bytes 6291460
  8.0 31.8 %copy-start.13 = (bf16[2048,256]{1,0:T(8,128)(2,1)S(1)}, bf16[2048,256]{1,0:T(8,128)(2,1)}, u32[]{:S(2)}) copy-start(bf16[2048,256]{1,0:T(8,128)(2,1)} %param.18) | copy-start | bytes 3145732
  8.0 28.2 %all-gather.5.cloned.1.call-start = ((), (), s32[]{:S(2)}) async-start(), calls=%async_computation.2 | async-start | bytes 1179648 | tf_op jit(solution)/shard_map/all_gather | solution.py:109
  8.8 112.3 %all-reduce.2.cloned.1.call-start = ((), (), s32[]{:S(2)}) async-start(), calls=%async_computation.3 | async-start | bytes 2097152 | tf_op jit(solution)/shard_map/psum | solution.py:147
  36.2 8.6 %copy-start.1 = (f32[16,1,256,512]{3,2,1,0:T(8,128)S(1)}, f32[16,1,256,512]{3,2,1,0:T(8,128)}, u32[]{:S(2)}) copy-start(f32[16,1,256,512]{3,2,1,0:T(8,128)} %param.14) | copy-start | bytes 25165828
  37.9 10.7 %copy-start.8 = (f32[256]{0:T(256)}, f32[256]{0:T(256)S(1)}, u32[]{:S(2)}) copy-start(f32[256]{0:T(256)S(1)} %broadcast_multiply_fusion.2) | copy-start | bytes 3076
  39.8 8.7 %copy-start.10 = (f32[256]{0:T(256)}, f32[256]{0:T(256)S(1)}, u32[]{:S(2)}) copy-start(f32[256]{0:T(256)S(1)} %add_rsqrt_fusion.2) | copy-start | bytes 3076
  44.2 0.6 copy-start.5
  44.2 0.6 copy-start.6
  44.9 3.7 %copy-start.2 = (bf16[256,2048]{1,0:T(8,128)(2,1)S(1)}, bf16[256,2048]{1,0:T(8,128)(2,1)}, u32[]{:S(2)}) copy-start(bf16[256,2048]{1,0:T(8,128)(2,1)} %all-gather.5.cloned.1.call-done) | copy-start | bytes 3145732
  44.9 3.7 %copy-start.12 = (bf16[2048,512]{1,0:T(8,128)(2,1)S(1)}, bf16[2048,512]{1,0:T(8,128)(2,1)}, u32[]{:S(2)}) copy-start(bf16[2048,512]{1,0:T(8,128)(2,1)} %param.20) | copy-start | bytes 6291460
  52.8 2.4 copy-start.3
  55.5 3.5 %copy-start.14 = (s32[16]{0:T(128)S(1)}, s32[16]{0:T(128)}, u32[]{:S(2)}) copy-start(s32[16]{0:T(128)} %param.17) | copy-start | bytes 196
  55.5 4.2 %copy-start.7 = (f32[16,16]{1,0:T(8,128)S(1)}, f32[16,16]{1,0:T(8,128)}, u32[]{:S(2)}) copy-start(f32[16,16]{1,0:T(8,128)} %get-tuple-element.16) | copy-start | bytes 3076
  55.5 4.2 %copy-start.9 = (f32[16]{0:T(128)S(1)}, f32[16]{0:T(128)}, u32[]{:S(2)}) copy-start(f32[16]{0:T(128)} %get-tuple-element.13) | copy-start | bytes 196
  57.3 88.9 %all-gather.7.cloned.1.call-start = ((), (), s32[]{:S(2)}) async-start(), calls=%async_computation.4 | async-start | bytes 2228224 | tf_op jit(solution)/shard_map/all_gather | solution.py:153
  57.9 138.2 %all-gather.9.cloned.1.call-start = ((), (), s32[]{:S(2)}) async-start(), calls=%async_computation.5 | async-start | bytes 2228224 | tf_op jit(solution)/shard_map/all_gather | solution.py:158
  58.5 186.1 %all-gather.11.cloned.1.call-start = ((), (), s32[]{:S(2)}) async-start(), calls=%async_computation.6 | async-start | bytes 2228224 | tf_op jit(solution)/shard_map/all_gather | solution.py:164
  68.3 5.1 %copy-start.11 = (pred[16]{0:T(512)(128)(4,1)S(1)}, pred[16]{0:T(512)(128)(4,1)}, u32[]{:S(2)}) copy-start(pred[16]{0:T(512)(128)(4,1)} %compare_and_fusion) | copy-start | bytes 52
  78.8 170.9 %all-to-all-start = ((bf16[16,1,256,512]{3,2,1,0:T(8,128)(2,1)}), bf16[16,1,256,512]{3,2,1,0:T(8,128)(2,1)}, u32[]{:S(2)}, u32[]{:S(2)}) async-start(bf16[16,1,256,512]{3,2,1,0:T(8,128)(2,1)} %fusion.4), calls=%async_computation.1 | async-start | bytes 8388608 | tf_op jit(solution)/shard_map/all_to_all | solution.py:132
  86.0 197.2 %reduce-scatter.2.cloned.1.call-start = ((), (), s32[]{:S(2)}) async-start(), calls=%async_computation.7 | async-start | bytes 1179648 | tf_op jit(solution)/shard_map/reduce_scatter | solution.py:169
  121.1 2.9 %copy-start.4 = (bf16[256,2048]{1,0:T(8,128)(2,1)S(1)}, bf16[256,2048]{1,0:T(8,128)(2,1)}, u32[]{:S(2)}) copy-start(bf16[256,2048]{1,0:T(8,128)(2,1)} %all-reduce.2.cloned.1.call-done) | copy-start | bytes 3145732
Sparse Core Ops, SparseCore 0:
  10.6 25.6 all-gather.4
  57.4 63.6 all-reduce.1
  249.9 33.3 reduce-scatter.1
Sparse Core Ops, SparseCore 1:
  59.9 86.3 all-gather.6
  148.2 47.8 all-gather.8
  198.1 46.4 all-gather.10
where the time goes:
time: 293 us; the launch traced here: 292 us
  waiting for transfers between devices  205 us (70%)
  matrix products  31.8 us (11%)
  other arithmetic  26.4 us (9%)
  between operations  15.7 us (5%)
  starting transfers between devices  7.63 us (3%)
  local copies, waits for them, and re-layouts  5.77 us (2%)
    all_gather x1, waiting for transfers between devices, per_device(): lax.all_gather(w_down, 'req', axis=1, tiled=True)  48.4 us
    all_gather x1, waiting for transfers between devices, per_device(): lax.all_gather(w_up, 'req', axis=0, tiled=True)  46.3 us
    psum x1, waiting for transfers between devices, per_device(): summed = lax.psum(partials.astype(jnp.bfloat16), 'mlp').astype(jnp.float32)  34.8 us
    reduce_scatter x1, waiting for transfers between devices, per_device(): lax.psum_scatter(down_terms.astype(jnp.bfloat16), 'mlp', scatter_dimensio...  26.8 us
    all_gather x1, waiting for transfers between devices, per_device(): group_rows = lax.all_gather(tokens, 'mlp', axis=0, tiled=True)  24.6 us
    all_gather x1, waiting for transfers between devices, per_device(): lax.all_gather(w_gate, 'req', axis=0, tiled=True)  21.7 us
    dot_general x1, matrix products, fold_update(): jnp.einsum('rshd,rshv->rhdv', scaled, values.astype(jnp.float32), precisi...  8.55 us
    all_to_all x1, starting transfers between devices, per_device(): lax.all_to_all(jnp.take(fresh, send_order, axis=0).astype(jnp.bfloat16),...  7.21 us
  transfers between devices with their start and end apart: 7, of which 6 were waited for; matrix products, arithmetic and copies ran while one was open for 14% of the time, Pallas kernels for 0%

commit v1 on v0

v1 whole, which is shorter than its diff:
```python
import functools
import math

import jax
import jax.numpy as jnp
from jax import lax
from jax.experimental import pallas as pl
from jax.experimental.pallas import tpu as pltpu
from jax.sharding import PartitionSpec as P

DRAFT = 16
EPS = 1e-05
BF = jnp.bfloat16
F32 = jnp.float32
VM = pl.BlockSpec(memory_space=pltpu.VMEM)
SM = pl.BlockSpec(memory_space=pltpu.SMEM)
ANY = pl.BlockSpec(memory_space=pl.ANY)


def sds(shape, dtype):
    return jax.ShapeDtypeStruct(shape, dtype)


def cost(flops, nbytes):
    return pl.CostEstimate(flops=flops, bytes_accessed=nbytes, transcendentals=0)


def params(mib):
    return pltpu.CompilerParams(vmem_limit_bytes=mib << 20)


def norm(v):
    centred = v - jnp.mean(v, axis=-1, keepdims=True)
    variance = jnp.mean(centred * centred, axis=-1, keepdims=True)
    return centred * lax.rsqrt(variance + EPS)


def norm_kernel(x_ref, o_ref):
    o_ref[...] = norm(x_ref[...].astype(F32)).astype(BF)


def norm_rows(x):
    return pl.pallas_call(
        norm_kernel, out_shape=sds(x.shape, BF), in_specs=[VM], out_specs=VM,
        cost_estimate=cost(x.size * 8, x.size * 4), name="norm_rows",
    )(x)


def pack_kernel(g_ref, u_ref, d_ref, o_ref):
    width = g_ref.shape[1]
    o_ref[:, :width] = g_ref[...]
    o_ref[:, width : 2 * width] = u_ref[...]
    o_ref[:, 2 * width :] = d_ref[...].astype(F32).T.astype(BF)


def pack_weights(g, u, d):
    return pl.pallas_call(
        pack_kernel, out_shape=sds((g.shape[0], 3 * g.shape[1]), BF),
        in_specs=[VM] * 3, out_specs=VM,
        cost_estimate=cost(g.size, g.size * 12), name="pack_weights",
    )(g, u, d)


def pair_kernel(a_ref, b_ref, *o_refs):
    rows = o_refs[0].shape[0]
    for i, o_ref in enumerate(o_refs):
        part = pl.ds(i * rows, rows)
        o_ref[...] = (a_ref[part, :].astype(F32) + b_ref[part, :].astype(F32)).astype(BF)


def pair_sum(a, b, pieces):
    rows = a.shape[0] // pieces
    return pl.pallas_call(
        pair_kernel, out_shape=[sds((rows, a.shape[1]), BF)] * pieces,
        in_specs=[VM] * 2, out_specs=[VM] * pieces,
        cost_estimate=cost(a.size, a.size * 6), name="pair_sum",
    )(a, b)


def residual_kernel(x_ref, a_ref, b_ref, c_ref, d_ref, res_ref, hid_ref):
    total = a_ref[...].astype(F32) + b_ref[...].astype(F32)
    total = total + c_ref[...].astype(F32) + d_ref[...].astype(F32)
    res = x_ref[...].astype(F32) + total
    res_ref[...] = res
    hid_ref[...] = norm(res).astype(BF)


def residual_rows(x, parts):
    return pl.pallas_call(
        residual_kernel, out_shape=[sds(x.shape, F32), sds(x.shape, BF)],
        in_specs=[VM] * 5, out_specs=[VM] * 2,
        cost_estimate=cost(x.size * 12, x.size * 16), name="residual_rows",
    )(x, *parts)


def final_kernel(x_ref, a_ref, b_ref, c_ref, d_ref, o_ref):
    total = a_ref[...].astype(F32) + b_ref[...].astype(F32)
    total = total + c_ref[...].astype(F32) + d_ref[...].astype(F32)
    o_ref[...] = (x_ref[...] + total).astype(BF)


def final_rows(x, parts):
    return pl.pallas_call(
        final_kernel, out_shape=sds(x.shape, BF),
        in_specs=[VM] * 5, out_specs=VM,
        cost_estimate=cost(x.size * 6, x.size * 14), name="final_rows",
    )(x, *parts)


def retention_kernel(
    order, *refs, rows_in, key_width, value_width
):
    xs = refs[:8]
    cos_h, sin_h, mask_h, grow_h, wq_h, wk_h, wv_h, wg_h, wo_h, st_h = refs[8:18]
    same_ref, other_ref, k_ref, v_ref = refs[18:22]
    xbuf, cosb, sinb, maskb, growb, wbuf, wob, stb, proj, keep, joined, sems = refs[22:]
    tile = key_width
    copies = []

    def send(src, dst):
        copy = pltpu.make_async_copy(src, dst, sems.at[len(copies)])
        copy.start()
        copies.append(copy)
        return copy

    c_x = [send(x, xbuf.at[pl.ds(i * rows_in, rows_in), :]) for i, x in enumerate(xs)]
    c_w = [send(wk_h, wbuf.at[0]), send(wq_h, wbuf.at[1])]
    c_small = [send(cos_h, cosb), send(sin_h, sinb), send(mask_h, maskb), send(grow_h, growb)]
    for w in (wv_h, wg_h):
        for j in range(value_width // tile):
            c_w.append(send(w.at[:, pl.ds(j * tile, tile)], wbuf.at[len(c_w)]))
    c_s = [send(st_h.at[order[i]], stb.at[i]) for i in range(16)]
    c_o = send(wo_h, wob)
    for c in c_x:
        c.wait()

    x = xbuf[...]

    def project(j):
        c_w[j].wait()
        return jnp.dot(x, wbuf[j], preferred_element_type=F32)

    half = key_width // 2
    key = project(0) * (1.0 / math.sqrt(key_width))
    for c in c_small:
        c.wait()
    cosv, sinv = cosb[...], sinb[...]

    def rotate(u):
        front, back = u[:, :half], u[:, half:]
        return jnp.concatenate(
            [front * cosv - back * sinv, front * sinv + back * cosv], axis=1
        ).astype(BF)

    rk = rotate(key)
    k_ref[...] = rk
    rq = rotate(project(1))
    scores = lax.dot_general(rq, rk, (((1,), (1,)), ((), ())), preferred_element_type=F32)
    weights = (scores * maskb[...]).astype(BF)
    keep[...] = rq
    for j in range(2):
        val = project(2 + j).astype(BF)
        v_ref[:, j * tile : (j + 1) * tile] = val
        proj[:, j * tile : (j + 1) * tile] = jnp.dot(weights, val, preferred_element_type=F32)
    gates = [project(4), project(5)]
    for c in c_s:
        c.wait()
    for i in range(16):
        part = pl.ds(i * DRAFT, DRAFT)
        carried = jnp.dot(keep[part, :], stb[i].astype(BF), preferred_element_type=F32)
        proj[part, :] += carried * growb[part, :]
    normed = norm(proj[...])
    for j in range(2):
        g = gates[j]
        act = g / (1.0 + jnp.exp(-g))
        joined[:, j * tile : (j + 1) * tile] = (
            normed[:, j * tile : (j + 1) * tile] * act
        ).astype(BF)
    c_o.wait()
    rows = joined.shape[0] // 2
    both = joined[...]
    for j in range(wob.shape[1] // 512):
        cols = pl.ds(j * 512, 512)
        out = jnp.dot(both, wob[:, cols], preferred_element_type=F32).astype(BF)
        same_ref[:, cols] = out[:rows]
        other_ref[:, cols] = out[rows:]


def retention(order, xs, cosv, sinv, mask, grow, wq, wk, wv, wg, wo, states):
    rows_in, width = xs[0].shape
    rows = rows_in * 8
    key_width, value_width = wq.shape[1], wv.shape[1]
    body = functools.partial(
        retention_kernel, rows_in=rows_in, key_width=key_width, value_width=value_width
    )
    tiles = (2 * key_width + 2 * value_width) // key_width
    return pl.pallas_call(
        body,
        out_shape=[
            sds((rows // 2, width), BF), sds((rows // 2, width), BF),
            sds((rows, key_width), BF), sds((rows, value_width), BF),
        ],
        in_specs=[SM] + [ANY] * 18,
        out_specs=[VM] * 4,
        scratch_shapes=[
            pltpu.VMEM((rows, width), BF),
            pltpu.VMEM(cosv.shape, F32), pltpu.VMEM(sinv.shape, F32),
            pltpu.VMEM(mask.shape, F32), pltpu.VMEM(grow.shape, F32),
            pltpu.VMEM((tiles, width, key_width), BF),
            pltpu.VMEM(wo.shape, BF),
            pltpu.VMEM(states.shape, F32),
            pltpu.VMEM((rows, value_width), F32),
            pltpu.VMEM((rows, key_width), BF),
            pltpu.VMEM((rows, value_width), BF),
            pltpu.SemaphoreType.DMA((36,)),
        ],
        compiler_params=params(48),
        cost_estimate=cost(2 * rows * width * 2048, 20 << 20),
        name="retention",
    )(order, *xs, cosv, sinv, mask, grow, wq, wk, wv, wg, wo, states)


def fresh_kernel(src, rel, old, st_ref, k_ref, v_ref, dw_ref, o_ref):
    i = pl.program_id(0)
    scaled = (k_ref[...].astype(F32) * dw_ref[...]).astype(BF)
    update = lax.dot_general(
        scaled, v_ref[...], (((0,), (0,)), ((), ())), preferred_element_type=F32
    )
    o_ref[0] = (old[src[i]] * st_ref[0] + update).astype(BF)


def fresh_states(src, rel, old, states, k, v, dw):
    n, key_width, value_width = states.shape
    return pl.pallas_call(
        fresh_kernel,
        grid_spec=pltpu.PrefetchScalarGridSpec(
            num_scalar_prefetch=3,
            grid=(n,),
            in_specs=[
                pl.BlockSpec((1, key_width, value_width), lambda i, s, r, o: (s[i], 0, 0)),
                pl.BlockSpec((DRAFT, key_width), lambda i, s, r, o: (r[i], 0)),
                pl.BlockSpec((DRAFT, value_width), lambda i, s, r, o: (r[i], 0)),
                pl.BlockSpec((DRAFT, key_width), lambda i, s, r, o: (s[i], 0)),
            ],
            out_specs=pl.BlockSpec((1, key_width, value_width), lambda i, s, r, o: (i, 0, 0)),
        ),
        out_shape=sds(states.shape, BF),
        cost_estimate=cost(2 * states.size * DRAFT, states.size * 6),
        name="fresh_states",
    )(src, rel, old, states, k, v, dw)


def widen_kernel(x_ref, o_ref):
    o_ref[...] = x_ref[...].astype(F32)


def widen(x):
    n = x.shape[0]
    block = (2,) + x.shape[1:]
    return pl.pallas_call(
        widen_kernel, grid=(n // 2,),
        in_specs=[pl.BlockSpec(block, lambda i: (i, 0, 0))],
        out_specs=pl.BlockSpec(block, lambda i: (i, 0, 0)),
        out_shape=sds(x.shape, F32),
        cost_estimate=cost(x.size, x.size * 6), name="widen",
    )(x)


def ffn_kernel(*refs, rows_in):
    xs = refs[:8]
    w_h, same_ref, other_ref, xbuf, wbuf, hid, sems = refs[8:]
    copies = []

    def send(src, dst):
        copy = pltpu.make_async_copy(src, dst, sems.at[len(copies)])
        copy.start()
        copies.append(copy)
        return copy

    c_x = [send(x, xbuf.at[pl.ds(i * rows_in, rows_in), :]) for i, x in enumerate(xs)]
    c_w = []
    for t in (0, 2, 1, 3):
        c_w.append(send(w_h.at[:, pl.ds(t * 256, 256)], wbuf.at[t]))
    c_d = [send(w_h.at[:, pl.ds(1024 + t * 256, 256)], wbuf.at[4 + t]) for t in range(2)]
    for c in c_x:
        c.wait()
    x = xbuf[...]
    for t in range(2):
        c_w[2 * t].wait()
        g = jnp.dot(x, wbuf[t], preferred_element_type=F32)
        c_w[2 * t + 1].wait()
        u = jnp.dot(x, wbuf[2 + t], preferred_element_type=F32)
        hid[t] = (g / (1.0 + jnp.exp(-g)) * u).astype(BF)
    for c in c_d:
        c.wait()
    rows = xbuf.shape[0] // 2
    contract = (((1,), (1,)), ((), ()))
    for j in range(xbuf.shape[1] // 512):
        cols = pl.ds(j * 512, 512)
        out = lax.dot_general(hid[0], wbuf[4, cols, :], contract, preferred_element_type=F32)
        out += lax.dot_general(hid[1], wbuf[5, cols, :], contract, preferred_element_type=F32)
        out = out.astype(BF)
        same_ref[:, cols] = out[:rows]
        other_ref[:, cols] = out[rows:]


def ffn(xs, w):
    rows_in, width = xs[0].shape
    rows = rows_in * 8
    return pl.pallas_call(
        functools.partial(ffn_kernel, rows_in=rows_in),
        out_shape=[sds((rows // 2, width), BF)] * 2,
        in_specs=[ANY] * 9,
        out_specs=[VM] * 2,
        scratch_shapes=[
            pltpu.VMEM((rows, width), BF),
            pltpu.VMEM((6, width, 256), BF),
            pltpu.VMEM((2, rows, 256), BF),
            pltpu.SemaphoreType.DMA((14,)),
        ],
        compiler_params=params(32),
        cost_estimate=cost(2 * rows * width * 1536, 9 << 20),
        name="feed_forward",
    )(*xs, w)


def along(shift):
    return [(z * 2 + c, (z + shift) % 4 * 2 + c) for z in range(4) for c in range(2)]


SWAP = [(m, m ^ 1) for m in range(8)]


def gather_rows(x):
    mine = [x] + [lax.ppermute(x, "mlp", along(s)) for s in (1, 2, 3)]
    return mine + [lax.ppermute(v, "mlp", SWAP) for v in mine]


def reduce_rows(same, other):
    pieces = pair_sum(same, lax.ppermute(other, "mlp", SWAP), 4)
    return [pieces[0]] + [lax.ppermute(pieces[s], "mlp", along(-s)) for s in (1, 2, 3)]


def per_device(
    tokens, cached_states, prompt_lengths, accepted, owner_slot,
    w_query, w_key, w_value, w_gate_ret, w_out, w_gate, w_up, w_down,
):
    requests, _, key_width, value_width = cached_states.shape
    states = cached_states.reshape(requests, key_width, value_width)
    w_all = lax.all_gather(pack_weights(w_gate, w_up, w_down), "req", axis=0, tiled=True)
    xs = gather_rows(norm_rows(tokens))

    mlp = lax.axis_index("mlp")
    z, core = mlp // 2, mlp % 2
    ids = jnp.arange(requests, dtype=jnp.int32)
    block = ids // 2
    order = ((z - block % 4) % 4 * 2 + (core + block // 4) % 2) * 2 + ids % 2
    dest = owner_slot // requests
    src = jnp.sum(jnp.where(dest[None, :] == ids[:, None], ids[None, :], 0), axis=1)
    rel = jnp.sum(jnp.where(order[None, :] == src[:, None], ids[None, :], 0), axis=1)
    lengths = jnp.sum(jnp.where(order[:, None] == ids[None, :], prompt_lengths[None, :], 0), axis=1)

    gamma = 1.0 - jnp.exp2(-5.0 - mlp.astype(F32))
    draft = jnp.arange(DRAFT, dtype=jnp.int32)
    position = (lengths[:, None] + draft[None, :]).astype(F32).reshape(-1)
    half = key_width // 2
    freq = jnp.exp(-math.log(10000.0) * jnp.arange(half, dtype=F32) / half)
    angles = position[:, None] * freq[None, :]
    rows = requests * DRAFT
    row = jnp.arange(rows, dtype=jnp.int32)
    gap = row[:, None] - row[None, :]
    inside = (gap >= 0) & (row[:, None] // DRAFT == row[None, :] // DRAFT)
    mask = jnp.where(inside, jnp.power(gamma, jnp.maximum(gap, 0).astype(F32)), 0.0)
    grow = jnp.power(gamma, (row % DRAFT + 1).astype(F32))[:, None]
    accepted_f = accepted.astype(F32)
    exponent = accepted_f[:, None] - 1.0 - draft.astype(F32)[None, :]
    dw = jnp.where(exponent >= 0, jnp.power(gamma, jnp.maximum(exponent, 0.0)), 0.0)
    dw = jnp.broadcast_to(dw.reshape(-1)[:, None], (rows, key_width))
    old = jnp.power(gamma, accepted_f)

    same, other, k, v = retention(
        order, xs, jnp.cos(angles), jnp.sin(angles), mask,
        jnp.broadcast_to(grow, (rows, value_width)),
        w_query, w_key, w_value, w_gate_ret, w_out, states,
    )
    fresh = fresh_states(src, rel, old, states, k, v, dw)
    landed = lax.all_to_all(fresh, "req", split_axis=0, concat_axis=0, tiled=True)
    res, hidden_in = residual_rows(tokens, reduce_rows(same, other))
    same, other = ffn(gather_rows(hidden_in), w_all)
    mixed = final_rows(res, reduce_rows(same, other))
    return mixed, widen(landed).reshape(cached_states.shape)


def solution(mesh):
    return jax.shard_map(
        per_device,
        mesh=mesh,
        in_specs=(
            P(("req", "mlp"), None),
            P("req", "mlp", None, None),
            P("req"),
            P("req"),
            P("req"),
            P(None, "mlp"),
            P(None, "mlp"),
            P(None, "mlp"),
            P(None, "mlp"),
            P("mlp", None),
            P("req", "mlp"),
            P("req", "mlp"),
            P("mlp", "req"),
        ),
        out_specs=(P(("req", "mlp"), None), P("req", "mlp", None, None)),
        check_vma=False,
    )
```

time: 293 us -> 156 us (0.53)
  the two profiles are of different devices: /device:TPU:28 before, /device:TPU:48 now
where the time goes in v1:
time: 156 us; the launch traced here: 155 us
  Pallas kernels  47.5 us (30%)
  waiting for transfers between devices  45.1 us (29%)
  starting transfers between devices  29.4 us (19%)
  between operations  14.3 us (9%)
  local copies, waits for them, and re-layouts  14 us (9%)
  other arithmetic  4.49 us (3%)
    all_to_all x1, waiting for transfers between devices, per_device(): lax.all_to_all(fresh, 'req', split_axis=0, concat_axis=0, tiled=True)  20.7 us
    pallas_call x1, Pallas kernels, fresh_states(): pl.pallas_call(fresh_kernel, grid_spec=pltpu.PrefetchScalarGridSpec(num_s...  13.8 us
    unnamed x36, local copies, waits for them, and re-layouts  12.9 us
    ppermute x6, starting transfers between devices, gather_rows(): mine = [x] + [lax.ppermute(x, 'mlp', along(s)) for s in (1, 2, 3)]  11 us
    ppermute x6, starting transfers between devices, reduce_rows(): lax.ppermute(pieces[s], 'mlp', along(-s))  10.2 us
    pallas_call x1, Pallas kernels, retention(): pl.pallas_call(body, out_shape=[sds((rows // 2, width), BF), sds((rows //...  9.39 us
    all_gather x1, waiting for transfers between devices, per_device(): lax.all_gather(pack_weights(w_gate, w_up, w_down), 'req', axis=0, tiled=T...  8 us
    all_to_all x1, starting transfers between devices, per_device(): lax.all_to_all(fresh, 'req', split_axis=0, concat_axis=0, tiled=True)  7.3 us
  transfers between devices with their start and end apart: 24, of which 16 were waited for; matrix products, arithmetic and copies ran while one was open for 4% of the time, Pallas kernels for 28%

profile of v1, /device:TPU:48, one launch (start us, length us, event | category | flops | bytes accessed | tf_op | source)
XLA Modules:
  0.0 154.8 jit_solution(5496501523948701916)
XLA Ops:
  7.2 1.9 %pack_weights.1 = bf16[128,1536]{1,0:T(8,128)(2,1)} custom-call(bf16[128,512]{1,0:T(8,128)(2,1)} %g_ref.1, bf16[128,512]{1,0:T(8,128)(2,1)} %u_ref.1, bf16[512,128]{1,0:T(8,128)(2,1)} %d_ref.1), custom_call_target="tpu_custom_call" | custom-call | flops 65536 | bytes 786432 | tf_op jit(solution)/shard_map/pack_weights/pallas_call | solution.py:57
  9.1 1.8 %norm_rows.1.refs_0_ = bf16[32,2048]{1,0:T(8,128)(2,1)} custom-call(bf16[32,2048]{1,0:T(8,128)(2,1)} %x_ref.3), custom_call_target="tpu_custom_call" | custom-call | flops 524288 | bytes 262144 | tf_op jit(solution)/shard_map/norm_rows/pallas_call | solution.py:43
  10.9 0.1 collective-permute-start.2
  11.0 3.3 %collective-permute-start.1 = (bf16[32,2048]{1,0:T(8,128)(2,1)}, bf16[32,2048]{1,0:T(8,128)(2,1)S(1)}, u32[]{:S(2)}, u32[]{:S(2)}) collective-permute-start(bf16[32,2048]{1,0:T(8,128)(2,1)} %norm_rows.1.refs_0_), channel_id=1, source_target_pairs={{0,4},{1,5},{2,6},{3,7},{4,0},{5,1},{6,2},{7,3},{8,12},{9,13},{10,... | collective-permute-start | bytes 393224 | tf_op jit(solution)/shard_map/ppermute | solution.py:335
  14.3 2.2 %collective-permute-start = (bf16[32,2048]{1,0:T(8,128)(2,1)}, bf16[32,2048]{1,0:T(8,128)(2,1)S(1)}, u32[]{:S(2)}, u32[]{:S(2)}) collective-permute-start(bf16[32,2048]{1,0:T(8,128)(2,1)} %norm_rows.1.refs_0_), channel_id=1, source_target_pairs={{0,2},{1,3},{2,4},{3,5},{4,6},{5,7},{6,0},{7,1},{8,10},{9,11},{10,... | collective-permute-start | bytes 393224 | tf_op jit(solution)/shard_map/ppermute | solution.py:335
  16.6 0.7 and_select_fusion
  17.3 0.1 select_reduce_fusion.1.src
  17.4 1.4 select_reduce_fusion
  18.8 0.1 convert_element_type.34
  18.9 0.5 multiply_sine_fusion
  19.5 0.3 power_select_fusion.refs_10_
  19.8 1.3 convert_add_fusion
  21.1 0.1 collective-permute-done.1.refs_2_
  21.2 0.4 collective-permute-start.5
  21.6 0.4 collective-permute-done.refs_1_
  22.0 0.1 fusion.3
  22.1 0.1 select_n.159
  22.2 0.2 collective-permute-done.6.refs_7_
  22.4 0.2 collective-permute-done.5.refs_6_
  22.6 0.7 collective-permute-done.4.refs_5_
  23.3 0.1 broadcast_in_dim.33.refs_11_
  23.5 1.2 copy-done.1
  24.7 1.2 copy-done.2
  25.9 0.9 copy-done.3
  26.8 9.4 %retention.1 = (bf16[128,2048]{1,0:T(8,128)(2,1)S(1)}, bf16[128,2048]{1,0:T(8,128)(2,1)S(1)}, bf16[256,256]{1,0:T(8,128)(2,1)S(1)}, bf16[256,512]{1,0:T(8,128)(2,1)S(1)}) custom-call(s32[16]{0:T(128)S(1)} %fusion.9.order, bf16[32,2048]{1,0:T(8,128)(2,1)S(1)} %copy-done.3, bf16[32,2048]{1,0:T(8,128)(2,1)S(1)} %collective-permute-done.refs_1_, ...), custom_call_target="tpu_custom_call" | custom-call | flops 2147483648 | bytes 20971520 | tf_op jit(solution)/shard_map/retention/pallas_call | solution.py:197
  36.2 0.8 copy-done.4
  37.0 0.7 copy-done.6
  37.7 0.7 copy-done.8
  38.4 0.8 broadcast_in_dim.34.dw_ref
  39.2 13.8 %fresh_states.1 = bf16[16,256,512]{2,1,0:T(8,128)(2,1)} custom-call(s32[16]{0:T(128)} %copy-done.17, s32[16]{0:T(128)} %get-tuple-element.38.rel, f32[16]{0:T(128)} %get-tuple-element.43.old, f32[16,256,512]{2,1,0:T(8,128)} %bitcast.5, bf16[256,256]{1,0:T(8,128)(2,1)} %copy-done.8, bf16[256,512]{1,0:T(8,128)(2,1)} %copy-done.6, ...), custom_call_target="tpu_custom_call" | custom-call | flops 67108864 | bytes 12582912 | tf_op jit(solution)/shard_map/fresh_states/pallas_call | solution.py:234
  52.9 7.3 %all-to-all-start = ((bf16[16,256,512]{2,1,0:T(8,128)(2,1)}), bf16[16,256,512]{2,1,0:T(8,128)(2,1)}, u32[]{:S(2)}, u32[]{:S(2)}) async-start(bf16[16,256,512]{2,1,0:T(8,128)(2,1)} %fresh_states.1), calls=%async_computation | async-start | bytes 8388608 | tf_op jit(solution)/shard_map/all_to_all | solution.py:387
  60.2 1.9 %collective-permute-done.7.b_ref = bf16[128,2048]{1,0:T(8,128)(2,1)S(1)} collective-permute-done((bf16[128,2048]{1,0:T(8,128)(2,1)S(1)}, bf16[128,2048]{1,0:T(8,128)(2,1)S(1)}, u32[]{:S(2)}, u32[]{:S(2)}) %collective-permute-start.7) | collective-permute-done | bytes 524320 | tf_op jit(solution)/shard_map/ppermute | solution.py:340
  62.1 0.8 copy-done.9
  62.9 2.0 %pair_sum.2 = (bf16[32,2048]{1,0:T(8,128)(2,1)}, bf16[32,2048]{1,0:T(8,128)(2,1)}, bf16[32,2048]{1,0:T(8,128)(2,1)}, bf16[32,2048]{1,0:T(8,128)(2,1)}) custom-call(bf16[128,2048]{1,0:T(8,128)(2,1)} %copy-done.4, bf16[128,2048]{1,0:T(8,128)(2,1)} %copy-done.9), custom_call_target="tpu_custom_call" | custom-call | flops 262144 | bytes 1572864 | tf_op jit(solution)/shard_map/pair_sum/pallas_call | solution.py:73
  65.0 3.0 %collective-permute-start.8 = (bf16[32,2048]{1,0:T(8,128)(2,1)}, bf16[32,2048]{1,0:T(8,128)(2,1)S(1)}, u32[]{:S(2)}, u32[]{:S(2)}) collective-permute-start(bf16[32,2048]{1,0:T(8,128)(2,1)} %get-tuple-element.21), channel_id=1, source_target_pairs={{0,6},{1,7},{2,0},{3,1},{4,2},{5,3},{6,4},{7,5},{8,14},{9,15},{10,... | collective-permute-start | bytes 393224 | tf_op jit(solution)/shard_map/ppermute | solution.py:341
  68.0 2.3 %collective-permute-start.10 = (bf16[32,2048]{1,0:T(8,128)(2,1)}, bf16[32,2048]{1,0:T(8,128)(2,1)S(1)}, u32[]{:S(2)}, u32[]{:S(2)}) collective-permute-start(bf16[32,2048]{1,0:T(8,128)(2,1)} %get-tuple-element.23), channel_id=1, source_target_pairs={{0,2},{1,3},{2,4},{3,5},{4,6},{5,7},{6,0},{7,1},{8,10},{9,11},{10,... | collective-permute-start | bytes 393224 | tf_op jit(solution)/shard_map/ppermute | solution.py:341
  70.3 1.9 %collective-permute-done.8.b_ref = bf16[32,2048]{1,0:T(8,128)(2,1)S(1)} collective-permute-done((bf16[32,2048]{1,0:T(8,128)(2,1)}, bf16[32,2048]{1,0:T(8,128)(2,1)S(1)}, u32[]{:S(2)}, u32[]{:S(2)}) %collective-permute-start.8) | collective-permute-done | bytes 131104 | tf_op jit(solution)/shard_map/ppermute | solution.py:341
  72.1 2.8 %collective-permute-done.9.c_ref = bf16[32,2048]{1,0:T(8,128)(2,1)S(1)} collective-permute-done((bf16[32,2048]{1,0:T(8,128)(2,1)}, bf16[32,2048]{1,0:T(8,128)(2,1)S(1)}, u32[]{:S(2)}, u32[]{:S(2)}) %collective-permute-start.9) | collective-permute-done | bytes 131104 | tf_op jit(solution)/shard_map/ppermute | solution.py:341
  74.9 0.4 collective-permute-done.10.d_ref
  75.3 0.2 copy-done.15
  75.6 0.4 copy-done.16
  76.0 2.1 %residual_rows.1 = (f32[32,2048]{1,0:T(8,128)}, bf16[32,2048]{1,0:T(8,128)(2,1)}) custom-call(bf16[32,2048]{1,0:T(8,128)(2,1)} %x_ref.3, bf16[32,2048]{1,0:T(8,128)(2,1)} %get-tuple-element.20.a_ref, bf16[32,2048]{1,0:T(8,128)(2,1)} %copy-done.14, bf16[32,2048]{1,0:T(8,128)(2,1)} %copy-done.15, bf16[32,2048]{1,0:T(8,128)(2,1)} %copy-done.16), custom_call_target="tpu_custom_call" | custom-call | flops 786432 | bytes 1048576 | tf_op jit(solution)/shard_map/residual_rows/pallas_call | solution.py:89
  78.1 3.2 %collective-permute-start.13 = (bf16[32,2048]{1,0:T(8,128)(2,1)}, bf16[32,2048]{1,0:T(8,128)(2,1)S(1)}, u32[]{:S(2)}, u32[]{:S(2)}) collective-permute-start(bf16[32,2048]{1,0:T(8,128)(2,1)} %get-tuple-element.25.refs_0_), channel_id=1, source_target_pairs={{0,6},{1,7},{2,0},{3,1},{4,2},{5,3},{6,4},{7,5},{8,14},{9,15},{10,... | collective-permute-start | bytes 393224 | tf_op jit(solution)/shard_map/ppermute | solution.py:335
  81.3 2.1 %collective-permute-start.11 = (bf16[32,2048]{1,0:T(8,128)(2,1)}, bf16[32,2048]{1,0:T(8,128)(2,1)S(1)}, u32[]{:S(2)}, u32[]{:S(2)}) collective-permute-start(bf16[32,2048]{1,0:T(8,128)(2,1)} %get-tuple-element.25.refs_0_), channel_id=1, source_target_pairs={{0,2},{1,3},{2,4},{3,5},{4,6},{5,7},{6,0},{7,1},{8,10},{9,11},{10,... | collective-permute-start | bytes 393224 | tf_op jit(solution)/shard_map/ppermute | solution.py:335
  83.4 2.1 %collective-permute-done.13.refs_3_ = bf16[32,2048]{1,0:T(8,128)(2,1)S(1)} collective-permute-done((bf16[32,2048]{1,0:T(8,128)(2,1)}, bf16[32,2048]{1,0:T(8,128)(2,1)S(1)}, u32[]{:S(2)}, u32[]{:S(2)}) %collective-permute-start.13) | collective-permute-done | bytes 131104 | tf_op jit(solution)/shard_map/ppermute | solution.py:335
  85.5 2.8 %collective-permute-done.12.refs_2_ = bf16[32,2048]{1,0:T(8,128)(2,1)S(1)} collective-permute-done((bf16[32,2048]{1,0:T(8,128)(2,1)}, bf16[32,2048]{1,0:T(8,128)(2,1)S(1)}, u32[]{:S(2)}, u32[]{:S(2)}) %collective-permute-start.12) | collective-permute-done | bytes 131104 | tf_op jit(solution)/shard_map/ppermute | solution.py:335
  88.3 0.5 collective-permute-start.15
  88.8 0.8 collective-permute-done.16.refs_6_
  89.6 0.2 collective-permute-done.15.refs_5_
  89.8 8.0 %all-gather.2.cloned.1.call-done.refs_8_ = bf16[2048,1536]{1,0:T(8,128)(2,1)} async-done(((bf16[128,1536]{1,0:T(8,128)(2,1)}), bf16[2048,1536]{1,0:T(8,128)(2,1)}) %all-gather.2.cloned.1.call-update) | async-done | bytes 6291472 | tf_op jit(solution)/shard_map/all_gather | solution.py:350
  97.8 2.8 %copy-done = bf16[2048,1536]{1,0:T(8,128)(2,1)S(1)} copy-done((bf16[2048,1536]{1,0:T(8,128)(2,1)S(1)}, bf16[2048,1536]{1,0:T(8,128)(2,1)}, u32[]{:S(2)}) %copy-start) | copy-done | bytes 6291480
  100.6 0.9 copy-done.7
  101.5 5.4 %feed_forward.1 = (bf16[128,2048]{1,0:T(8,128)(2,1)S(1)}, bf16[128,2048]{1,0:T(8,128)(2,1)S(1)}) custom-call(bf16[32,2048]{1,0:T(8,128)(2,1)S(1)} %copy-done.7, bf16[32,2048]{1,0:T(8,128)(2,1)S(1)} %collective-permute-done.11.refs_1_, bf16[32,2048]{1,0:T(8,128)(2,1)S(1)} %collective-permute-done.12.refs_2_, ...), custom_call_target="tpu_custom_call" | custom-call | flops 1610612736 | bytes 9437184 | tf_op jit(solution)/shard_map/feed_forward/pallas_call | solution.py:310
  107.0 0.8 copy-done.5
  107.8 1.9 %collective-permute-done.18.b_ref = bf16[128,2048]{1,0:T(8,128)(2,1)S(1)} collective-permute-done((bf16[128,2048]{1,0:T(8,128)(2,1)S(1)}, bf16[128,2048]{1,0:T(8,128)(2,1)S(1)}, u32[]{:S(2)}, u32[]{:S(2)}) %collective-permute-start.18) | collective-permute-done | bytes 524320 | tf_op jit(solution)/shard_map/ppermute | solution.py:340
  109.7 0.8 copy-done.10
  110.5 2.0 %pair_sum.3 = (bf16[32,2048]{1,0:T(8,128)(2,1)}, bf16[32,2048]{1,0:T(8,128)(2,1)}, bf16[32,2048]{1,0:T(8,128)(2,1)}, bf16[32,2048]{1,0:T(8,128)(2,1)}) custom-call(bf16[128,2048]{1,0:T(8,128)(2,1)} %copy-done.5, bf16[128,2048]{1,0:T(8,128)(2,1)} %copy-done.10), custom_call_target="tpu_custom_call" | custom-call | flops 262144 | bytes 1572864 | tf_op jit(solution)/shard_map/pair_sum/pallas_call | solution.py:73
  112.5 0.5 collective-permute-start.19
  113.0 2.5 %collective-permute-start.20 = (bf16[32,2048]{1,0:T(8,128)(2,1)}, bf16[32,2048]{1,0:T(8,128)(2,1)S(1)}, u32[]{:S(2)}, u32[]{:S(2)}) collective-permute-start(bf16[32,2048]{1,0:T(8,128)(2,1)} %get-tuple-element.30), channel_id=1, source_target_pairs={{0,4},{1,5},{2,6},{3,7},{4,0},{5,1},{6,2},{7,3},{8,12},{9,13},{10,... | collective-permute-start | bytes 393224 | tf_op jit(solution)/shard_map/ppermute | solution.py:341
  115.5 1.8 %collective-permute-start.21 = (bf16[32,2048]{1,0:T(8,128)(2,1)}, bf16[32,2048]{1,0:T(8,128)(2,1)S(1)}, u32[]{:S(2)}, u32[]{:S(2)}) collective-permute-start(bf16[32,2048]{1,0:T(8,128)(2,1)} %get-tuple-element.31), channel_id=1, source_target_pairs={{0,2},{1,3},{2,4},{3,5},{4,6},{5,7},{6,0},{7,1},{8,10},{9,11},{10,... | collective-permute-start | bytes 393224 | tf_op jit(solution)/shard_map/ppermute | solution.py:341
  117.4 20.7 %all-to-all-done.x_ref = bf16[16,256,512]{2,1,0:T(8,128)(2,1)} async-done(((bf16[16,256,512]{2,1,0:T(8,128)(2,1)}), bf16[16,256,512]{2,1,0:T(8,128)(2,1)}, u32[]{:S(2)}, u32[]{:S(2)}) %all-to-all-start) | async-done | bytes 4194336 | tf_op jit(solution)/shard_map/all_to_all | solution.py:387
  138.0 7.3 %widen.1 = f32[16,256,512]{2,1,0:T(8,128)} custom-call(bf16[16,256,512]{2,1,0:T(8,128)(2,1)} %all-to-all-done.x_ref), custom_call_target="tpu_custom_call" | custom-call | flops 2097152 | bytes 12582912 | tf_op jit(solution)/shard_map/widen/pallas_call | solution.py:260
  145.3 0.6 copy-done.11
  146.0 1.9 %final_rows.1 = bf16[32,2048]{1,0:T(8,128)(2,1)} custom-call(f32[32,2048]{1,0:T(8,128)} %get-tuple-element.24.x_ref, bf16[32,2048]{1,0:T(8,128)(2,1)} %get-tuple-element.28.a_ref, bf16[32,2048]{1,0:T(8,128)(2,1)} %copy-done.11, bf16[32,2048]{1,0:T(8,128)(2,1)} %copy-done.12, bf16[32,2048]{1,0:T(8,128)(2,1)} %copy-done.13), custom_call_target="tpu_custom_call" | custom-call | flops 393216 | bytes 917504 | tf_op jit(solution)/shard_map/final_rows/pallas_call | solution.py:103
  (48 shorter events, 0.4 us)
Async XLA Ops:
  7.2 90.7 %all-gather.2.cloned.1.call-start = ((), (), s32[]{:S(2)}) async-start(), calls=%async_computation.1 | async-start | bytes 6684672 | tf_op jit(solution)/shard_map/all_gather | solution.py:350
  10.9 11.3 %collective-permute-start.3 = (bf16[32,2048]{1,0:T(8,128)(2,1)}, bf16[32,2048]{1,0:T(8,128)(2,1)S(1)}, u32[]{:S(2)}, u32[]{:S(2)}) collective-permute-start(bf16[32,2048]{1,0:T(8,128)(2,1)} %norm_rows.1.refs_0_), channel_id=1, source_target_pairs={{0,1},{1,0},{2,3},{3,2},{4,5},{5,4},{6,7},{7,6},{8,9},{9,8},{10,11... | collective-permute-start | bytes 393224 | tf_op jit(solution)/shard_map/ppermute | solution.py:336
  10.9 10.2 %collective-permute-start.2 = (bf16[32,2048]{1,0:T(8,128)(2,1)}, bf16[32,2048]{1,0:T(8,128)(2,1)S(1)}, u32[]{:S(2)}, u32[]{:S(2)}) collective-permute-start(bf16[32,2048]{1,0:T(8,128)(2,1)} %norm_rows.1.refs_0_), channel_id=1, source_target_pairs={{0,6},{1,7},{2,0},{3,1},{4,2},{5,3},{6,4},{7,5},{8,14},{9,15},{10,... | collective-permute-start | bytes 393224 | tf_op jit(solution)/shard_map/ppermute | solution.py:335
  11.0 10.2 %collective-permute-start.1 = (bf16[32,2048]{1,0:T(8,128)(2,1)}, bf16[32,2048]{1,0:T(8,128)(2,1)S(1)}, u32[]{:S(2)}, u32[]{:S(2)}) collective-permute-start(bf16[32,2048]{1,0:T(8,128)(2,1)} %norm_rows.1.refs_0_), channel_id=1, source_target_pairs={{0,4},{1,5},{2,6},{3,7},{4,0},{5,1},{6,2},{7,3},{8,12},{9,13},{10,... | collective-permute-start | bytes 393224 | tf_op jit(solution)/shard_map/ppermute | solution.py:335
  14.3 7.7 %collective-permute-start = (bf16[32,2048]{1,0:T(8,128)(2,1)}, bf16[32,2048]{1,0:T(8,128)(2,1)S(1)}, u32[]{:S(2)}, u32[]{:S(2)}) collective-permute-start(bf16[32,2048]{1,0:T(8,128)(2,1)} %norm_rows.1.refs_0_), channel_id=1, source_target_pairs={{0,2},{1,3},{2,4},{3,5},{4,6},{5,7},{6,0},{7,1},{8,10},{9,11},{10,... | collective-permute-start | bytes 393224 | tf_op jit(solution)/shard_map/ppermute | solution.py:335
  17.4 18.8 %copy-start.17 = (s32[16]{0:T(128)}, s32[16]{0:T(128)S(1)}, u32[]{:S(2)}) copy-start(s32[16]{0:T(128)S(1)} %select_reduce_fusion.1.src) | copy-start | bytes 196
  21.1 1.3 collective-permute-start.6
  21.2 1.4 collective-permute-start.5
  22.0 1.3 collective-permute-start.4
  23.4 1.2 copy-start.1
  24.7 1.2 copy-start.2
  25.9 0.9 copy-start.3
  36.2 0.8 copy-start.4
  37.0 0.7 copy-start.6
  37.7 0.7 copy-start.8
  52.9 85.1 %all-to-all-start = ((bf16[16,256,512]{2,1,0:T(8,128)(2,1)}), bf16[16,256,512]{2,1,0:T(8,128)(2,1)}, u32[]{:S(2)}, u32[]{:S(2)}) async-start(bf16[16,256,512]{2,1,0:T(8,128)(2,1)} %fresh_states.1), calls=%async_computation | async-start | bytes 8388608 | tf_op jit(solution)/shard_map/all_to_all | solution.py:387
  60.2 1.9 %collective-permute-start.7 = (bf16[128,2048]{1,0:T(8,128)(2,1)S(1)}, bf16[128,2048]{1,0:T(8,128)(2,1)S(1)}, u32[]{:S(2)}, u32[]{:S(2)}) collective-permute-start(bf16[128,2048]{1,0:T(8,128)(2,1)S(1)} %get-tuple-element.19), channel_id=1, source_target_pairs={{0,1},{1,0},{2,3},{3,2},{4,5},{5,4},{6,7},{7,6},{8,9},{9,8},{10,11... | collective-permute-start | bytes 1572872 | tf_op jit(solution)/shard_map/ppermute | solution.py:340
  62.1 0.8 copy-start.9
  65.0 7.2 %collective-permute-start.8 = (bf16[32,2048]{1,0:T(8,128)(2,1)}, bf16[32,2048]{1,0:T(8,128)(2,1)S(1)}, u32[]{:S(2)}, u32[]{:S(2)}) collective-permute-start(bf16[32,2048]{1,0:T(8,128)(2,1)} %get-tuple-element.21), channel_id=1, source_target_pairs={{0,6},{1,7},{2,0},{3,1},{4,2},{5,3},{6,4},{7,5},{8,14},{9,15},{10,... | collective-permute-start | bytes 393224 | tf_op jit(solution)/shard_map/ppermute | solution.py:341
  68.0 7.0 %collective-permute-start.9 = (bf16[32,2048]{1,0:T(8,128)(2,1)}, bf16[32,2048]{1,0:T(8,128)(2,1)S(1)}, u32[]{:S(2)}, u32[]{:S(2)}) collective-permute-start(bf16[32,2048]{1,0:T(8,128)(2,1)} %get-tuple-element.22), channel_id=1, source_target_pairs={{0,4},{1,5},{2,6},{3,7},{4,0},{5,1},{6,2},{7,3},{8,12},{9,13},{10,... | collective-permute-start | bytes 393224 | tf_op jit(solution)/shard_map/ppermute | solution.py:341
  68.0 7.4 %collective-permute-start.10 = (bf16[32,2048]{1,0:T(8,128)(2,1)}, bf16[32,2048]{1,0:T(8,128)(2,1)S(1)}, u32[]{:S(2)}, u32[]{:S(2)}) collective-permute-start(bf16[32,2048]{1,0:T(8,128)(2,1)} %get-tuple-element.23), channel_id=1, source_target_pairs={{0,2},{1,3},{2,4},{3,5},{4,6},{5,7},{6,0},{7,1},{8,10},{9,11},{10,... | collective-permute-start | bytes 393224 | tf_op jit(solution)/shard_map/ppermute | solution.py:341
  72.1 3.2 %copy-start.14 = (bf16[32,2048]{1,0:T(8,128)(2,1)}, bf16[32,2048]{1,0:T(8,128)(2,1)S(1)}, u32[]{:S(2)}) copy-start(bf16[32,2048]{1,0:T(8,128)(2,1)S(1)} %collective-permute-done.8.b_ref) | copy-start | bytes 393220
  74.9 0.6 copy-start.15
  75.3 0.7 copy-start.16
  78.1 7.4 %collective-permute-start.13 = (bf16[32,2048]{1,0:T(8,128)(2,1)}, bf16[32,2048]{1,0:T(8,128)(2,1)S(1)}, u32[]{:S(2)}, u32[]{:S(2)}) collective-permute-start(bf16[32,2048]{1,0:T(8,128)(2,1)} %get-tuple-element.25.refs_0_), channel_id=1, source_target_pairs={{0,6},{1,7},{2,0},{3,1},{4,2},{5,3},{6,4},{7,5},{8,14},{9,15},{10,... | collective-permute-start | bytes 393224 | tf_op jit(solution)/shard_map/ppermute | solution.py:335
  81.3 7.0 %collective-permute-start.12 = (bf16[32,2048]{1,0:T(8,128)(2,1)}, bf16[32,2048]{1,0:T(8,128)(2,1)S(1)}, u32[]{:S(2)}, u32[]{:S(2)}) collective-permute-start(bf16[32,2048]{1,0:T(8,128)(2,1)} %get-tuple-element.25.refs_0_), channel_id=1, source_target_pairs={{0,4},{1,5},{2,6},{3,7},{4,0},{5,1},{6,2},{7,3},{8,12},{9,13},{10,... | collective-permute-start | bytes 393224 | tf_op jit(solution)/shard_map/ppermute | solution.py:335
  81.3 7.0 %collective-permute-start.11 = (bf16[32,2048]{1,0:T(8,128)(2,1)}, bf16[32,2048]{1,0:T(8,128)(2,1)S(1)}, u32[]{:S(2)}, u32[]{:S(2)}) collective-permute-start(bf16[32,2048]{1,0:T(8,128)(2,1)} %get-tuple-element.25.refs_0_), channel_id=1, source_target_pairs={{0,2},{1,3},{2,4},{3,5},{4,6},{5,7},{6,0},{7,1},{8,10},{9,11},{10,... | collective-permute-start | bytes 393224 | tf_op jit(solution)/shard_map/ppermute | solution.py:335
  83.4 5.4 %collective-permute-start.14 = (bf16[32,2048]{1,0:T(8,128)(2,1)}, bf16[32,2048]{1,0:T(8,128)(2,1)S(1)}, u32[]{:S(2)}, u32[]{:S(2)}) collective-permute-start(bf16[32,2048]{1,0:T(8,128)(2,1)} %get-tuple-element.25.refs_0_), channel_id=1, source_target_pairs={{0,1},{1,0},{2,3},{3,2},{4,5},{5,4},{6,7},{7,6},{8,9},{9,8},{10,11... | collective-permute-start | bytes 393224 | tf_op jit(solution)/shard_map/ppermute | solution.py:336
  85.5 3.3 %collective-permute-start.17 = (bf16[32,2048]{1,0:T(8,128)(2,1)S(1)}, bf16[32,2048]{1,0:T(8,128)(2,1)S(1)}, u32[]{:S(2)}, u32[]{:S(2)}) collective-permute-start(bf16[32,2048]{1,0:T(8,128)(2,1)S(1)} %collective-permute-done.13.refs_3_), channel_id=1, source_target_pairs={{0,1},{1,0},{2,3},{3,2},{4,5},{5,4},{6,7},{7,6},{8,9},{9,8},{10,11... | collective-permute-start | bytes 393224 | tf_op jit(solution)/shard_map/ppermute | solution.py:336
  88.3 1.3 collective-permute-start.16
  88.3 1.5 collective-permute-start.15
  97.8 2.8 %copy-start = (bf16[2048,1536]{1,0:T(8,128)(2,1)S(1)}, bf16[2048,1536]{1,0:T(8,128)(2,1)}, u32[]{:S(2)}) copy-start(bf16[2048,1536]{1,0:T(8,128)(2,1)} %all-gather.2.cloned.1.call-done.refs_8_) | copy-start | bytes 18874372
  100.6 0.9 copy-start.7
  107.0 0.8 copy-start.5
  107.8 1.9 %collective-permute-start.18 = (bf16[128,2048]{1,0:T(8,128)(2,1)S(1)}, bf16[128,2048]{1,0:T(8,128)(2,1)S(1)}, u32[]{:S(2)}, u32[]{:S(2)}) collective-permute-start(bf16[128,2048]{1,0:T(8,128)(2,1)S(1)} %get-tuple-element.27), channel_id=1, source_target_pairs={{0,1},{1,0},{2,3},{3,2},{4,5},{5,4},{6,7},{7,6},{8,9},{9,8},{10,11... | collective-permute-start | bytes 1572872 | tf_op jit(solution)/shard_map/ppermute | solution.py:340
  109.7 0.8 copy-start.10
  112.5 32.8 %collective-permute-start.19 = (bf16[32,2048]{1,0:T(8,128)(2,1)}, bf16[32,2048]{1,0:T(8,128)(2,1)S(1)}, u32[]{:S(2)}, u32[]{:S(2)}) collective-permute-start(bf16[32,2048]{1,0:T(8,128)(2,1)} %get-tuple-element.29), channel_id=1, source_target_pairs={{0,6},{1,7},{2,0},{3,1},{4,2},{5,3},{6,4},{7,5},{8,14},{9,15},{10,... | collective-permute-start | bytes 393224 | tf_op jit(solution)/shard_map/ppermute | solution.py:341
  113.0 32.3 %collective-permute-start.20 = (bf16[32,2048]{1,0:T(8,128)(2,1)}, bf16[32,2048]{1,0:T(8,128)(2,1)S(1)}, u32[]{:S(2)}, u32[]{:S(2)}) collective-permute-start(bf16[32,2048]{1,0:T(8,128)(2,1)} %get-tuple-element.30), channel_id=1, source_target_pairs={{0,4},{1,5},{2,6},{3,7},{4,0},{5,1},{6,2},{7,3},{8,12},{9,13},{10,... | collective-permute-start | bytes 393224 | tf_op jit(solution)/shard_map/ppermute | solution.py:341
  115.5 29.8 %collective-permute-start.21 = (bf16[32,2048]{1,0:T(8,128)(2,1)}, bf16[32,2048]{1,0:T(8,128)(2,1)S(1)}, u32[]{:S(2)}, u32[]{:S(2)}) collective-permute-start(bf16[32,2048]{1,0:T(8,128)(2,1)} %get-tuple-element.31), channel_id=1, source_target_pairs={{0,2},{1,3},{2,4},{3,5},{4,6},{5,7},{6,0},{7,1},{8,10},{9,11},{10,... | collective-permute-start | bytes 393224 | tf_op jit(solution)/shard_map/ppermute | solution.py:341
  145.3 0.7 copy-start.11
  145.3 0.7 copy-start.12
  145.3 0.7 copy-start.13
Sparse Core Ops, SparseCore 0:
  10.2 87.6 all-gather.1

commit v2 on v1

v2 whole, which is shorter than its diff:
```python
import functools
import math

import jax
import jax.numpy as jnp
from jax import lax
from jax.experimental import pallas as pl
from jax.experimental.pallas import tpu as pltpu
from jax.sharding import PartitionSpec as P

DRAFT = 16
EPS = 1e-05
BF = jnp.bfloat16
F32 = jnp.float32
VM = pl.BlockSpec(memory_space=pltpu.VMEM)
SM = pl.BlockSpec(memory_space=pltpu.SMEM)
ANY = pl.BlockSpec(memory_space=pl.ANY)
HBM = pl.BlockSpec(memory_space=pltpu.HBM)


def sds(shape, dtype):
    return jax.ShapeDtypeStruct(shape, dtype)


def cost(flops, nbytes):
    return pl.CostEstimate(flops=flops, bytes_accessed=nbytes, transcendentals=0)


def params(mib):
    return pltpu.CompilerParams(vmem_limit_bytes=max(mib, 62) << 20)


def norm(v):
    centred = v - jnp.mean(v, axis=-1, keepdims=True)
    variance = jnp.mean(centred * centred, axis=-1, keepdims=True)
    return centred * lax.rsqrt(variance + EPS)


def staged(body, ins, outs, name, flops=0):
    n, m = len(ins), len(outs)

    def kernel(*refs):
        bufs, sems = refs[n + m : -1], refs[-1]
        copies = [pltpu.make_async_copy(refs[i], bufs[i], sems.at[i]) for i in range(n)]
        for c in copies:
            c.start()
        for c in copies:
            c.wait()
        body(*bufs, *refs[n : n + m])

    size = sum(v.size * v.dtype.itemsize for v in list(ins) + list(outs))
    return pl.pallas_call(
        kernel, out_shape=outs, in_specs=[ANY] * n, out_specs=[VM] * m,
        scratch_shapes=[pltpu.VMEM(v.shape, v.dtype) for v in ins]
        + [pltpu.SemaphoreType.DMA((n,))],
        cost_estimate=cost(flops, size), compiler_params=params(16), name=name,
    )(*ins)


def prepare_body(g_ref, u_ref, d_ref, x_ref, y_ref, a_ref, b_ref, o_ref):
    width = g_ref.shape[1]
    half, rows = width // 2, x_ref.shape[0]
    a_ref[:, :width] = g_ref[...]
    a_ref[:, width:] = u_ref[:, :half]
    b_ref[:, :half] = u_ref[:, half:]
    b_ref[:, half:] = d_ref[...].astype(F32).T.astype(BF)
    mine = norm(x_ref[...].astype(F32)).astype(BF)
    theirs = norm(y_ref[...].astype(F32)).astype(BF)
    for i in range(4):
        o_ref[i, :rows, :] = mine
        o_ref[i, rows:, :] = theirs


def prepare(g, u, d, x, y):
    part = sds((g.shape[0], 3 * g.shape[1] // 2), BF)
    both = sds((4, 2 * x.shape[0], x.shape[1]), BF)
    return staged(prepare_body, (g, u, d, x, y), [part, part, both], "prepare")


def pair_body(a_ref, b_ref, *o_refs):
    rows = o_refs[0].shape[0]
    for i, o_ref in enumerate(o_refs):
        part = pl.ds(i * rows, rows)
        o_ref[...] = (a_ref[part, :].astype(F32) + b_ref[part, :].astype(F32)).astype(BF)


def pair_sum(a, b, pieces):
    piece = sds((a.shape[0] // pieces, a.shape[1]), BF)
    return staged(pair_body, (a, b), [piece] * pieces, "pair_sum")


def total(refs):
    out = refs[0][...].astype(F32)
    for r in refs[1:]:
        out = out + r[...].astype(F32)
    return out


def residual_body(x_ref, a_ref, b_ref, c_ref, d_ref, res_ref, hid_ref):
    res = x_ref[...].astype(F32) + total((a_ref, b_ref, c_ref, d_ref))
    res_ref[...] = res
    hid_ref[...] = norm(res).astype(BF)


def residual_rows(x, parts):
    return staged(residual_body, (x, *parts), [sds(x.shape, F32), sds(x.shape, BF)], "residual_rows")


def final_body(x_ref, a_ref, b_ref, c_ref, d_ref, o_ref):
    o_ref[...] = (x_ref[...] + total((a_ref, b_ref, c_ref, d_ref))).astype(BF)


def final_rows(x, parts):
    return staged(final_body, (x, *parts), [sds(x.shape, BF)], "final_rows")[0]


def block_slot(place, request):
    z, core = request // 4, request // 2 % 2
    block = (place[3] + core) % 2 * 4 + (place[2] - z + 4) % 4
    return block * 2 + request % 2


def retention_kernel(
    place, decay, *refs, rows_in, key_width, value_width
):
    x_h, table_h, wq_h, wk_h, wv_h, wg_h, wo_h, st_h = refs[:8]
    same_ref, other_ref, k_ref, v_ref = refs[8:12]
    xbuf, tableb, wbuf, wob, stb, proj, keep, joined, sems = refs[12:]
    tile = key_width
    requests = stb.shape[0]
    rows = xbuf.shape[0]
    copies = []

    def send(src, dst):
        copy = pltpu.make_async_copy(src, dst, sems.at[len(copies)])
        copy.start()
        copies.append(copy)
        return copy

    c_x = []
    for i in range(4):
        for j in range(2):
            at = (4 * j + (place[2] - i + 4) % 4) * rows_in
            rows_at = pl.ds(pl.multiple_of(at, rows_in), rows_in)
            c_x.append(send(x_h.at[i, pl.ds(j * rows_in, rows_in), :], xbuf.at[rows_at, :]))
    c_w = [send(wk_h, wbuf.at[0])]
    c_t = send(table_h, tableb)
    c_w.append(send(wq_h, wbuf.at[1]))
    for w in (wv_h, wg_h):
        for j in range(value_width // tile):
            c_w.append(send(w.at[:, pl.ds(j * tile, tile)], wbuf.at[len(c_w)]))
    c_s = [send(st_h.at[i], stb.at[block_slot(place, i)]) for i in range(requests)]
    c_o = send(wo_h, wob)
    half = key_width // 2
    row = lax.broadcasted_iota(jnp.int32, (rows, rows), 0)
    col = lax.broadcasted_iota(jnp.int32, (rows, rows), 1)
    gap = row - col
    inside = (gap >= 0) & (row // DRAFT == col // DRAFT)
    mask = jnp.where(inside, jnp.exp(decay[0] * jnp.maximum(gap, 0).astype(F32)), 0.0)
    for c in c_x:
        c.wait()

    x = xbuf[...]

    def project(j):
        c_w[j].wait()
        return jnp.dot(x, wbuf[j], preferred_element_type=F32)

    key = project(0) * (1.0 / math.sqrt(key_width))
    c_t.wait()
    cosv, sinv = tableb[:, :half], tableb[:, half : 2 * half]

    def rotate(u):
        front, back = u[:, :half], u[:, half:]
        return jnp.concatenate(
            [front * cosv - back * sinv, front * sinv + back * cosv], axis=1
        ).astype(BF)

    rk = rotate(key)
    fade = tableb[:, 2 * half : 3 * half]
    k_ref[...] = (rk.astype(F32) * jnp.concatenate([fade, fade], axis=1)).astype(BF)
    rq = rotate(project(1))
    scores = lax.dot_general(rq, rk, (((1,), (1,)), ((), ())), preferred_element_type=F32)
    weights = (scores * mask).astype(BF)
    keep[...] = rq
    for j in range(2):
        val = project(2 + j).astype(BF)
        v_ref[:, j * tile : (j + 1) * tile] = val
        proj[:, j * tile : (j + 1) * tile] = jnp.dot(weights, val, preferred_element_type=F32)
    gates = [project(4), project(5)]
    for c in c_s:
        c.wait()
    for i in range(requests):
        part = pl.ds(i * DRAFT, DRAFT)
        carried = jnp.dot(keep[part, :], stb[i].astype(BF), preferred_element_type=F32)
        grow = tableb[part, 3 * half : 4 * half]
        proj[part, :] += carried * jnp.concatenate([grow] * (value_width // half), axis=1)
    normed = norm(proj[...])
    for j in range(2):
        g = gates[j]
        act = g / (1.0 + jnp.exp(-g))
        joined[:, j * tile : (j + 1) * tile] = (
            normed[:, j * tile : (j + 1) * tile] * act
        ).astype(BF)
    c_o.wait()
    both = joined[...]
    for j in range(wob.shape[1] // 512):
        cols = pl.ds(j * 512, 512)
        out = jnp.dot(both, wob[:, cols], preferred_element_type=F32).astype(BF)
        same_ref[:, cols] = out[: rows // 2]
        other_ref[:, cols] = out[rows // 2 :]


def retention(place, decay, xs, table, wq, wk, wv, wg, wo, states):
    rows_in, width = xs.shape[1] // 2, xs.shape[2]
    rows = rows_in * 8
    key_width, value_width = wq.shape[1], wv.shape[1]
    body = functools.partial(
        retention_kernel, rows_in=rows_in, key_width=key_width, value_width=value_width
    )
    tiles = (2 * key_width + 2 * value_width) // key_width
    return pl.pallas_call(
        body,
        out_shape=[
            sds((rows // 2, width), BF), sds((rows // 2, width), BF),
            sds((rows, key_width), BF), sds((rows, value_width), BF),
        ],
        in_specs=[SM] * 2 + [ANY] * 8,
        out_specs=[VM] * 4,
        scratch_shapes=[
            pltpu.VMEM((rows, width), BF),
            pltpu.VMEM(table.shape, F32),
            pltpu.VMEM((tiles, width, key_width), BF),
            pltpu.VMEM(wo.shape, BF),
            pltpu.VMEM(states.shape, F32),
            pltpu.VMEM((rows, value_width), F32),
            pltpu.VMEM((rows, key_width), BF),
            pltpu.VMEM((rows, value_width), BF),
            pltpu.SemaphoreType.DMA((32,)),
        ],
        compiler_params=params(48),
        cost_estimate=cost(2 * rows * width * 2048, 20 << 20),
        name="retention",
    )(place, decay, xs, table, wq, wk, wv, wg, wo, states)


def fresh_kernel(place, owner, old, st_h, k_h, v_h, o_h, stb, kb, vb, ob, in_sems, out_sems):
    n = stb.shape[0]
    copies = [
        pltpu.make_async_copy(k_h, kb, in_sems.at[n]), pltpu.make_async_copy(v_h, vb, in_sems.at[n + 1])
    ]
    loads = [pltpu.make_async_copy(st_h.at[i], stb.at[i], in_sems.at[i]) for i in range(n)]
    stores = [pltpu.make_async_copy(ob.at[i], o_h.at[owner[i] // n], out_sems.at[i]) for i in range(n)]
    for c in copies + loads:
        c.start()
    for c in copies:
        c.wait()
    keys = kb[...].astype(F32).T
    values = vb[...]
    slot = lax.broadcasted_iota(jnp.int32, keys.shape, 1) // DRAFT
    for i in range(n):
        own = jnp.where(slot == block_slot(place, i), keys, 0.0).astype(BF)
        update = jnp.dot(own, values, preferred_element_type=F32)
        loads[i].wait()
        ob[i] = (old[i] * stb[i] + update).astype(BF)
        stores[i].start()
    for c in stores:
        c.wait()


def fresh_states(place, owner, old, states, k, v):
    n = states.shape[0]
    return pl.pallas_call(
        fresh_kernel,
        in_specs=[SM] * 3 + [ANY] * 3,
        out_specs=ANY,
        out_shape=sds(states.shape, BF),
        scratch_shapes=[
            pltpu.VMEM(states.shape, F32), pltpu.VMEM(k.shape, BF), pltpu.VMEM(v.shape, BF),
            pltpu.VMEM(states.shape, BF),
            pltpu.SemaphoreType.DMA((n + 2,)), pltpu.SemaphoreType.DMA((n,)),
        ],
        compiler_params=params(32),
        cost_estimate=cost(2 * states.size * DRAFT, states.size * 6),
        name="fresh_states",
    )(place, owner, old, states, k, v)


def widen_kernel(x_h, o_h, xb, ob, in_sems, out_sems):
    n = x_h.shape[0]
    loads = [pltpu.make_async_copy(x_h.at[i], xb.at[i], in_sems.at[i]) for i in range(n)]
    stores = [pltpu.make_async_copy(ob.at[i], o_h.at[i], out_sems.at[i]) for i in range(n)]
    for c in loads:
        c.start()
    for i in range(n):
        loads[i].wait()
        ob[i] = xb[i].astype(F32)
        stores[i].start()
    for c in stores:
        c.wait()


def widen(x):
    n = x.shape[0]
    return pl.pallas_call(
        widen_kernel, in_specs=[ANY], out_specs=ANY,
        out_shape=sds(x.shape, F32),
        scratch_shapes=[
            pltpu.VMEM(x.shape, BF), pltpu.VMEM(x.shape, F32),
            pltpu.SemaphoreType.DMA((n,)), pltpu.SemaphoreType.DMA((n,)),
        ],
        compiler_params=params(32),
        cost_estimate=cost(x.size, x.size * 6), name="widen",
    )(x)


def ring_order(me):
    return [me, (me + 3) % 4, (me + 1) % 4, (me + 2) % 4]


def ffn_kernel(place, *refs, rows_in):
    xs = refs[:8]
    w_refs = refs[8:16]
    same_ref, other_ref, xbuf, wa, wb, hid, sems = refs[16:]
    copies = []

    def send(src, dst):
        copy = pltpu.make_async_copy(src, dst, sems.at[len(copies)])
        copy.start()
        copies.append(copy)
        return copy

    c_x = [send(x, xbuf.at[pl.ds(i * rows_in, rows_in), :]) for i, x in enumerate(xs)]
    shard = xbuf.shape[1] // 16
    px, py = ring_order(place[0]), ring_order(place[1])

    def spread(refs, buf, outer, inner):
        out = []
        for i in range(16):
            at = outer[i // 4], inner[i % 4]
            where = (at[0] * 4 + at[1]) if buf is wa else (at[1] * 4 + at[0])
            rows = pl.ds(pl.multiple_of(where * shard, shard), shard)
            out.append(send(refs[i // 4].at[pl.ds(i % 4 * shard, shard), :], buf.at[rows, :]))
        return out

    c_a = spread(w_refs[:4], wa, px, py)
    c_b = spread(w_refs[4:], wb, py, px)
    for c in c_x + c_a:
        c.wait()
    x = xbuf[...]

    def act(g, u):
        return (g / (1.0 + jnp.exp(-g)) * u).astype(BF)

    g0 = jnp.dot(x, wa[:, 0:256], preferred_element_type=F32)
    u0 = jnp.dot(x, wa[:, 512:768], preferred_element_type=F32)
    hid[0] = act(g0, u0)
    g1 = jnp.dot(x, wa[:, 256:512], preferred_element_type=F32)
    for c in c_b:
        c.wait()
    u1 = jnp.dot(x, wb[:, 0:256], preferred_element_type=F32)
    hid[1] = act(g1, u1)
    rows = xbuf.shape[0] // 2
    contract = (((1,), (1,)), ((), ()))
    for j in range(xbuf.shape[1] // 512):
        cols = pl.ds(j * 512, 512)
        out = lax.dot_general(hid[0], wb[cols, 256:512], contract, preferred_element_type=F32)
        out += lax.dot_general(hid[1], wb[cols, 512:768], contract, preferred_element_type=F32)
        out = out.astype(BF)
        same_ref[:, cols] = out[:rows]
        other_ref[:, cols] = out[rows:]


def ffn(place, xs, w):
    rows_in, width = xs[0].shape
    rows = rows_in * 8
    return pl.pallas_call(
        functools.partial(ffn_kernel, rows_in=rows_in),
        out_shape=[sds((rows // 2, width), BF)] * 2,
        in_specs=[SM] + [ANY] * 16,
        out_specs=[VM] * 2,
        scratch_shapes=[
            pltpu.VMEM((rows, width), BF),
            pltpu.VMEM((width, 768), BF),
            pltpu.VMEM((width, 768), BF),
            pltpu.VMEM((2, rows, 256), BF),
            pltpu.SemaphoreType.DMA((40,)),
        ],
        compiler_params=params(32),
        cost_estimate=cost(2 * rows * width * 1536, 9 << 20),
        name="feed_forward",
    )(place, *xs, *w)


def hop(v, axis, shift):
    pairs = [
        (x * 4 + y, (x + shift) % 4 * 4 + y if axis == "x" else x * 4 + (y + shift) % 4)
        for x in range(4)
        for y in range(4)
    ]
    return lax.ppermute(v, "req", pairs)


def ring(v, axis):
    before = hop(v, axis, 1)
    return [v, before, hop(v, axis, -1), hop(before, axis, 1)]


def join_kernel(*refs):
    ins, outs, sems = refs[:8], refs[8:10], refs[10]
    rows = ins[0].shape[0]
    copies = [
        pltpu.make_async_copy(r, outs[i // 4].at[pl.ds(i % 4 * rows, rows), :], sems.at[i])
        for i, r in enumerate(ins)
    ]
    for c in copies:
        c.start()
    for c in copies:
        c.wait()


def join(a, b):
    shape = sds((a[0].shape[0] * 4, a[0].shape[1]), BF)
    return pl.pallas_call(
        join_kernel, out_shape=[shape] * 2, in_specs=[ANY] * 8, out_specs=[VM] * 2,
        scratch_shapes=[pltpu.SemaphoreType.DMA((8,))],
        compiler_params=params(4), cost_estimate=cost(0, 4 << 20), name="join",
    )(*a, *b)


def along(shift):
    return [(z * 2 + c, (z + shift) % 4 * 2 + c) for z in range(4) for c in range(2)]


SWAP = [(m, m ^ 1) for m in range(8)]


def gather_rows(x):
    mine = [x] + [lax.ppermute(x, "mlp", along(s)) for s in (1, 2, 3)]
    return mine + [lax.ppermute(v, "mlp", SWAP) for v in mine]


def pair_rows(same, other):
    return pair_sum(same, lax.ppermute(other, "mlp", SWAP), 4)


def reduce_rows(pieces):
    return [pieces[0]] + [lax.ppermute(pieces[s], "mlp", along(-s)) for s in (1, 2, 3)]


def per_device(
    tokens, cached_states, prompt_lengths, accepted, owner_slot,
    w_query, w_key, w_value, w_gate_ret, w_out, w_gate, w_up, w_down,
):
    requests, _, key_width, value_width = cached_states.shape
    states = cached_states.reshape(requests, key_width, value_width)
    req, mlp = lax.axis_index("req"), lax.axis_index("mlp")
    z, core = mlp // 2, mlp % 2
    place = jnp.stack([req // 4, req % 4, z, core]).astype(jnp.int32)
    gamma = 1.0 - jnp.exp2(-5.0 - mlp.astype(F32))
    decay = jnp.log(gamma)
    old = jnp.exp(decay * accepted.astype(F32))

    swapped = lax.ppermute(tokens, "mlp", SWAP)
    part_a, part_b, normed = prepare(w_gate, w_up, w_down, tokens, swapped)
    xs = lax.all_to_all(
        normed, "mlp", split_axis=0, concat_axis=0, tiled=True,
        axis_index_groups=[[c, 2 + c, 4 + c, 6 + c] for c in range(2)],
    )
    block_a, block_b = join(ring(part_a, "y"), ring(part_b, "x"))
    near = [hop(block_a, "x", 1), hop(block_a, "x", -1), hop(block_b, "y", 1), hop(block_b, "y", -1)]

    ids = jnp.arange(requests, dtype=jnp.int32)
    block = ids // 2
    order = ((z - block % 4) % 4 * 2 + (core + block // 4) % 2) * 2 + ids % 2
    pick = order[:, None] == ids[None, :]
    lengths = jnp.sum(jnp.where(pick, prompt_lengths[None, :], 0), axis=1)
    kept = jnp.sum(jnp.where(pick, accepted[None, :], 0), axis=1)
    rows, half = requests * DRAFT, key_width // 2
    draft = jnp.arange(DRAFT, dtype=jnp.int32)
    position = (lengths[:, None] + draft[None, :]).astype(F32).reshape(-1)
    ahead = (kept[:, None] - 1 - draft[None, :]).astype(F32).reshape(-1)
    freq = jnp.exp(-math.log(10000.0) * jnp.arange(half, dtype=F32) / half)
    angles = position[:, None] * freq[None, :]
    fade = jnp.where(ahead >= 0, jnp.exp(decay * jnp.maximum(ahead, 0.0)), 0.0)
    grow = jnp.exp(decay * (jnp.arange(rows, dtype=jnp.int32) % DRAFT + 1).astype(F32))
    wide = (rows, half)
    table = jnp.concatenate(
        [
            jnp.cos(angles), jnp.sin(angles),
            jnp.broadcast_to(fade[:, None], wide), jnp.broadcast_to(grow[:, None], wide),
        ],
        axis=1,
    )

    spot, _ = lax.optimization_barrier((place, block_a))
    same, other, k, v = retention(
        spot, decay.reshape(1), xs, table, w_query, w_key, w_value, w_gate_ret, w_out, states
    )
    near, (same, other, k, v) = lax.optimization_barrier((near, (same, other, k, v)))
    w_all = [block_a, near[0], near[1], hop(near[0], "x", 1), block_b, near[2], near[3], hop(near[2], "y", 1)]
    sums = reduce_rows(pair_rows(same, other))
    k, sums[1] = lax.optimization_barrier((k, sums[1]))
    fresh = fresh_states(place, owner_slot, old, states, k, v)
    fresh, w_all = lax.optimization_barrier((fresh, w_all))
    landed = lax.all_to_all(fresh, "req", split_axis=0, concat_axis=0, tiled=True)
    res, hidden_in = residual_rows(tokens, sums)
    same, other = ffn(place, gather_rows(hidden_in), w_all)
    mixed = final_rows(res, reduce_rows(pair_rows(same, other)))
    return mixed, widen(landed).reshape(cached_states.shape)


def solution(mesh):
    return jax.shard_map(
        per_device,
        mesh=mesh,
        in_specs=(
            P(("req", "mlp"), None),
            P("req", "mlp", None, None),
            P("req"),
            P("req"),
            P("req"),
            P(None, "mlp"),
            P(None, "mlp"),
            P(None, "mlp"),
            P(None, "mlp"),
            P("mlp", None),
            P("req", "mlp"),
            P("req", "mlp"),
            P("mlp", "req"),
        ),
        out_specs=(P(("req", "mlp"), None), P("req", "mlp", None, None)),
        check_vma=False,
    )
```

time: 156 us -> 140 us (0.90)
  the two profiles are of different devices: /device:TPU:48 before, /device:TPU:28 now
where the time goes in v2:
time: 140 us; the launch traced here: 139 us
  waiting for transfers between devices  42.9 us (31%)
  starting transfers between devices  42.1 us (30%)
  Pallas kernels  41.5 us (30%)
  local copies, waits for them, and re-layouts  6.18 us (4%)
  other arithmetic  4.81 us (3%)
    ppermute x6, waiting for transfers between devices, reduce_rows(): lax.ppermute(pieces[s], 'mlp', along(-s))  15.9 us
    ppermute x12, starting transfers between devices, hop(): return lax.ppermute(v, 'req', pairs)  13.7 us
    pallas_call x5, Pallas kernels, staged(): pl.pallas_call(kernel, out_shape=outs, in_specs=[ANY] * n, out_specs=[VM]...  10.7 us
    ppermute x6, starting transfers between devices, reduce_rows(): lax.ppermute(pieces[s], 'mlp', along(-s))  10.2 us
    pallas_call x1, Pallas kernels, retention(): pl.pallas_call(body, out_shape=[sds((rows // 2, width), BF), sds((rows //...  10.1 us
    all_to_all x1, starting transfers between devices, per_device(): lax.all_to_all(fresh, 'req', split_axis=0, concat_axis=0, tiled=True)  9.1 us
    all_to_all x1, waiting for transfers between devices, per_device(): lax.all_to_all(fresh, 'req', split_axis=0, concat_axis=0, tiled=True)  8.98 us
    pallas_call x1, Pallas kernels, ffn(): pl.pallas_call(functools.partial(ffn_kernel, rows_in=rows_in), out_shape=...  6.79 us
  transfers between devices with their start and end apart: 30, of which 18 were waited for; matrix products, arithmetic and copies ran while one was open for 5% of the time, Pallas kernels for 25%

profile of v2, /device:TPU:28, one launch (start us, length us, event | category | flops | bytes accessed | tf_op | source)
XLA Modules:
  0.0 138.7 jit_solution(14456845667662036236)
XLA Ops:
  0.9 0.9 select_reduce_fusion.1
  1.7 0.7 add_convert_fusion
  2.4 0.7 copy-done.9
  3.0 2.6 %prepare.1 = (bf16[128,768]{1,0:T(8,128)(2,1)}, bf16[128,768]{1,0:T(8,128)(2,1)}, bf16[4,64,2048]{2,1,0:T(8,128)(2,1)}) custom-call(bf16[128,512]{1,0:T(8,128)(2,1)} %refs_0_.2, bf16[128,512]{1,0:T(8,128)(2,1)} %refs_1_.1, bf16[512,128]{1,0:T(8,128)(2,1)} %refs_2_.2, bf16[32,2048]{1,0:T(8,128)(2,1)} %refs_0_.3, bf16[32,2048]{1,0:T(8,128)(2,1)} %copy-done.9), custom_call_target="tpu_custom_call" | custom-call | bytes 2097152 | tf_op jit(solution)/shard_map/prepare/pallas_call | solution.py:52
  5.9 1.2 collective-permute-start.4
  7.1 1.8 %collective-permute-start.2 = (bf16[128,768]{1,0:T(8,128)(2,1)}, bf16[128,768]{1,0:T(8,128)(2,1)S(1)}, u32[]{:S(2)}, u32[]{:S(2)}) collective-permute-start(bf16[128,768]{1,0:T(8,128)(2,1)} %get-tuple-element.43.refs_0_), channel_id=1, source_target_pairs={{0,24},{8,0},{16,8},{24,16},{32,56},{40,32},{48,40},{56,48},{64,88... | collective-permute-start | bytes 589832 | tf_op jit(solution)/shard_map/ppermute | solution.py:401
  8.9 0.8 collective-permute-start.5
  9.7 5.3 %all-to-all-start = ((bf16[4,64,2048]{2,1,0:T(8,128)(2,1)}), bf16[4,64,2048]{2,1,0:T(8,128)(2,1)S(1)}, u32[]{:S(2)}, u32[]{:S(2)}) async-start(bf16[4,64,2048]{2,1,0:T(8,128)(2,1)} %get-tuple-element.48), calls=%async_computation | async-start | bytes 2097152 | tf_op jit(solution)/shard_map/all_to_all | solution.py:466
  15.0 1.5 %collective-permute-start.3 = (bf16[128,768]{1,0:T(8,128)(2,1)S(1)}, bf16[128,768]{1,0:T(8,128)(2,1)S(1)}, u32[]{:S(2)}, u32[]{:S(2)}) collective-permute-start(bf16[128,768]{1,0:T(8,128)(2,1)S(1)} %collective-permute-done.1.refs_1_), channel_id=1, source_target_pairs={{0,8},{8,16},{16,24},{24,0},{32,40},{40,48},{48,56},{56,32},{64,72... | collective-permute-start | bytes 589832 | tf_op jit(solution)/shard_map/ppermute | solution.py:401
  16.6 1.2 collective-permute-start.6
  17.8 0.7 exponential_select_fusion
  18.5 2.6 %collective-permute-done.3.refs_3_ = bf16[128,768]{1,0:T(8,128)(2,1)S(1)} collective-permute-done((bf16[128,768]{1,0:T(8,128)(2,1)S(1)}, bf16[128,768]{1,0:T(8,128)(2,1)S(1)}, u32[]{:S(2)}, u32[]{:S(2)}) %collective-permute-start.3) | collective-permute-done | bytes 196640 | tf_op jit(solution)/shard_map/ppermute | solution.py:401
  21.0 1.4 %collective-permute-done.6.refs_7_ = bf16[128,768]{1,0:T(8,128)(2,1)} collective-permute-done((bf16[128,768]{1,0:T(8,128)(2,1)S(1)}, bf16[128,768]{1,0:T(8,128)(2,1)}, u32[]{:S(2)}, u32[]{:S(2)}) %collective-permute-start.6) | collective-permute-done | bytes 196640 | tf_op jit(solution)/shard_map/ppermute | solution.py:401
  22.4 2.7 %join.1 = (bf16[512,768]{1,0:T(8,128)(2,1)}, bf16[512,768]{1,0:T(8,128)(2,1)}) custom-call(bf16[128,768]{1,0:T(8,128)(2,1)} %get-tuple-element.43.refs_0_, bf16[128,768]{1,0:T(8,128)(2,1)} %copy-done.4, bf16[128,768]{1,0:T(8,128)(2,1)} %copy-done.6, bf16[128,768]{1,0:T(8,128)(2,1)} %copy-done.8, bf16[128,768]{1,0:T(8,128)(2,1)} %get-tuple-element.44.refs_4_, ...), custom_call_target="tpu_custom_call" | custom-call | bytes 4194304 | tf_op jit(solution)/shard_map/join/pallas_call | solution.py:424
  25.2 0.6 collective-permute-start.10
  25.8 2.7 %collective-permute-start.9 = (bf16[512,768]{1,0:T(8,128)(2,1)}, bf16[512,768]{1,0:T(8,128)(2,1)}, u32[]{:S(2)}, u32[]{:S(2)}) collective-permute-start(bf16[512,768]{1,0:T(8,128)(2,1)} %get-tuple-element.73.refs_12_), channel_id=1, source_target_pairs={{0,8},{8,16},{16,24},{24,0},{32,40},{40,48},{48,56},{56,32},{64,72... | collective-permute-start | bytes 2359304 | tf_op jit(solution)/shard_map/ppermute | solution.py:401
  28.5 0.5 collective-permute-start.8
  29.0 1.5 %collective-permute-start.7 = (bf16[512,768]{1,0:T(8,128)(2,1)}, bf16[512,768]{1,0:T(8,128)(2,1)}, u32[]{:S(2)}, u32[]{:S(2)}) collective-permute-start(bf16[512,768]{1,0:T(8,128)(2,1)} %get-tuple-element.69.refs_8_), channel_id=1, source_target_pairs={{0,32},{8,40},{16,48},{24,56},{32,64},{40,72},{48,80},{56,88},{64,... | collective-permute-start | bytes 2359304 | tf_op jit(solution)/shard_map/ppermute | solution.py:401
  30.5 0.8 reshape.159
  31.3 0.8 convert_element_type.34
  32.1 0.7 pad_add_fusion.place
  32.8 0.5 multiply_cosine_fusion
  33.5 0.8 pad_maximum_fusion.refs_1_
  34.3 1.0 copy-done
  35.3 10.1 %retention.1 = (bf16[128,2048]{1,0:T(8,128)(2,1)}, bf16[128,2048]{1,0:T(8,128)(2,1)}, bf16[256,256]{1,0:T(8,128)(2,1)}, bf16[256,512]{1,0:T(8,128)(2,1)}) custom-call(s32[4]{0:T(128)} %pad_add_fusion.place, f32[1]{0:T(128)} %bitcast.4.decay, bf16[4,64,2048]{2,1,0:T(8,128)(2,1)} %copy-done, f32[256,512]{1,0:T(8,128)} %pad_maximum_fusion.refs_1_, ...), custom_call_target="tpu_custom_call" | custom-call | flops 2147483648 | bytes 20971520 | tf_op jit(solution)/shard_map/retention/pallas_call | solution.py:222
  45.4 0.3 collective-permute-done.8.refs_10_
  45.7 2.0 %collective-permute-done.7.refs_9_ = bf16[512,768]{1,0:T(8,128)(2,1)} collective-permute-done((bf16[512,768]{1,0:T(8,128)(2,1)}, bf16[512,768]{1,0:T(8,128)(2,1)}, u32[]{:S(2)}, u32[]{:S(2)}) %collective-permute-start.7) | collective-permute-done | bytes 786464 | tf_op jit(solution)/shard_map/ppermute | solution.py:401
  47.7 0.4 collective-permute-start.22
  48.1 1.1 collective-permute-start.23
  49.2 2.2 %collective-permute-done.11.refs_1_ = bf16[128,2048]{1,0:T(8,128)(2,1)} collective-permute-done((bf16[128,2048]{1,0:T(8,128)(2,1)}, bf16[128,2048]{1,0:T(8,128)(2,1)}, u32[]{:S(2)}, u32[]{:S(2)}) %collective-permute-start.11) | collective-permute-done | bytes 524320 | tf_op jit(solution)/shard_map/ppermute | solution.py:444
  51.5 2.0 %pair_sum.2 = (bf16[32,2048]{1,0:T(8,128)(2,1)}, bf16[32,2048]{1,0:T(8,128)(2,1)}, bf16[32,2048]{1,0:T(8,128)(2,1)}, bf16[32,2048]{1,0:T(8,128)(2,1)}) custom-call(bf16[128,2048]{1,0:T(8,128)(2,1)} %get-tuple-element.53.refs_0_, bf16[128,2048]{1,0:T(8,128)(2,1)} %collective-permute-done.11.refs_1_), custom_call_target="tpu_custom_call" | custom-call | bytes 1572864 | tf_op jit(solution)/shard_map/pair_sum/pallas_call | solution.py:52
  53.5 2.9 %collective-permute-start.12 = (bf16[32,2048]{1,0:T(8,128)(2,1)}, bf16[32,2048]{1,0:T(8,128)(2,1)S(1)}, u32[]{:S(2)}, u32[]{:S(2)}) collective-permute-start(bf16[32,2048]{1,0:T(8,128)(2,1)} %get-tuple-element.57), channel_id=1, source_target_pairs={{0,6},{1,7},{2,0},{3,1},{4,2},{5,3},{6,4},{7,5},{8,14},{9,15},{10,... | collective-permute-start | bytes 393224 | tf_op jit(solution)/shard_map/ppermute | solution.py:448
  56.4 0.5 multiply_exponential_fusion.old
  56.9 2.8 %collective-permute-done.12.refs_2_ = bf16[32,2048]{1,0:T(8,128)(2,1)S(1)} collective-permute-done((bf16[32,2048]{1,0:T(8,128)(2,1)}, bf16[32,2048]{1,0:T(8,128)(2,1)S(1)}, u32[]{:S(2)}, u32[]{:S(2)}) %collective-permute-start.12) | collective-permute-done | bytes 131104 | tf_op jit(solution)/shard_map/ppermute | solution.py:448
  59.7 6.7 %fresh_states.1 = bf16[16,256,512]{2,1,0:T(8,128)(2,1)} custom-call(s32[4]{0:T(128)} %pad_add_fusion.place, s32[16]{0:T(128)} %owner.1, f32[16]{0:T(128)} %multiply_exponential_fusion.old, f32[16,256,512]{2,1,0:T(8,128)} %bitcast.10, bf16[256,256]{1,0:T(8,128)(2,1)} %get-tuple-element.63.k_h, bf16[256,512]{1,0:T(8,128)(2,1)} %get-tuple-element.64.v_h), custom_call_target="tpu_custom_call" | custom-call | flops 67108864 | bytes 12582912 | tf_op jit(solution)/shard_map/fresh_states/pallas_call | solution.py:273
  66.5 9.1 %all-to-all-start.1 = ((bf16[16,256,512]{2,1,0:T(8,128)(2,1)}), bf16[16,256,512]{2,1,0:T(8,128)(2,1)}, u32[]{:S(2)}, u32[]{:S(2)}) async-start(bf16[16,256,512]{2,1,0:T(8,128)(2,1)} %fresh_states.1), calls=%async_computation.1 | async-start | bytes 8388608 | tf_op jit(solution)/shard_map/all_to_all | solution.py:506
  75.6 2.8 %collective-permute-start.13 = (bf16[32,2048]{1,0:T(8,128)(2,1)S(1)}, bf16[32,2048]{1,0:T(8,128)(2,1)S(1)}, u32[]{:S(2)}, u32[]{:S(2)}) collective-permute-start(bf16[32,2048]{1,0:T(8,128)(2,1)S(1)} %copy-done.25), channel_id=1, source_target_pairs={{0,4},{1,5},{2,6},{3,7},{4,0},{5,1},{6,2},{7,3},{8,12},{9,13},{10,... | collective-permute-start | bytes 393224 | tf_op jit(solution)/shard_map/ppermute | solution.py:448
  78.4 1.8 %collective-permute-start.14 = (bf16[32,2048]{1,0:T(8,128)(2,1)S(1)}, bf16[32,2048]{1,0:T(8,128)(2,1)S(1)}, u32[]{:S(2)}, u32[]{:S(2)}) collective-permute-start(bf16[32,2048]{1,0:T(8,128)(2,1)S(1)} %copy-done.24), channel_id=1, source_target_pairs={{0,2},{1,3},{2,4},{3,5},{4,6},{5,7},{6,0},{7,1},{8,10},{9,11},{10,... | collective-permute-start | bytes 393224 | tf_op jit(solution)/shard_map/ppermute | solution.py:448
  80.2 2.9 %collective-permute-done.13.refs_3_ = bf16[32,2048]{1,0:T(8,128)(2,1)S(1)} collective-permute-done((bf16[32,2048]{1,0:T(8,128)(2,1)S(1)}, bf16[32,2048]{1,0:T(8,128)(2,1)S(1)}, u32[]{:S(2)}, u32[]{:S(2)}) %collective-permute-start.13) | collective-permute-done | bytes 131104 | tf_op jit(solution)/shard_map/ppermute | solution.py:448
  83.1 1.9 %collective-permute-done.14.refs_4_ = bf16[32,2048]{1,0:T(8,128)(2,1)S(1)} collective-permute-done((bf16[32,2048]{1,0:T(8,128)(2,1)S(1)}, bf16[32,2048]{1,0:T(8,128)(2,1)S(1)}, u32[]{:S(2)}, u32[]{:S(2)}) %collective-permute-start.14) | collective-permute-done | bytes 131104 | tf_op jit(solution)/shard_map/ppermute | solution.py:448
  85.0 0.6 copy-done.15
  85.6 2.1 %residual_rows.1 = (f32[32,2048]{1,0:T(8,128)}, bf16[32,2048]{1,0:T(8,128)(2,1)}) custom-call(bf16[32,2048]{1,0:T(8,128)(2,1)} %refs_0_.3, bf16[32,2048]{1,0:T(8,128)(2,1)} %get-tuple-element.55.refs_1_, bf16[32,2048]{1,0:T(8,128)(2,1)} %copy-done.10, bf16[32,2048]{1,0:T(8,128)(2,1)} %copy-done.14, bf16[32,2048]{1,0:T(8,128)(2,1)} %copy-done.15), custom_call_target="tpu_custom_call" | custom-call | bytes 1048576 | tf_op jit(solution)/shard_map/residual_rows/pallas_call | solution.py:52
  87.8 0.9 collective-permute-start.17
  88.7 1.7 %collective-permute-start.16 = (bf16[32,2048]{1,0:T(8,128)(2,1)}, bf16[32,2048]{1,0:T(8,128)(2,1)S(1)}, u32[]{:S(2)}, u32[]{:S(2)}) collective-permute-start(bf16[32,2048]{1,0:T(8,128)(2,1)} %get-tuple-element.62.refs_0_), channel_id=1, source_target_pairs={{0,4},{1,5},{2,6},{3,7},{4,0},{5,1},{6,2},{7,3},{8,12},{9,13},{10,... | collective-permute-start | bytes 393224 | tf_op jit(solution)/shard_map/ppermute | solution.py:439
  90.4 0.9 collective-permute-start.15
  91.3 2.8 %collective-permute-done.17.refs_3_ = bf16[32,2048]{1,0:T(8,128)(2,1)S(1)} collective-permute-done((bf16[32,2048]{1,0:T(8,128)(2,1)}, bf16[32,2048]{1,0:T(8,128)(2,1)S(1)}, u32[]{:S(2)}, u32[]{:S(2)}) %collective-permute-start.17) | collective-permute-done | bytes 131104 | tf_op jit(solution)/shard_map/ppermute | solution.py:439
  94.0 2.2 %collective-permute-done.16.refs_2_ = bf16[32,2048]{1,0:T(8,128)(2,1)S(1)} collective-permute-done((bf16[32,2048]{1,0:T(8,128)(2,1)}, bf16[32,2048]{1,0:T(8,128)(2,1)S(1)}, u32[]{:S(2)}, u32[]{:S(2)}) %collective-permute-start.16) | collective-permute-done | bytes 131104 | tf_op jit(solution)/shard_map/ppermute | solution.py:439
  96.3 1.2 collective-permute-done.15.refs_1_
  97.6 1.2 collective-permute-done.19.refs_5_
  98.9 0.6 copy-done.22
  99.5 6.8 %feed_forward.1 = (bf16[128,2048]{1,0:T(8,128)(2,1)}, bf16[128,2048]{1,0:T(8,128)(2,1)}) custom-call(s32[4]{0:T(128)} %pad_add_fusion.place, bf16[32,2048]{1,0:T(8,128)(2,1)} %get-tuple-element.62.refs_0_, bf16[32,2048]{1,0:T(8,128)(2,1)} %copy-done.18, bf16[32,2048]{1,0:T(8,128)(2,1)} %copy-done.17, bf16[32,2048]{1,0:T(8,128)(2,1)} %copy-done.16, ...), custom_call_target="tpu_custom_call" | custom-call | flops 1610612736 | bytes 9437184 | tf_op jit(solution)/shard_map/feed_forward/pallas_call | solution.py:377
  106.5 2.0 %collective-permute-done.24.refs_1_ = bf16[128,2048]{1,0:T(8,128)(2,1)S(1)} collective-permute-done((bf16[128,2048]{1,0:T(8,128)(2,1)}, bf16[128,2048]{1,0:T(8,128)(2,1)S(1)}, u32[]{:S(2)}, u32[]{:S(2)}) %collective-permute-start.24) | collective-permute-done | bytes 524320 | tf_op jit(solution)/shard_map/ppermute | solution.py:444
  108.5 0.8 copy-done.3
  109.3 2.0 %pair_sum.3 = (bf16[32,2048]{1,0:T(8,128)(2,1)}, bf16[32,2048]{1,0:T(8,128)(2,1)}, bf16[32,2048]{1,0:T(8,128)(2,1)}, bf16[32,2048]{1,0:T(8,128)(2,1)}) custom-call(bf16[128,2048]{1,0:T(8,128)(2,1)} %get-tuple-element.77.refs_0_, bf16[128,2048]{1,0:T(8,128)(2,1)} %copy-done.3), custom_call_target="tpu_custom_call" | custom-call | bytes 1572864 | tf_op jit(solution)/shard_map/pair_sum/pallas_call | solution.py:52
  111.3 1.3 collective-permute-start.25
  112.7 1.2 collective-permute-start.26
  113.8 0.3 collective-permute-start.27
  114.2 3.8 %collective-permute-done.25.refs_2_ = bf16[32,2048]{1,0:T(8,128)(2,1)S(1)} collective-permute-done((bf16[32,2048]{1,0:T(8,128)(2,1)}, bf16[32,2048]{1,0:T(8,128)(2,1)S(1)}, u32[]{:S(2)}, u32[]{:S(2)}) %collective-permute-start.25) | collective-permute-done | bytes 131104 | tf_op jit(solution)/shard_map/ppermute | solution.py:448
  118.0 2.8 %collective-permute-done.26.refs_3_ = bf16[32,2048]{1,0:T(8,128)(2,1)S(1)} collective-permute-done((bf16[32,2048]{1,0:T(8,128)(2,1)}, bf16[32,2048]{1,0:T(8,128)(2,1)S(1)}, u32[]{:S(2)}, u32[]{:S(2)}) %collective-permute-start.26) | collective-permute-done | bytes 131104 | tf_op jit(solution)/shard_map/ppermute | solution.py:448
  120.8 1.7 %collective-permute-done.27.refs_4_ = bf16[32,2048]{1,0:T(8,128)(2,1)S(1)} collective-permute-done((bf16[32,2048]{1,0:T(8,128)(2,1)}, bf16[32,2048]{1,0:T(8,128)(2,1)S(1)}, u32[]{:S(2)}, u32[]{:S(2)}) %collective-permute-start.27) | collective-permute-done | bytes 131104 | tf_op jit(solution)/shard_map/ppermute | solution.py:448
  122.5 0.6 copy-done.13
  123.1 1.9 %final_rows.1 = bf16[32,2048]{1,0:T(8,128)(2,1)} custom-call(f32[32,2048]{1,0:T(8,128)} %get-tuple-element.61.refs_0_, bf16[32,2048]{1,0:T(8,128)(2,1)} %get-tuple-element.79.refs_1_, bf16[32,2048]{1,0:T(8,128)(2,1)} %copy-done.11, bf16[32,2048]{1,0:T(8,128)(2,1)} %copy-done.12, bf16[32,2048]{1,0:T(8,128)(2,1)} %copy-done.13), custom_call_target="tpu_custom_call" | custom-call | bytes 917504 | tf_op jit(solution)/shard_map/final_rows/pallas_call | solution.py:52
  125.0 9.0 %all-to-all-done.1.x_h = bf16[16,256,512]{2,1,0:T(8,128)(2,1)} async-done(((bf16[16,256,512]{2,1,0:T(8,128)(2,1)}), bf16[16,256,512]{2,1,0:T(8,128)(2,1)}, u32[]{:S(2)}, u32[]{:S(2)}) %all-to-all-start.1) | async-done | bytes 4194336 | tf_op jit(solution)/shard_map/all_to_all | solution.py:506
  134.0 4.5 %widen.1 = f32[16,256,512]{2,1,0:T(8,128)} custom-call(bf16[16,256,512]{2,1,0:T(8,128)(2,1)} %all-to-all-done.1.x_h), custom_call_target="tpu_custom_call" | custom-call | flops 2097152 | bytes 12582912 | tf_op jit(solution)/shard_map/widen/pallas_call | solution.py:305
  (73 shorter events, 1.1 us)
Async XLA Ops:
  0.6 1.8 %collective-permute-start = (bf16[32,2048]{1,0:T(8,128)(2,1)}, bf16[32,2048]{1,0:T(8,128)(2,1)S(1)}, u32[]{:S(2)}, u32[]{:S(2)}) collective-permute-start(bf16[32,2048]{1,0:T(8,128)(2,1)} %refs_0_.3), channel_id=1, source_target_pairs={{0,1},{1,0},{2,3},{3,2},{4,5},{5,4},{6,7},{7,6},{8,9},{9,8},{10,11... | collective-permute-start | bytes 393224 | tf_op jit(solution)/shard_map/ppermute | solution.py:464
  2.4 0.7 copy-start.9
  5.6 9.4 %collective-permute-start.1 = (bf16[128,768]{1,0:T(8,128)(2,1)}, bf16[128,768]{1,0:T(8,128)(2,1)S(1)}, u32[]{:S(2)}, u32[]{:S(2)}) collective-permute-start(bf16[128,768]{1,0:T(8,128)(2,1)} %get-tuple-element.43.refs_0_), channel_id=1, source_target_pairs={{0,8},{8,16},{16,24},{24,0},{32,40},{40,48},{48,56},{56,32},{64,72... | collective-permute-start | bytes 589832 | tf_op jit(solution)/shard_map/ppermute | solution.py:401
  5.9 10.6 %collective-permute-start.4 = (bf16[128,768]{1,0:T(8,128)(2,1)}, bf16[128,768]{1,0:T(8,128)(2,1)S(1)}, u32[]{:S(2)}, u32[]{:S(2)}) collective-permute-start(bf16[128,768]{1,0:T(8,128)(2,1)} %get-tuple-element.44.refs_4_), channel_id=1, source_target_pairs={{0,32},{8,40},{16,48},{24,56},{32,64},{40,72},{48,80},{56,88},{64,... | collective-permute-start | bytes 589832 | tf_op jit(solution)/shard_map/ppermute | solution.py:401
  7.1 11.3 %collective-permute-start.2 = (bf16[128,768]{1,0:T(8,128)(2,1)}, bf16[128,768]{1,0:T(8,128)(2,1)S(1)}, u32[]{:S(2)}, u32[]{:S(2)}) collective-permute-start(bf16[128,768]{1,0:T(8,128)(2,1)} %get-tuple-element.43.refs_0_), channel_id=1, source_target_pairs={{0,24},{8,0},{16,8},{24,16},{32,56},{40,32},{48,40},{56,48},{64,88... | collective-permute-start | bytes 589832 | tf_op jit(solution)/shard_map/ppermute | solution.py:401
  8.9 9.5 %collective-permute-start.5 = (bf16[128,768]{1,0:T(8,128)(2,1)}, bf16[128,768]{1,0:T(8,128)(2,1)S(1)}, u32[]{:S(2)}, u32[]{:S(2)}) collective-permute-start(bf16[128,768]{1,0:T(8,128)(2,1)} %get-tuple-element.44.refs_4_), channel_id=1, source_target_pairs={{0,96},{8,104},{16,112},{24,120},{32,0},{40,8},{48,16},{56,24},{64... | collective-permute-start | bytes 589832 | tf_op jit(solution)/shard_map/ppermute | solution.py:401
  9.7 24.6 %all-to-all-start = ((bf16[4,64,2048]{2,1,0:T(8,128)(2,1)}), bf16[4,64,2048]{2,1,0:T(8,128)(2,1)S(1)}, u32[]{:S(2)}, u32[]{:S(2)}) async-start(bf16[4,64,2048]{2,1,0:T(8,128)(2,1)} %get-tuple-element.48), calls=%async_computation | async-start | bytes 2097152 | tf_op jit(solution)/shard_map/all_to_all | solution.py:466
  15.0 7.4 %copy-start.4 = (bf16[128,768]{1,0:T(8,128)(2,1)}, bf16[128,768]{1,0:T(8,128)(2,1)S(1)}, u32[]{:S(2)}) copy-start(bf16[128,768]{1,0:T(8,128)(2,1)S(1)} %collective-permute-done.1.refs_1_) | copy-start | bytes 589828
  15.0 6.0 %collective-permute-start.3 = (bf16[128,768]{1,0:T(8,128)(2,1)S(1)}, bf16[128,768]{1,0:T(8,128)(2,1)S(1)}, u32[]{:S(2)}, u32[]{:S(2)}) collective-permute-start(bf16[128,768]{1,0:T(8,128)(2,1)S(1)} %collective-permute-done.1.refs_1_), channel_id=1, source_target_pairs={{0,8},{8,16},{16,24},{24,0},{32,40},{40,48},{48,56},{56,32},{64,72... | collective-permute-start | bytes 589832 | tf_op jit(solution)/shard_map/ppermute | solution.py:401
  16.6 5.9 %copy-start.5 = (bf16[128,768]{1,0:T(8,128)(2,1)}, bf16[128,768]{1,0:T(8,128)(2,1)S(1)}, u32[]{:S(2)}) copy-start(bf16[128,768]{1,0:T(8,128)(2,1)S(1)} %collective-permute-done.4.refs_5_) | copy-start | bytes 589828
  16.6 5.9 %collective-permute-start.6 = (bf16[128,768]{1,0:T(8,128)(2,1)S(1)}, bf16[128,768]{1,0:T(8,128)(2,1)}, u32[]{:S(2)}, u32[]{:S(2)}) collective-permute-start(bf16[128,768]{1,0:T(8,128)(2,1)S(1)} %collective-permute-done.4.refs_5_), channel_id=1, source_target_pairs={{0,32},{8,40},{16,48},{24,56},{32,64},{40,72},{48,80},{56,88},{64,... | collective-permute-start | bytes 589832 | tf_op jit(solution)/shard_map/ppermute | solution.py:401
  18.4 4.0 %copy-start.6 = (bf16[128,768]{1,0:T(8,128)(2,1)}, bf16[128,768]{1,0:T(8,128)(2,1)S(1)}, u32[]{:S(2)}) copy-start(bf16[128,768]{1,0:T(8,128)(2,1)S(1)} %collective-permute-done.2.refs_2_) | copy-start | bytes 589828
  18.4 4.0 %copy-start.7 = (bf16[128,768]{1,0:T(8,128)(2,1)}, bf16[128,768]{1,0:T(8,128)(2,1)S(1)}, u32[]{:S(2)}) copy-start(bf16[128,768]{1,0:T(8,128)(2,1)S(1)} %collective-permute-done.5.refs_6_) | copy-start | bytes 589828
  21.0 1.4 %copy-start.8 = (bf16[128,768]{1,0:T(8,128)(2,1)}, bf16[128,768]{1,0:T(8,128)(2,1)S(1)}, u32[]{:S(2)}) copy-start(bf16[128,768]{1,0:T(8,128)(2,1)S(1)} %collective-permute-done.3.refs_3_) | copy-start | bytes 589828
  25.2 20.2 %collective-permute-start.10 = (bf16[512,768]{1,0:T(8,128)(2,1)}, bf16[512,768]{1,0:T(8,128)(2,1)S(1)}, u32[]{:S(2)}, u32[]{:S(2)}) collective-permute-start(bf16[512,768]{1,0:T(8,128)(2,1)} %get-tuple-element.73.refs_12_), channel_id=1, source_target_pairs={{0,24},{8,0},{16,8},{24,16},{32,56},{40,32},{48,40},{56,48},{64,88... | collective-permute-start | bytes 2359304 | tf_op jit(solution)/shard_map/ppermute | solution.py:401
  25.8 19.7 %collective-permute-start.9 = (bf16[512,768]{1,0:T(8,128)(2,1)}, bf16[512,768]{1,0:T(8,128)(2,1)}, u32[]{:S(2)}, u32[]{:S(2)}) collective-permute-start(bf16[512,768]{1,0:T(8,128)(2,1)} %get-tuple-element.73.refs_12_), channel_id=1, source_target_pairs={{0,8},{8,16},{16,24},{24,0},{32,40},{40,48},{48,56},{56,32},{64,72... | collective-permute-start | bytes 2359304 | tf_op jit(solution)/shard_map/ppermute | solution.py:401
  28.5 17.2 %collective-permute-start.8 = (bf16[512,768]{1,0:T(8,128)(2,1)}, bf16[512,768]{1,0:T(8,128)(2,1)}, u32[]{:S(2)}, u32[]{:S(2)}) collective-permute-start(bf16[512,768]{1,0:T(8,128)(2,1)} %get-tuple-element.69.refs_8_), channel_id=1, source_target_pairs={{0,96},{8,104},{16,112},{24,120},{32,0},{40,8},{48,16},{56,24},{64... | collective-permute-start | bytes 2359304 | tf_op jit(solution)/shard_map/ppermute | solution.py:401
  29.0 18.7 %collective-permute-start.7 = (bf16[512,768]{1,0:T(8,128)(2,1)}, bf16[512,768]{1,0:T(8,128)(2,1)}, u32[]{:S(2)}, u32[]{:S(2)}) collective-permute-start(bf16[512,768]{1,0:T(8,128)(2,1)} %get-tuple-element.69.refs_8_), channel_id=1, source_target_pairs={{0,32},{8,40},{16,48},{24,56},{32,64},{40,72},{48,80},{56,88},{64,... | collective-permute-start | bytes 2359304 | tf_op jit(solution)/shard_map/ppermute | solution.py:401
  34.3 1.0 copy-start
  35.3 21.0 %copy-start.23 = (s32[16]{0:T(128)S(1)}, s32[16]{0:T(128)}, u32[]{:S(2)}) copy-start(s32[16]{0:T(128)} %param.16) | copy-start | bytes 196
  45.4 21.1 %copy-start.1 = (bf16[512,768]{1,0:T(8,128)(2,1)}, bf16[512,768]{1,0:T(8,128)(2,1)S(1)}, u32[]{:S(2)}) copy-start(bf16[512,768]{1,0:T(8,128)(2,1)S(1)} %collective-permute-done.10.refs_14_) | copy-start | bytes 2359300
  47.7 18.8 %collective-permute-start.22 = (bf16[512,768]{1,0:T(8,128)(2,1)}, bf16[512,768]{1,0:T(8,128)(2,1)S(1)}, u32[]{:S(2)}, u32[]{:S(2)}) collective-permute-start(bf16[512,768]{1,0:T(8,128)(2,1)} %collective-permute-done.7.refs_9_), channel_id=1, source_target_pairs={{0,32},{8,40},{16,48},{24,56},{32,64},{40,72},{48,80},{56,88},{64,... | collective-permute-start | bytes 2359304 | tf_op jit(solution)/shard_map/ppermute | solution.py:401
  48.1 18.4 %collective-permute-start.23 = (bf16[512,768]{1,0:T(8,128)(2,1)}, bf16[512,768]{1,0:T(8,128)(2,1)}, u32[]{:S(2)}, u32[]{:S(2)}) collective-permute-start(bf16[512,768]{1,0:T(8,128)(2,1)} %collective-permute-done.9.refs_13_), channel_id=1, source_target_pairs={{0,8},{8,16},{16,24},{24,0},{32,40},{40,48},{48,56},{56,32},{64,72... | collective-permute-start | bytes 2359304 | tf_op jit(solution)/shard_map/ppermute | solution.py:401
  49.2 2.3 %collective-permute-start.11 = (bf16[128,2048]{1,0:T(8,128)(2,1)}, bf16[128,2048]{1,0:T(8,128)(2,1)}, u32[]{:S(2)}, u32[]{:S(2)}) collective-permute-start(bf16[128,2048]{1,0:T(8,128)(2,1)} %get-tuple-element.54), channel_id=1, source_target_pairs={{0,1},{1,0},{2,3},{3,2},{4,5},{5,4},{6,7},{7,6},{8,9},{9,8},{10,11... | collective-permute-start | bytes 1572872 | tf_op jit(solution)/shard_map/ppermute | solution.py:444
  53.5 6.2 %collective-permute-start.12 = (bf16[32,2048]{1,0:T(8,128)(2,1)}, bf16[32,2048]{1,0:T(8,128)(2,1)S(1)}, u32[]{:S(2)}, u32[]{:S(2)}) collective-permute-start(bf16[32,2048]{1,0:T(8,128)(2,1)} %get-tuple-element.57), channel_id=1, source_target_pairs={{0,6},{1,7},{2,0},{3,1},{4,2},{5,3},{6,4},{7,5},{8,14},{9,15},{10,... | collective-permute-start | bytes 393224 | tf_op jit(solution)/shard_map/ppermute | solution.py:448
  59.7 6.7 %copy-start.10 = (bf16[32,2048]{1,0:T(8,128)(2,1)}, bf16[32,2048]{1,0:T(8,128)(2,1)S(1)}, u32[]{:S(2)}) copy-start(bf16[32,2048]{1,0:T(8,128)(2,1)S(1)} %collective-permute-done.12.refs_2_) | copy-start | bytes 393220
  66.5 9.2 %copy-start.25 = (bf16[32,2048]{1,0:T(8,128)(2,1)S(1)}, bf16[32,2048]{1,0:T(8,128)(2,1)}, u32[]{:S(2)}) copy-start(bf16[32,2048]{1,0:T(8,128)(2,1)} %get-tuple-element.59) | copy-start | bytes 393220
  66.5 11.9 %copy-start.24 = (bf16[32,2048]{1,0:T(8,128)(2,1)S(1)}, bf16[32,2048]{1,0:T(8,128)(2,1)}, u32[]{:S(2)}) copy-start(bf16[32,2048]{1,0:T(8,128)(2,1)} %get-tuple-element.60) | copy-start | bytes 393220
  66.5 9.1 %copy-start.2 = (bf16[512,768]{1,0:T(8,128)(2,1)}, bf16[512,768]{1,0:T(8,128)(2,1)S(1)}, u32[]{:S(2)}) copy-start(bf16[512,768]{1,0:T(8,128)(2,1)S(1)} %collective-permute-done.22.refs_11_) | copy-start | bytes 2359300
  66.5 67.5 %all-to-all-start.1 = ((bf16[16,256,512]{2,1,0:T(8,128)(2,1)}), bf16[16,256,512]{2,1,0:T(8,128)(2,1)}, u32[]{:S(2)}, u32[]{:S(2)}) async-start(bf16[16,256,512]{2,1,0:T(8,128)(2,1)} %fresh_states.1), calls=%async_computation.1 | async-start | bytes 8388608 | tf_op jit(solution)/shard_map/all_to_all | solution.py:506
  75.6 7.4 %collective-permute-start.13 = (bf16[32,2048]{1,0:T(8,128)(2,1)S(1)}, bf16[32,2048]{1,0:T(8,128)(2,1)S(1)}, u32[]{:S(2)}, u32[]{:S(2)}) collective-permute-start(bf16[32,2048]{1,0:T(8,128)(2,1)S(1)} %copy-done.25), channel_id=1, source_target_pairs={{0,4},{1,5},{2,6},{3,7},{4,0},{5,1},{6,2},{7,3},{8,12},{9,13},{10,... | collective-permute-start | bytes 393224 | tf_op jit(solution)/shard_map/ppermute | solution.py:448
  78.4 6.6 %collective-permute-start.14 = (bf16[32,2048]{1,0:T(8,128)(2,1)S(1)}, bf16[32,2048]{1,0:T(8,128)(2,1)S(1)}, u32[]{:S(2)}, u32[]{:S(2)}) collective-permute-start(bf16[32,2048]{1,0:T(8,128)(2,1)S(1)} %copy-done.24), channel_id=1, source_target_pairs={{0,2},{1,3},{2,4},{3,5},{4,6},{5,7},{6,0},{7,1},{8,10},{9,11},{10,... | collective-permute-start | bytes 393224 | tf_op jit(solution)/shard_map/ppermute | solution.py:448
  83.1 1.9 %copy-start.14 = (bf16[32,2048]{1,0:T(8,128)(2,1)}, bf16[32,2048]{1,0:T(8,128)(2,1)S(1)}, u32[]{:S(2)}) copy-start(bf16[32,2048]{1,0:T(8,128)(2,1)S(1)} %collective-permute-done.13.refs_3_) | copy-start | bytes 393220
  85.0 0.6 copy-start.15
  87.8 6.2 %collective-permute-start.17 = (bf16[32,2048]{1,0:T(8,128)(2,1)}, bf16[32,2048]{1,0:T(8,128)(2,1)S(1)}, u32[]{:S(2)}, u32[]{:S(2)}) collective-permute-start(bf16[32,2048]{1,0:T(8,128)(2,1)} %get-tuple-element.62.refs_0_), channel_id=1, source_target_pairs={{0,6},{1,7},{2,0},{3,1},{4,2},{5,3},{6,4},{7,5},{8,14},{9,15},{10,... | collective-permute-start | bytes 393224 | tf_op jit(solution)/shard_map/ppermute | solution.py:439
  88.7 7.6 %collective-permute-start.16 = (bf16[32,2048]{1,0:T(8,128)(2,1)}, bf16[32,2048]{1,0:T(8,128)(2,1)S(1)}, u32[]{:S(2)}, u32[]{:S(2)}) collective-permute-start(bf16[32,2048]{1,0:T(8,128)(2,1)} %get-tuple-element.62.refs_0_), channel_id=1, source_target_pairs={{0,4},{1,5},{2,6},{3,7},{4,0},{5,1},{6,2},{7,3},{8,12},{9,13},{10,... | collective-permute-start | bytes 393224 | tf_op jit(solution)/shard_map/ppermute | solution.py:439
  90.4 7.1 %collective-permute-start.15 = (bf16[32,2048]{1,0:T(8,128)(2,1)}, bf16[32,2048]{1,0:T(8,128)(2,1)S(1)}, u32[]{:S(2)}, u32[]{:S(2)}) collective-permute-start(bf16[32,2048]{1,0:T(8,128)(2,1)} %get-tuple-element.62.refs_0_), channel_id=1, source_target_pairs={{0,2},{1,3},{2,4},{3,5},{4,6},{5,7},{6,0},{7,1},{8,10},{9,11},{10,... | collective-permute-start | bytes 393224 | tf_op jit(solution)/shard_map/ppermute | solution.py:439
  91.3 6.2 %collective-permute-start.18 = (bf16[32,2048]{1,0:T(8,128)(2,1)}, bf16[32,2048]{1,0:T(8,128)(2,1)S(1)}, u32[]{:S(2)}, u32[]{:S(2)}) collective-permute-start(bf16[32,2048]{1,0:T(8,128)(2,1)} %get-tuple-element.62.refs_0_), channel_id=1, source_target_pairs={{0,1},{1,0},{2,3},{3,2},{4,5},{5,4},{6,7},{7,6},{8,9},{9,8},{10,11... | collective-permute-start | bytes 393224 | tf_op jit(solution)/shard_map/ppermute | solution.py:440
  94.0 4.8 %copy-start.16 = (bf16[32,2048]{1,0:T(8,128)(2,1)}, bf16[32,2048]{1,0:T(8,128)(2,1)S(1)}, u32[]{:S(2)}) copy-start(bf16[32,2048]{1,0:T(8,128)(2,1)S(1)} %collective-permute-done.17.refs_3_) | copy-start | bytes 393220
  94.0 3.4 %collective-permute-start.21 = (bf16[32,2048]{1,0:T(8,128)(2,1)S(1)}, bf16[32,2048]{1,0:T(8,128)(2,1)S(1)}, u32[]{:S(2)}, u32[]{:S(2)}) collective-permute-start(bf16[32,2048]{1,0:T(8,128)(2,1)S(1)} %collective-permute-done.17.refs_3_), channel_id=1, source_target_pairs={{0,1},{1,0},{2,3},{3,2},{4,5},{5,4},{6,7},{7,6},{8,9},{9,8},{10,11... | collective-permute-start | bytes 393224 | tf_op jit(solution)/shard_map/ppermute | solution.py:440
  96.3 2.5 %copy-start.17 = (bf16[32,2048]{1,0:T(8,128)(2,1)}, bf16[32,2048]{1,0:T(8,128)(2,1)S(1)}, u32[]{:S(2)}) copy-start(bf16[32,2048]{1,0:T(8,128)(2,1)S(1)} %collective-permute-done.16.refs_2_) | copy-start | bytes 393220
  96.3 1.3 collective-permute-start.20
  97.5 1.4 copy-start.18
  97.5 1.3 collective-permute-start.19
  97.5 1.4 copy-start.19
  97.5 1.3 copy-start.20
  97.6 1.2 copy-start.21
  98.8 0.7 copy-start.22
  106.3 2.2 %collective-permute-start.24 = (bf16[128,2048]{1,0:T(8,128)(2,1)}, bf16[128,2048]{1,0:T(8,128)(2,1)S(1)}, u32[]{:S(2)}, u32[]{:S(2)}) collective-permute-start(bf16[128,2048]{1,0:T(8,128)(2,1)} %get-tuple-element.78), channel_id=1, source_target_pairs={{0,1},{1,0},{2,3},{3,2},{4,5},{5,4},{6,7},{7,6},{8,9},{9,8},{10,11... | collective-permute-start | bytes 1572872 | tf_op jit(solution)/shard_map/ppermute | solution.py:444
  108.5 0.8 copy-start.3
  111.3 6.6 %collective-permute-start.25 = (bf16[32,2048]{1,0:T(8,128)(2,1)}, bf16[32,2048]{1,0:T(8,128)(2,1)S(1)}, u32[]{:S(2)}, u32[]{:S(2)}) collective-permute-start(bf16[32,2048]{1,0:T(8,128)(2,1)} %get-tuple-element.80), channel_id=1, source_target_pairs={{0,6},{1,7},{2,0},{3,1},{4,2},{5,3},{6,4},{7,5},{8,14},{9,15},{10,... | collective-permute-start | bytes 393224 | tf_op jit(solution)/shard_map/ppermute | solution.py:448
  112.7 8.1 %collective-permute-start.26 = (bf16[32,2048]{1,0:T(8,128)(2,1)}, bf16[32,2048]{1,0:T(8,128)(2,1)S(1)}, u32[]{:S(2)}, u32[]{:S(2)}) collective-permute-start(bf16[32,2048]{1,0:T(8,128)(2,1)} %get-tuple-element.81), channel_id=1, source_target_pairs={{0,4},{1,5},{2,6},{3,7},{4,0},{5,1},{6,2},{7,3},{8,12},{9,13},{10,... | collective-permute-start | bytes 393224 | tf_op jit(solution)/shard_map/ppermute | solution.py:448
  113.8 8.6 %collective-permute-start.27 = (bf16[32,2048]{1,0:T(8,128)(2,1)}, bf16[32,2048]{1,0:T(8,128)(2,1)S(1)}, u32[]{:S(2)}, u32[]{:S(2)}) collective-permute-start(bf16[32,2048]{1,0:T(8,128)(2,1)} %get-tuple-element.82), channel_id=1, source_target_pairs={{0,2},{1,3},{2,4},{3,5},{4,6},{5,7},{6,0},{7,1},{8,10},{9,11},{10,... | collective-permute-start | bytes 393224 | tf_op jit(solution)/shard_map/ppermute | solution.py:448
  118.0 4.5 %copy-start.11 = (bf16[32,2048]{1,0:T(8,128)(2,1)}, bf16[32,2048]{1,0:T(8,128)(2,1)S(1)}, u32[]{:S(2)}) copy-start(bf16[32,2048]{1,0:T(8,128)(2,1)S(1)} %collective-permute-done.25.refs_2_) | copy-start | bytes 393220
  120.8 1.7 %copy-start.12 = (bf16[32,2048]{1,0:T(8,128)(2,1)}, bf16[32,2048]{1,0:T(8,128)(2,1)S(1)}, u32[]{:S(2)}) copy-start(bf16[32,2048]{1,0:T(8,128)(2,1)S(1)} %collective-permute-done.26.refs_3_) | copy-start | bytes 393220
  122.5 0.7 copy-start.13

commit v3 on v2

--- a/solution.py
+++ b/solution.py
@@ -27,7 +27,7 @@
 
 
 def params(mib):
-    return pltpu.CompilerParams(vmem_limit_bytes=max(mib, 62) << 20)
+    return pltpu.CompilerParams(vmem_limit_bytes=mib << 20)
 
 
 def norm(v):
@@ -36,7 +36,7 @@
     return centred * lax.rsqrt(variance + EPS)
 
 
-def staged(body, ins, outs, name, flops=0):
+def staged(body, ins, outs, name, mib=8):
     n, m = len(ins), len(outs)
 
     def kernel(*refs):
@@ -53,7 +53,7 @@
         kernel, out_shape=outs, in_specs=[ANY] * n, out_specs=[VM] * m,
         scratch_shapes=[pltpu.VMEM(v.shape, v.dtype) for v in ins]
         + [pltpu.SemaphoreType.DMA((n,))],
-        cost_estimate=cost(flops, size), compiler_params=params(16), name=name,
+        cost_estimate=cost(0, size), compiler_params=params(mib), name=name,
     )(*ins)
 
 
@@ -74,7 +74,7 @@
 def prepare(g, u, d, x, y):
     part = sds((g.shape[0], 3 * g.shape[1] // 2), BF)
     both = sds((4, 2 * x.shape[0], x.shape[1]), BF)
-    return staged(prepare_body, (g, u, d, x, y), [part, part, both], "prepare")
+    return staged(prepare_body, (g, u, d, x, y), [part, part, both], "prepare", 62)
 
 
 def pair_body(a_ref, b_ref, *o_refs):
@@ -238,7 +238,7 @@
             pltpu.VMEM((rows, value_width), BF),
             pltpu.SemaphoreType.DMA((32,)),
         ],
-        compiler_params=params(48),
+        compiler_params=params(62),
         cost_estimate=cost(2 * rows * width * 2048, 20 << 20),
         name="retention",
     )(place, decay, xs, table, wq, wk, wv, wg, wo, states)
@@ -280,7 +280,7 @@
             pltpu.VMEM(states.shape, BF),
             pltpu.SemaphoreType.DMA((n + 2,)), pltpu.SemaphoreType.DMA((n,)),
         ],
-        compiler_params=params(32),
+        compiler_params=params(62),
         cost_estimate=cost(2 * states.size * DRAFT, states.size * 6),
         name="fresh_states",
     )(place, owner, old, states, k, v)
@@ -309,7 +309,7 @@
             pltpu.VMEM(x.shape, BF), pltpu.VMEM(x.shape, F32),
             pltpu.SemaphoreType.DMA((n,)), pltpu.SemaphoreType.DMA((n,)),
         ],
-        compiler_params=params(32),
+        compiler_params=params(62),
         cost_estimate=cost(x.size, x.size * 6), name="widen",
     )(x)
 
@@ -386,7 +386,7 @@
             pltpu.VMEM((2, rows, 256), BF),
             pltpu.SemaphoreType.DMA((40,)),
         ],
-        compiler_params=params(32),
+        compiler_params=params(62),
         cost_estimate=cost(2 * rows * width * 1536, 9 << 20),
         name="feed_forward",
     )(place, *xs, *w)
@@ -424,7 +424,7 @@
     return pl.pallas_call(
         join_kernel, out_shape=[shape] * 2, in_specs=[ANY] * 8, out_specs=[VM] * 2,
         scratch_shapes=[pltpu.SemaphoreType.DMA((8,))],
-        compiler_params=params(4), cost_estimate=cost(0, 4 << 20), name="join",
+        compiler_params=params(62), cost_estimate=cost(0, 4 << 20), name="join",
     )(*a, *b)
 
 

time: 140 us -> 139 us (level)
  Pallas kernels: 41.5 us -> 36.4 us
  waiting for transfers between devices: 42.9 us -> 46.8 us
    pallas_call x5, Pallas kernels: 10.7 us -> 5.61 us  [staged(): pl.pallas_call(kernel, out_shape=outs, in_specs=[ANY] * n, out_specs=[VM]...]
    all_to_all x1, waiting for transfers between devices: 8.98 us -> 13.9 us  [per_device(): lax.all_to_all(fresh, 'req', split_axis=0, concat_axis=0, tiled=True)]
    unnamed x52 -> x40, local copies, waits for them, and re-layouts: 4.44 us -> 4.41 us
  transfers between devices with their start and end apart: 30 -> 30, of which waited for: 18 -> 17; matrix products, arithmetic and copies ran while one was open for 5% -> 5% of each run, Pallas kernels for 25% -> 21%
where the time goes in v3:
time: 139 us; the launch traced here: 137 us
  waiting for transfers between devices  46.8 us (34%)
  starting transfers between devices  42.1 us (30%)
  Pallas kernels  36.4 us (26%)
  local copies, waits for them, and re-layouts  6.15 us (4%)
  other arithmetic  4.84 us (3%)
    ppermute x6, waiting for transfers between devices, reduce_rows(): lax.ppermute(pieces[s], 'mlp', along(-s))  15.3 us
    all_to_all x1, waiting for transfers between devices, per_device(): lax.all_to_all(fresh, 'req', split_axis=0, concat_axis=0, tiled=True)  13.9 us
    ppermute x12, starting transfers between devices, hop(): return lax.ppermute(v, 'req', pairs)  13.7 us
    ppermute x6, starting transfers between devices, reduce_rows(): lax.ppermute(pieces[s], 'mlp', along(-s))  10.1 us
    pallas_call x1, Pallas kernels, retention(): pl.pallas_call(body, out_shape=[sds((rows // 2, width), BF), sds((rows //...  10.1 us
    all_to_all x1, starting transfers between devices, per_device(): lax.all_to_all(fresh, 'req', split_axis=0, concat_axis=0, tiled=True)  9.08 us
    pallas_call x1, Pallas kernels, ffn(): pl.pallas_call(functools.partial(ffn_kernel, rows_in=rows_in), out_shape=...  6.77 us
    pallas_call x1, Pallas kernels, fresh_states(): pl.pallas_call(fresh_kernel, in_specs=[SM] * 3 + [ANY] * 3, out_specs=ANY...  6.73 us
  transfers between devices with their start and end apart: 30, of which 17 were waited for; matrix products, arithmetic and copies ran while one was open for 5% of the time, Pallas kernels for 21%

profile of v3, /device:TPU:28, one launch (start us, length us, event | category | flops | bytes accessed | tf_op | source)
XLA Modules:
  0.0 137.5 jit_solution(14080715917843036804)
XLA Ops:
  0.9 0.9 select_reduce_fusion.1
  1.7 0.7 add_convert_fusion
  2.4 0.7 copy-done.11
  3.0 2.6 %prepare.1 = (bf16[128,768]{1,0:T(8,128)(2,1)}, bf16[128,768]{1,0:T(8,128)(2,1)}, bf16[4,64,2048]{2,1,0:T(8,128)(2,1)}) custom-call(bf16[128,512]{1,0:T(8,128)(2,1)} %refs_0_.2, bf16[128,512]{1,0:T(8,128)(2,1)} %refs_1_.1, bf16[512,128]{1,0:T(8,128)(2,1)} %refs_2_.2, bf16[32,2048]{1,0:T(8,128)(2,1)} %refs_0_.3, bf16[32,2048]{1,0:T(8,128)(2,1)} %copy-done.11), custom_call_target="tpu_custom_call" | custom-call | bytes 2097152 | tf_op jit(solution)/shard_map/prepare/pallas_call | solution.py:52
  5.6 0.3 collective-permute-start.1
  5.9 1.2 collective-permute-start.4
  7.1 1.8 %collective-permute-start.2 = (bf16[128,768]{1,0:T(8,128)(2,1)}, bf16[128,768]{1,0:T(8,128)(2,1)S(1)}, u32[]{:S(2)}, u32[]{:S(2)}) collective-permute-start(bf16[128,768]{1,0:T(8,128)(2,1)} %get-tuple-element.43.refs_0_), channel_id=1, source_target_pairs={{0,24},{8,0},{16,8},{24,16},{32,56},{40,32},{48,40},{56,48},{64,88... | collective-permute-start | bytes 589832 | tf_op jit(solution)/shard_map/ppermute | solution.py:401
  8.9 0.8 collective-permute-start.5
  9.7 5.3 %all-to-all-start = ((bf16[4,64,2048]{2,1,0:T(8,128)(2,1)}), bf16[4,64,2048]{2,1,0:T(8,128)(2,1)S(1)}, u32[]{:S(2)}, u32[]{:S(2)}) async-start(bf16[4,64,2048]{2,1,0:T(8,128)(2,1)} %get-tuple-element.48), calls=%async_computation | async-start | bytes 2097152 | tf_op jit(solution)/shard_map/all_to_all | solution.py:466
  15.1 1.5 %collective-permute-start.3 = (bf16[128,768]{1,0:T(8,128)(2,1)S(1)}, bf16[128,768]{1,0:T(8,128)(2,1)S(1)}, u32[]{:S(2)}, u32[]{:S(2)}) collective-permute-start(bf16[128,768]{1,0:T(8,128)(2,1)S(1)} %collective-permute-done.1.refs_1_), channel_id=1, source_target_pairs={{0,8},{8,16},{16,24},{24,0},{32,40},{40,48},{48,56},{56,32},{64,72... | collective-permute-start | bytes 589832 | tf_op jit(solution)/shard_map/ppermute | solution.py:401
  16.6 1.2 collective-permute-start.6
  17.8 0.7 exponential_select_fusion
  18.5 2.6 %collective-permute-done.3.refs_3_ = bf16[128,768]{1,0:T(8,128)(2,1)S(1)} collective-permute-done((bf16[128,768]{1,0:T(8,128)(2,1)S(1)}, bf16[128,768]{1,0:T(8,128)(2,1)S(1)}, u32[]{:S(2)}, u32[]{:S(2)}) %collective-permute-start.3) | collective-permute-done | bytes 196640 | tf_op jit(solution)/shard_map/ppermute | solution.py:401
  21.0 1.4 %collective-permute-done.6.refs_7_ = bf16[128,768]{1,0:T(8,128)(2,1)} collective-permute-done((bf16[128,768]{1,0:T(8,128)(2,1)S(1)}, bf16[128,768]{1,0:T(8,128)(2,1)}, u32[]{:S(2)}, u32[]{:S(2)}) %collective-permute-start.6) | collective-permute-done | bytes 196640 | tf_op jit(solution)/shard_map/ppermute | solution.py:401
  22.4 2.7 %join.1 = (bf16[512,768]{1,0:T(8,128)(2,1)}, bf16[512,768]{1,0:T(8,128)(2,1)}) custom-call(bf16[128,768]{1,0:T(8,128)(2,1)} %get-tuple-element.43.refs_0_, bf16[128,768]{1,0:T(8,128)(2,1)} %copy-done.6, bf16[128,768]{1,0:T(8,128)(2,1)} %copy-done.8, bf16[128,768]{1,0:T(8,128)(2,1)} %copy-done.10, bf16[128,768]{1,0:T(8,128)(2,1)} %get-tuple-element.44.refs_4_, ...), custom_call_target="tpu_custom_call" | custom-call | bytes 4194304 | tf_op jit(solution)/shard_map/join/pallas_call | solution.py:424
  25.2 0.6 collective-permute-start.10
  25.7 2.7 %collective-permute-start.9 = (bf16[512,768]{1,0:T(8,128)(2,1)}, bf16[512,768]{1,0:T(8,128)(2,1)}, u32[]{:S(2)}, u32[]{:S(2)}) collective-permute-start(bf16[512,768]{1,0:T(8,128)(2,1)} %get-tuple-element.73.refs_12_), channel_id=1, source_target_pairs={{0,8},{8,16},{16,24},{24,0},{32,40},{40,48},{48,56},{56,32},{64,72... | collective-permute-start | bytes 2359304 | tf_op jit(solution)/shard_map/ppermute | solution.py:401
  28.5 0.5 collective-permute-start.8
  29.0 1.5 %collective-permute-start.7 = (bf16[512,768]{1,0:T(8,128)(2,1)}, bf16[512,768]{1,0:T(8,128)(2,1)}, u32[]{:S(2)}, u32[]{:S(2)}) collective-permute-start(bf16[512,768]{1,0:T(8,128)(2,1)} %get-tuple-element.69.refs_8_), channel_id=1, source_target_pairs={{0,32},{8,40},{16,48},{24,56},{32,64},{40,72},{48,80},{56,88},{64,... | collective-permute-start | bytes 2359304 | tf_op jit(solution)/shard_map/ppermute | solution.py:401
  30.5 0.8 reshape.159
  31.3 0.8 convert_element_type.34
  32.1 0.7 pad_add_fusion.place
  32.7 0.5 multiply_cosine_fusion
  33.5 0.8 pad_maximum_fusion.refs_1_
  34.3 1.0 copy-done.4
  35.3 10.1 %retention.1 = (bf16[128,2048]{1,0:T(8,128)(2,1)}, bf16[128,2048]{1,0:T(8,128)(2,1)}, bf16[256,256]{1,0:T(8,128)(2,1)}, bf16[256,512]{1,0:T(8,128)(2,1)}) custom-call(s32[4]{0:T(128)} %pad_add_fusion.place, f32[1]{0:T(128)} %bitcast.4.decay, bf16[4,64,2048]{2,1,0:T(8,128)(2,1)} %copy-done.4, f32[256,512]{1,0:T(8,128)} %pad_maximum_fusion.refs_1_, ...), custom_call_target="tpu_custom_call" | custom-call | flops 2147483648 | bytes 20971520 | tf_op jit(solution)/shard_map/retention/pallas_call | solution.py:222
  45.4 0.3 collective-permute-done.8.refs_10_
  45.7 2.0 %collective-permute-done.7.refs_9_ = bf16[512,768]{1,0:T(8,128)(2,1)} collective-permute-done((bf16[512,768]{1,0:T(8,128)(2,1)}, bf16[512,768]{1,0:T(8,128)(2,1)}, u32[]{:S(2)}, u32[]{:S(2)}) %collective-permute-start.7) | collective-permute-done | bytes 786464 | tf_op jit(solution)/shard_map/ppermute | solution.py:401
  47.7 0.4 collective-permute-start.22
  48.1 1.1 collective-permute-start.23
  49.2 2.1 %collective-permute-done.11.refs_1_ = bf16[128,2048]{1,0:T(8,128)(2,1)S(1)} collective-permute-done((bf16[128,2048]{1,0:T(8,128)(2,1)}, bf16[128,2048]{1,0:T(8,128)(2,1)S(1)}, u32[]{:S(2)}, u32[]{:S(2)}) %collective-permute-start.11) | collective-permute-done | bytes 524320 | tf_op jit(solution)/shard_map/ppermute | solution.py:444
  51.3 1.0 copy-done.1
  52.4 0.2 pair_sum.2
  52.6 2.9 %collective-permute-start.12 = (bf16[32,2048]{1,0:T(8,128)(2,1)S(1)}, bf16[32,2048]{1,0:T(8,128)(2,1)S(1)}, u32[]{:S(2)}, u32[]{:S(2)}) collective-permute-start(bf16[32,2048]{1,0:T(8,128)(2,1)S(1)} %get-tuple-element.57), channel_id=1, source_target_pairs={{0,6},{1,7},{2,0},{3,1},{4,2},{5,3},{6,4},{7,5},{8,14},{9,15},{10,... | collective-permute-start | bytes 393224 | tf_op jit(solution)/shard_map/ppermute | solution.py:448
  55.5 0.5 multiply_exponential_fusion.old
  56.0 2.5 %collective-permute-done.12.refs_2_ = bf16[32,2048]{1,0:T(8,128)(2,1)S(1)} collective-permute-done((bf16[32,2048]{1,0:T(8,128)(2,1)S(1)}, bf16[32,2048]{1,0:T(8,128)(2,1)S(1)}, u32[]{:S(2)}, u32[]{:S(2)}) %collective-permute-start.12) | collective-permute-done | bytes 131104 | tf_op jit(solution)/shard_map/ppermute | solution.py:448
  58.5 6.7 %fresh_states.1 = bf16[16,256,512]{2,1,0:T(8,128)(2,1)} custom-call(s32[4]{0:T(128)} %pad_add_fusion.place, s32[16]{0:T(128)} %owner.1, f32[16]{0:T(128)} %multiply_exponential_fusion.old, f32[16,256,512]{2,1,0:T(8,128)} %bitcast.10, bf16[256,256]{1,0:T(8,128)(2,1)} %get-tuple-element.63.k_h, bf16[256,512]{1,0:T(8,128)(2,1)} %get-tuple-element.64.v_h), custom_call_target="tpu_custom_call" | custom-call | flops 67108864 | bytes 12582912 | tf_op jit(solution)/shard_map/fresh_states/pallas_call | solution.py:273
  65.3 9.1 %all-to-all-start.1 = ((bf16[16,256,512]{2,1,0:T(8,128)(2,1)}), bf16[16,256,512]{2,1,0:T(8,128)(2,1)}, u32[]{:S(2)}, u32[]{:S(2)}) async-start(bf16[16,256,512]{2,1,0:T(8,128)(2,1)} %fresh_states.1), calls=%async_computation.1 | async-start | bytes 8388608 | tf_op jit(solution)/shard_map/all_to_all | solution.py:506
  74.4 2.8 %collective-permute-start.13 = (bf16[32,2048]{1,0:T(8,128)(2,1)S(1)}, bf16[32,2048]{1,0:T(8,128)(2,1)S(1)}, u32[]{:S(2)}, u32[]{:S(2)}) collective-permute-start(bf16[32,2048]{1,0:T(8,128)(2,1)S(1)} %get-tuple-element.59), channel_id=1, source_target_pairs={{0,4},{1,5},{2,6},{3,7},{4,0},{5,1},{6,2},{7,3},{8,12},{9,13},{10,... | collective-permute-start | bytes 393224 | tf_op jit(solution)/shard_map/ppermute | solution.py:448
  77.2 1.8 %collective-permute-start.14 = (bf16[32,2048]{1,0:T(8,128)(2,1)S(1)}, bf16[32,2048]{1,0:T(8,128)(2,1)S(1)}, u32[]{:S(2)}, u32[]{:S(2)}) collective-permute-start(bf16[32,2048]{1,0:T(8,128)(2,1)S(1)} %get-tuple-element.60), channel_id=1, source_target_pairs={{0,2},{1,3},{2,4},{3,5},{4,6},{5,7},{6,0},{7,1},{8,10},{9,11},{10,... | collective-permute-start | bytes 393224 | tf_op jit(solution)/shard_map/ppermute | solution.py:448
  78.9 2.9 %collective-permute-done.13.refs_3_ = bf16[32,2048]{1,0:T(8,128)(2,1)S(1)} collective-permute-done((bf16[32,2048]{1,0:T(8,128)(2,1)S(1)}, bf16[32,2048]{1,0:T(8,128)(2,1)S(1)}, u32[]{:S(2)}, u32[]{:S(2)}) %collective-permute-start.13) | collective-permute-done | bytes 131104 | tf_op jit(solution)/shard_map/ppermute | solution.py:448
  81.8 1.8 %collective-permute-done.14.refs_4_ = bf16[32,2048]{1,0:T(8,128)(2,1)S(1)} collective-permute-done((bf16[32,2048]{1,0:T(8,128)(2,1)S(1)}, bf16[32,2048]{1,0:T(8,128)(2,1)S(1)}, u32[]{:S(2)}, u32[]{:S(2)}) %collective-permute-start.14) | collective-permute-done | bytes 131104 | tf_op jit(solution)/shard_map/ppermute | solution.py:448
  83.7 1.2 residual_rows.1
  84.8 1.0 collective-permute-start.17
  85.8 1.7 %collective-permute-start.16 = (bf16[32,2048]{1,0:T(8,128)(2,1)S(1)}, bf16[32,2048]{1,0:T(8,128)(2,1)S(1)}, u32[]{:S(2)}, u32[]{:S(2)}) collective-permute-start(bf16[32,2048]{1,0:T(8,128)(2,1)S(1)} %get-tuple-element.62.refs_0_), channel_id=1, source_target_pairs={{0,4},{1,5},{2,6},{3,7},{4,0},{5,1},{6,2},{7,3},{8,12},{9,13},{10,... | collective-permute-start | bytes 393224 | tf_op jit(solution)/shard_map/ppermute | solution.py:439
  87.5 0.9 collective-permute-start.15
  88.4 2.4 %collective-permute-done.17.refs_3_ = bf16[32,2048]{1,0:T(8,128)(2,1)S(1)} collective-permute-done((bf16[32,2048]{1,0:T(8,128)(2,1)S(1)}, bf16[32,2048]{1,0:T(8,128)(2,1)S(1)}, u32[]{:S(2)}, u32[]{:S(2)}) %collective-permute-start.17) | collective-permute-done | bytes 131104 | tf_op jit(solution)/shard_map/ppermute | solution.py:439
  90.8 2.2 %collective-permute-done.16.refs_2_ = bf16[32,2048]{1,0:T(8,128)(2,1)S(1)} collective-permute-done((bf16[32,2048]{1,0:T(8,128)(2,1)S(1)}, bf16[32,2048]{1,0:T(8,128)(2,1)S(1)}, u32[]{:S(2)}, u32[]{:S(2)}) %collective-permute-start.16) | collective-permute-done | bytes 131104 | tf_op jit(solution)/shard_map/ppermute | solution.py:439
  93.0 1.3 collective-permute-done.15.refs_1_
  94.4 1.3 collective-permute-done.19.refs_5_
  95.8 0.6 copy-done.18
  96.4 6.8 %feed_forward.1 = (bf16[128,2048]{1,0:T(8,128)(2,1)}, bf16[128,2048]{1,0:T(8,128)(2,1)}) custom-call(s32[4]{0:T(128)} %pad_add_fusion.place, bf16[32,2048]{1,0:T(8,128)(2,1)} %copy-done.3, bf16[32,2048]{1,0:T(8,128)(2,1)} %copy-done.14, bf16[32,2048]{1,0:T(8,128)(2,1)} %copy-done.13, bf16[32,2048]{1,0:T(8,128)(2,1)} %copy-done.12, ...), custom_call_target="tpu_custom_call" | custom-call | flops 1610612736 | bytes 9437184 | tf_op jit(solution)/shard_map/feed_forward/pallas_call | solution.py:377
  103.2 0.2 collective-permute-start.24
  103.4 2.0 %collective-permute-done.24.refs_1_ = bf16[128,2048]{1,0:T(8,128)(2,1)S(1)} collective-permute-done((bf16[128,2048]{1,0:T(8,128)(2,1)}, bf16[128,2048]{1,0:T(8,128)(2,1)S(1)}, u32[]{:S(2)}, u32[]{:S(2)}) %collective-permute-start.24) | collective-permute-done | bytes 524320 | tf_op jit(solution)/shard_map/ppermute | solution.py:444
  105.4 1.0 copy-done.2
  106.7 1.2 collective-permute-start.25
  107.8 1.2 collective-permute-start.26
  109.1 0.3 collective-permute-start.27
  109.4 3.7 %collective-permute-done.25.refs_2_ = bf16[32,2048]{1,0:T(8,128)(2,1)S(1)} collective-permute-done((bf16[32,2048]{1,0:T(8,128)(2,1)S(1)}, bf16[32,2048]{1,0:T(8,128)(2,1)S(1)}, u32[]{:S(2)}, u32[]{:S(2)}) %collective-permute-start.25) | collective-permute-done | bytes 131104 | tf_op jit(solution)/shard_map/ppermute | solution.py:448
  113.1 2.6 %collective-permute-done.26.refs_3_ = bf16[32,2048]{1,0:T(8,128)(2,1)S(1)} collective-permute-done((bf16[32,2048]{1,0:T(8,128)(2,1)S(1)}, bf16[32,2048]{1,0:T(8,128)(2,1)S(1)}, u32[]{:S(2)}, u32[]{:S(2)}) %collective-permute-start.26) | collective-permute-done | bytes 131104 | tf_op jit(solution)/shard_map/ppermute | solution.py:448
  115.7 1.7 %collective-permute-done.27.refs_4_ = bf16[32,2048]{1,0:T(8,128)(2,1)S(1)} collective-permute-done((bf16[32,2048]{1,0:T(8,128)(2,1)S(1)}, bf16[32,2048]{1,0:T(8,128)(2,1)S(1)}, u32[]{:S(2)}, u32[]{:S(2)}) %collective-permute-start.27) | collective-permute-done | bytes 131104 | tf_op jit(solution)/shard_map/ppermute | solution.py:448
  117.4 1.5 %final_rows.1 = bf16[32,2048]{1,0:T(8,128)(2,1)} custom-call(f32[32,2048]{1,0:T(8,128)S(1)} %get-tuple-element.61.refs_0_, bf16[32,2048]{1,0:T(8,128)(2,1)S(1)} %get-tuple-element.79.refs_1_, bf16[32,2048]{1,0:T(8,128)(2,1)S(1)} %collective-permute-done.25.refs_2_, bf16[32,2048]{1,0:T(8,128)(2,1)S(1)} %collective-permute-done.26.refs_3_, ...), custom_call_target="tpu_custom_call" | custom-call | bytes 917504 | tf_op jit(solution)/shard_map/final_rows/pallas_call | solution.py:52
  118.9 13.9 %all-to-all-done.1.x_h = bf16[16,256,512]{2,1,0:T(8,128)(2,1)} async-done(((bf16[16,256,512]{2,1,0:T(8,128)(2,1)}), bf16[16,256,512]{2,1,0:T(8,128)(2,1)}, u32[]{:S(2)}, u32[]{:S(2)}) %all-to-all-start.1) | async-done | bytes 4194336 | tf_op jit(solution)/shard_map/all_to_all | solution.py:506
  132.8 4.5 %widen.1 = f32[16,256,512]{2,1,0:T(8,128)} custom-call(bf16[16,256,512]{2,1,0:T(8,128)(2,1)} %all-to-all-done.1.x_h), custom_call_target="tpu_custom_call" | custom-call | flops 2097152 | bytes 12582912 | tf_op jit(solution)/shard_map/widen/pallas_call | solution.py:305
  (61 shorter events, 0.6 us)
Async XLA Ops:
  0.6 1.8 %collective-permute-start = (bf16[32,2048]{1,0:T(8,128)(2,1)}, bf16[32,2048]{1,0:T(8,128)(2,1)S(1)}, u32[]{:S(2)}, u32[]{:S(2)}) collective-permute-start(bf16[32,2048]{1,0:T(8,128)(2,1)} %refs_0_.3), channel_id=1, source_target_pairs={{0,1},{1,0},{2,3},{3,2},{4,5},{5,4},{6,7},{7,6},{8,9},{9,8},{10,11... | collective-permute-start | bytes 393224 | tf_op jit(solution)/shard_map/ppermute | solution.py:464
  2.4 0.7 copy-start.11
  5.6 9.4 %collective-permute-start.1 = (bf16[128,768]{1,0:T(8,128)(2,1)}, bf16[128,768]{1,0:T(8,128)(2,1)S(1)}, u32[]{:S(2)}, u32[]{:S(2)}) collective-permute-start(bf16[128,768]{1,0:T(8,128)(2,1)} %get-tuple-element.43.refs_0_), channel_id=1, source_target_pairs={{0,8},{8,16},{16,24},{24,0},{32,40},{40,48},{48,56},{56,32},{64,72... | collective-permute-start | bytes 589832 | tf_op jit(solution)/shard_map/ppermute | solution.py:401
  5.9 10.6 %collective-permute-start.4 = (bf16[128,768]{1,0:T(8,128)(2,1)}, bf16[128,768]{1,0:T(8,128)(2,1)S(1)}, u32[]{:S(2)}, u32[]{:S(2)}) collective-permute-start(bf16[128,768]{1,0:T(8,128)(2,1)} %get-tuple-element.44.refs_4_), channel_id=1, source_target_pairs={{0,32},{8,40},{16,48},{24,56},{32,64},{40,72},{48,80},{56,88},{64,... | collective-permute-start | bytes 589832 | tf_op jit(solution)/shard_map/ppermute | solution.py:401
  7.1 11.3 %collective-permute-start.2 = (bf16[128,768]{1,0:T(8,128)(2,1)}, bf16[128,768]{1,0:T(8,128)(2,1)S(1)}, u32[]{:S(2)}, u32[]{:S(2)}) collective-permute-start(bf16[128,768]{1,0:T(8,128)(2,1)} %get-tuple-element.43.refs_0_), channel_id=1, source_target_pairs={{0,24},{8,0},{16,8},{24,16},{32,56},{40,32},{48,40},{56,48},{64,88... | collective-permute-start | bytes 589832 | tf_op jit(solution)/shard_map/ppermute | solution.py:401
  8.9 9.5 %collective-permute-start.5 = (bf16[128,768]{1,0:T(8,128)(2,1)}, bf16[128,768]{1,0:T(8,128)(2,1)S(1)}, u32[]{:S(2)}, u32[]{:S(2)}) collective-permute-start(bf16[128,768]{1,0:T(8,128)(2,1)} %get-tuple-element.44.refs_4_), channel_id=1, source_target_pairs={{0,96},{8,104},{16,112},{24,120},{32,0},{40,8},{48,16},{56,24},{64... | collective-permute-start | bytes 589832 | tf_op jit(solution)/shard_map/ppermute | solution.py:401
  9.7 24.6 %all-to-all-start = ((bf16[4,64,2048]{2,1,0:T(8,128)(2,1)}), bf16[4,64,2048]{2,1,0:T(8,128)(2,1)S(1)}, u32[]{:S(2)}, u32[]{:S(2)}) async-start(bf16[4,64,2048]{2,1,0:T(8,128)(2,1)} %get-tuple-element.48), calls=%async_computation | async-start | bytes 2097152 | tf_op jit(solution)/shard_map/all_to_all | solution.py:466
  15.0 7.4 %copy-start.6 = (bf16[128,768]{1,0:T(8,128)(2,1)}, bf16[128,768]{1,0:T(8,128)(2,1)S(1)}, u32[]{:S(2)}) copy-start(bf16[128,768]{1,0:T(8,128)(2,1)S(1)} %collective-permute-done.1.refs_1_) | copy-start | bytes 589828
  15.1 6.0 %collective-permute-start.3 = (bf16[128,768]{1,0:T(8,128)(2,1)S(1)}, bf16[128,768]{1,0:T(8,128)(2,1)S(1)}, u32[]{:S(2)}, u32[]{:S(2)}) collective-permute-start(bf16[128,768]{1,0:T(8,128)(2,1)S(1)} %collective-permute-done.1.refs_1_), channel_id=1, source_target_pairs={{0,8},{8,16},{16,24},{24,0},{32,40},{40,48},{48,56},{56,32},{64,72... | collective-permute-start | bytes 589832 | tf_op jit(solution)/shard_map/ppermute | solution.py:401
  16.6 5.9 %copy-start.7 = (bf16[128,768]{1,0:T(8,128)(2,1)}, bf16[128,768]{1,0:T(8,128)(2,1)S(1)}, u32[]{:S(2)}) copy-start(bf16[128,768]{1,0:T(8,128)(2,1)S(1)} %collective-permute-done.4.refs_5_) | copy-start | bytes 589828
  16.6 5.9 %collective-permute-start.6 = (bf16[128,768]{1,0:T(8,128)(2,1)S(1)}, bf16[128,768]{1,0:T(8,128)(2,1)}, u32[]{:S(2)}, u32[]{:S(2)}) collective-permute-start(bf16[128,768]{1,0:T(8,128)(2,1)S(1)} %collective-permute-done.4.refs_5_), channel_id=1, source_target_pairs={{0,32},{8,40},{16,48},{24,56},{32,64},{40,72},{48,80},{56,88},{64,... | collective-permute-start | bytes 589832 | tf_op jit(solution)/shard_map/ppermute | solution.py:401
  18.4 4.0 %copy-start.8 = (bf16[128,768]{1,0:T(8,128)(2,1)}, bf16[128,768]{1,0:T(8,128)(2,1)S(1)}, u32[]{:S(2)}) copy-start(bf16[128,768]{1,0:T(8,128)(2,1)S(1)} %collective-permute-done.2.refs_2_) | copy-start | bytes 589828
  18.4 4.0 %copy-start.9 = (bf16[128,768]{1,0:T(8,128)(2,1)}, bf16[128,768]{1,0:T(8,128)(2,1)S(1)}, u32[]{:S(2)}) copy-start(bf16[128,768]{1,0:T(8,128)(2,1)S(1)} %collective-permute-done.5.refs_6_) | copy-start | bytes 589828
  21.0 1.4 %copy-start.10 = (bf16[128,768]{1,0:T(8,128)(2,1)}, bf16[128,768]{1,0:T(8,128)(2,1)S(1)}, u32[]{:S(2)}) copy-start(bf16[128,768]{1,0:T(8,128)(2,1)S(1)} %collective-permute-done.3.refs_3_) | copy-start | bytes 589828
  25.2 20.2 %collective-permute-start.10 = (bf16[512,768]{1,0:T(8,128)(2,1)}, bf16[512,768]{1,0:T(8,128)(2,1)S(1)}, u32[]{:S(2)}, u32[]{:S(2)}) collective-permute-start(bf16[512,768]{1,0:T(8,128)(2,1)} %get-tuple-element.73.refs_12_), channel_id=1, source_target_pairs={{0,24},{8,0},{16,8},{24,16},{32,56},{40,32},{48,40},{56,48},{64,88... | collective-permute-start | bytes 2359304 | tf_op jit(solution)/shard_map/ppermute | solution.py:401
  25.7 19.6 %collective-permute-start.9 = (bf16[512,768]{1,0:T(8,128)(2,1)}, bf16[512,768]{1,0:T(8,128)(2,1)}, u32[]{:S(2)}, u32[]{:S(2)}) collective-permute-start(bf16[512,768]{1,0:T(8,128)(2,1)} %get-tuple-element.73.refs_12_), channel_id=1, source_target_pairs={{0,8},{8,16},{16,24},{24,0},{32,40},{40,48},{48,56},{56,32},{64,72... | collective-permute-start | bytes 2359304 | tf_op jit(solution)/shard_map/ppermute | solution.py:401
  28.5 17.2 %collective-permute-start.8 = (bf16[512,768]{1,0:T(8,128)(2,1)}, bf16[512,768]{1,0:T(8,128)(2,1)}, u32[]{:S(2)}, u32[]{:S(2)}) collective-permute-start(bf16[512,768]{1,0:T(8,128)(2,1)} %get-tuple-element.69.refs_8_), channel_id=1, source_target_pairs={{0,96},{8,104},{16,112},{24,120},{32,0},{40,8},{48,16},{56,24},{64... | collective-permute-start | bytes 2359304 | tf_op jit(solution)/shard_map/ppermute | solution.py:401
  29.0 18.7 %collective-permute-start.7 = (bf16[512,768]{1,0:T(8,128)(2,1)}, bf16[512,768]{1,0:T(8,128)(2,1)}, u32[]{:S(2)}, u32[]{:S(2)}) collective-permute-start(bf16[512,768]{1,0:T(8,128)(2,1)} %get-tuple-element.69.refs_8_), channel_id=1, source_target_pairs={{0,32},{8,40},{16,48},{24,56},{32,64},{40,72},{48,80},{56,88},{64,... | collective-permute-start | bytes 2359304 | tf_op jit(solution)/shard_map/ppermute | solution.py:401
  34.3 1.0 copy-start.4
  35.3 20.2 %copy-start.19 = (s32[16]{0:T(128)S(1)}, s32[16]{0:T(128)}, u32[]{:S(2)}) copy-start(s32[16]{0:T(128)} %param.16) | copy-start | bytes 196
  45.4 19.9 %copy-start.5 = (bf16[512,768]{1,0:T(8,128)(2,1)}, bf16[512,768]{1,0:T(8,128)(2,1)S(1)}, u32[]{:S(2)}) copy-start(bf16[512,768]{1,0:T(8,128)(2,1)S(1)} %collective-permute-done.10.refs_14_) | copy-start | bytes 2359300
  47.7 17.6 %collective-permute-start.22 = (bf16[512,768]{1,0:T(8,128)(2,1)}, bf16[512,768]{1,0:T(8,128)(2,1)}, u32[]{:S(2)}, u32[]{:S(2)}) collective-permute-start(bf16[512,768]{1,0:T(8,128)(2,1)} %collective-permute-done.7.refs_9_), channel_id=1, source_target_pairs={{0,32},{8,40},{16,48},{24,56},{32,64},{40,72},{48,80},{56,88},{64,... | collective-permute-start | bytes 2359304 | tf_op jit(solution)/shard_map/ppermute | solution.py:401
  48.1 17.2 %collective-permute-start.23 = (bf16[512,768]{1,0:T(8,128)(2,1)}, bf16[512,768]{1,0:T(8,128)(2,1)}, u32[]{:S(2)}, u32[]{:S(2)}) collective-permute-start(bf16[512,768]{1,0:T(8,128)(2,1)} %collective-permute-done.9.refs_13_), channel_id=1, source_target_pairs={{0,8},{8,16},{16,24},{24,0},{32,40},{40,48},{48,56},{56,32},{64,72... | collective-permute-start | bytes 2359304 | tf_op jit(solution)/shard_map/ppermute | solution.py:401
  49.2 2.1 %collective-permute-start.11 = (bf16[128,2048]{1,0:T(8,128)(2,1)}, bf16[128,2048]{1,0:T(8,128)(2,1)S(1)}, u32[]{:S(2)}, u32[]{:S(2)}) collective-permute-start(bf16[128,2048]{1,0:T(8,128)(2,1)} %get-tuple-element.54), channel_id=1, source_target_pairs={{0,1},{1,0},{2,3},{3,2},{4,5},{5,4},{6,7},{7,6},{8,9},{9,8},{10,11... | collective-permute-start | bytes 1572872 | tf_op jit(solution)/shard_map/ppermute | solution.py:444
  51.3 1.0 copy-start.1
  52.6 5.9 %collective-permute-start.12 = (bf16[32,2048]{1,0:T(8,128)(2,1)S(1)}, bf16[32,2048]{1,0:T(8,128)(2,1)S(1)}, u32[]{:S(2)}, u32[]{:S(2)}) collective-permute-start(bf16[32,2048]{1,0:T(8,128)(2,1)S(1)} %get-tuple-element.57), channel_id=1, source_target_pairs={{0,6},{1,7},{2,0},{3,1},{4,2},{5,3},{6,4},{7,5},{8,14},{9,15},{10,... | collective-permute-start | bytes 393224 | tf_op jit(solution)/shard_map/ppermute | solution.py:448
  65.3 18.4 %copy-start = (bf16[32,2048]{1,0:T(8,128)(2,1)S(1)}, bf16[32,2048]{1,0:T(8,128)(2,1)}, u32[]{:S(2)}) copy-start(bf16[32,2048]{1,0:T(8,128)(2,1)} %refs_0_.3) | copy-start | bytes 393220
  65.3 67.5 %all-to-all-start.1 = ((bf16[16,256,512]{2,1,0:T(8,128)(2,1)}), bf16[16,256,512]{2,1,0:T(8,128)(2,1)}, u32[]{:S(2)}, u32[]{:S(2)}) async-start(bf16[16,256,512]{2,1,0:T(8,128)(2,1)} %fresh_states.1), calls=%async_computation.1 | async-start | bytes 8388608 | tf_op jit(solution)/shard_map/all_to_all | solution.py:506
  74.4 7.5 %collective-permute-start.13 = (bf16[32,2048]{1,0:T(8,128)(2,1)S(1)}, bf16[32,2048]{1,0:T(8,128)(2,1)S(1)}, u32[]{:S(2)}, u32[]{:S(2)}) collective-permute-start(bf16[32,2048]{1,0:T(8,128)(2,1)S(1)} %get-tuple-element.59), channel_id=1, source_target_pairs={{0,4},{1,5},{2,6},{3,7},{4,0},{5,1},{6,2},{7,3},{8,12},{9,13},{10,... | collective-permute-start | bytes 393224 | tf_op jit(solution)/shard_map/ppermute | solution.py:448
  77.2 6.5 %collective-permute-start.14 = (bf16[32,2048]{1,0:T(8,128)(2,1)S(1)}, bf16[32,2048]{1,0:T(8,128)(2,1)S(1)}, u32[]{:S(2)}, u32[]{:S(2)}) collective-permute-start(bf16[32,2048]{1,0:T(8,128)(2,1)S(1)} %get-tuple-element.60), channel_id=1, source_target_pairs={{0,2},{1,3},{2,4},{3,5},{4,6},{5,7},{6,0},{7,1},{8,10},{9,11},{10,... | collective-permute-start | bytes 393224 | tf_op jit(solution)/shard_map/ppermute | solution.py:448
  84.8 10.9 %copy-start.3 = (bf16[32,2048]{1,0:T(8,128)(2,1)}, bf16[32,2048]{1,0:T(8,128)(2,1)S(1)}, u32[]{:S(2)}) copy-start(bf16[32,2048]{1,0:T(8,128)(2,1)S(1)} %get-tuple-element.62.refs_0_) | copy-start | bytes 393220
  84.8 6.0 %collective-permute-start.17 = (bf16[32,2048]{1,0:T(8,128)(2,1)S(1)}, bf16[32,2048]{1,0:T(8,128)(2,1)S(1)}, u32[]{:S(2)}, u32[]{:S(2)}) collective-permute-start(bf16[32,2048]{1,0:T(8,128)(2,1)S(1)} %get-tuple-element.62.refs_0_), channel_id=1, source_target_pairs={{0,6},{1,7},{2,0},{3,1},{4,2},{5,3},{6,4},{7,5},{8,14},{9,15},{10,... | collective-permute-start | bytes 393224 | tf_op jit(solution)/shard_map/ppermute | solution.py:439
  85.8 7.2 %collective-permute-start.16 = (bf16[32,2048]{1,0:T(8,128)(2,1)S(1)}, bf16[32,2048]{1,0:T(8,128)(2,1)S(1)}, u32[]{:S(2)}, u32[]{:S(2)}) collective-permute-start(bf16[32,2048]{1,0:T(8,128)(2,1)S(1)} %get-tuple-element.62.refs_0_), channel_id=1, source_target_pairs={{0,4},{1,5},{2,6},{3,7},{4,0},{5,1},{6,2},{7,3},{8,12},{9,13},{10,... | collective-permute-start | bytes 393224 | tf_op jit(solution)/shard_map/ppermute | solution.py:439
  87.5 6.8 %collective-permute-start.15 = (bf16[32,2048]{1,0:T(8,128)(2,1)S(1)}, bf16[32,2048]{1,0:T(8,128)(2,1)S(1)}, u32[]{:S(2)}, u32[]{:S(2)}) collective-permute-start(bf16[32,2048]{1,0:T(8,128)(2,1)S(1)} %get-tuple-element.62.refs_0_), channel_id=1, source_target_pairs={{0,2},{1,3},{2,4},{3,5},{4,6},{5,7},{6,0},{7,1},{8,10},{9,11},{10,... | collective-permute-start | bytes 393224 | tf_op jit(solution)/shard_map/ppermute | solution.py:439
  88.4 6.0 %collective-permute-start.18 = (bf16[32,2048]{1,0:T(8,128)(2,1)S(1)}, bf16[32,2048]{1,0:T(8,128)(2,1)S(1)}, u32[]{:S(2)}, u32[]{:S(2)}) collective-permute-start(bf16[32,2048]{1,0:T(8,128)(2,1)S(1)} %get-tuple-element.62.refs_0_), channel_id=1, source_target_pairs={{0,1},{1,0},{2,3},{3,2},{4,5},{5,4},{6,7},{7,6},{8,9},{9,8},{10,11... | collective-permute-start | bytes 393224 | tf_op jit(solution)/shard_map/ppermute | solution.py:440
  90.8 4.9 %copy-start.12 = (bf16[32,2048]{1,0:T(8,128)(2,1)}, bf16[32,2048]{1,0:T(8,128)(2,1)S(1)}, u32[]{:S(2)}) copy-start(bf16[32,2048]{1,0:T(8,128)(2,1)S(1)} %collective-permute-done.17.refs_3_) | copy-start | bytes 393220
  90.8 3.6 %collective-permute-start.21 = (bf16[32,2048]{1,0:T(8,128)(2,1)S(1)}, bf16[32,2048]{1,0:T(8,128)(2,1)S(1)}, u32[]{:S(2)}, u32[]{:S(2)}) collective-permute-start(bf16[32,2048]{1,0:T(8,128)(2,1)S(1)} %collective-permute-done.17.refs_3_), channel_id=1, source_target_pairs={{0,1},{1,0},{2,3},{3,2},{4,5},{5,4},{6,7},{7,6},{8,9},{9,8},{10,11... | collective-permute-start | bytes 393224 | tf_op jit(solution)/shard_map/ppermute | solution.py:440
  93.0 2.7 %copy-start.13 = (bf16[32,2048]{1,0:T(8,128)(2,1)}, bf16[32,2048]{1,0:T(8,128)(2,1)S(1)}, u32[]{:S(2)}) copy-start(bf16[32,2048]{1,0:T(8,128)(2,1)S(1)} %collective-permute-done.16.refs_2_) | copy-start | bytes 393220
  93.0 1.4 %collective-permute-start.20 = (bf16[32,2048]{1,0:T(8,128)(2,1)S(1)}, bf16[32,2048]{1,0:T(8,128)(2,1)S(1)}, u32[]{:S(2)}, u32[]{:S(2)}) collective-permute-start(bf16[32,2048]{1,0:T(8,128)(2,1)S(1)} %collective-permute-done.16.refs_2_), channel_id=1, source_target_pairs={{0,1},{1,0},{2,3},{3,2},{4,5},{5,4},{6,7},{7,6},{8,9},{9,8},{10,11... | collective-permute-start | bytes 393224 | tf_op jit(solution)/shard_map/ppermute | solution.py:440
  94.4 1.4 copy-start.14
  94.4 1.3 collective-permute-start.19
  94.4 1.4 copy-start.15
  94.4 1.4 copy-start.16
  94.4 1.3 copy-start.17
  95.8 0.7 copy-start.18
  103.2 2.2 %collective-permute-start.24 = (bf16[128,2048]{1,0:T(8,128)(2,1)}, bf16[128,2048]{1,0:T(8,128)(2,1)S(1)}, u32[]{:S(2)}, u32[]{:S(2)}) collective-permute-start(bf16[128,2048]{1,0:T(8,128)(2,1)} %get-tuple-element.78), channel_id=1, source_target_pairs={{0,1},{1,0},{2,3},{3,2},{4,5},{5,4},{6,7},{7,6},{8,9},{9,8},{10,11... | collective-permute-start | bytes 1572872 | tf_op jit(solution)/shard_map/ppermute | solution.py:444
  105.4 1.0 copy-start.2
  106.7 6.4 %collective-permute-start.25 = (bf16[32,2048]{1,0:T(8,128)(2,1)S(1)}, bf16[32,2048]{1,0:T(8,128)(2,1)S(1)}, u32[]{:S(2)}, u32[]{:S(2)}) collective-permute-start(bf16[32,2048]{1,0:T(8,128)(2,1)S(1)} %get-tuple-element.80), channel_id=1, source_target_pairs={{0,6},{1,7},{2,0},{3,1},{4,2},{5,3},{6,4},{7,5},{8,14},{9,15},{10,... | collective-permute-start | bytes 393224 | tf_op jit(solution)/shard_map/ppermute | solution.py:448
  107.8 7.9 %collective-permute-start.26 = (bf16[32,2048]{1,0:T(8,128)(2,1)S(1)}, bf16[32,2048]{1,0:T(8,128)(2,1)S(1)}, u32[]{:S(2)}, u32[]{:S(2)}) collective-permute-start(bf16[32,2048]{1,0:T(8,128)(2,1)S(1)} %get-tuple-element.81), channel_id=1, source_target_pairs={{0,4},{1,5},{2,6},{3,7},{4,0},{5,1},{6,2},{7,3},{8,12},{9,13},{10,... | collective-permute-start | bytes 393224 | tf_op jit(solution)/shard_map/ppermute | solution.py:448
  109.1 8.3 %collective-permute-start.27 = (bf16[32,2048]{1,0:T(8,128)(2,1)S(1)}, bf16[32,2048]{1,0:T(8,128)(2,1)S(1)}, u32[]{:S(2)}, u32[]{:S(2)}) collective-permute-start(bf16[32,2048]{1,0:T(8,128)(2,1)S(1)} %get-tuple-element.82), channel_id=1, source_target_pairs={{0,2},{1,3},{2,4},{3,5},{4,6},{5,7},{6,0},{7,1},{8,10},{9,11},{10,... | collective-permute-start | bytes 393224 | tf_op jit(solution)/shard_map/ppermute | solution.py:448

commit v4 on v3

--- a/solution.py
+++ b/solution.py
@@ -467,8 +467,6 @@
         normed, "mlp", split_axis=0, concat_axis=0, tiled=True,
         axis_index_groups=[[c, 2 + c, 4 + c, 6 + c] for c in range(2)],
     )
-    block_a, block_b = join(ring(part_a, "y"), ring(part_b, "x"))
-    near = [hop(block_a, "x", 1), hop(block_a, "x", -1), hop(block_b, "y", 1), hop(block_b, "y", -1)]
 
     ids = jnp.arange(requests, dtype=jnp.int32)
     block = ids // 2
@@ -493,14 +491,19 @@
         axis=1,
     )
 
+    ring_a, ring_b = ring(part_a, "y"), ring(part_b, "x")
+    ring_a[0], table = lax.optimization_barrier((ring_a[0], table))
+    block_a, block_b = join(ring_a, ring_b)
+    near = [hop(block_a, "x", 1), hop(block_a, "x", -1), hop(block_b, "y", 1), hop(block_b, "y", -1)]
+
     spot, _ = lax.optimization_barrier((place, block_a))
     same, other, k, v = retention(
         spot, decay.reshape(1), xs, table, w_query, w_key, w_value, w_gate_ret, w_out, states
     )
-    near, (same, other, k, v) = lax.optimization_barrier((near, (same, other, k, v)))
+    near[0], near[2], (same, other, k, v) = lax.optimization_barrier((near[0], near[2], (same, other, k, v)))
     w_all = [block_a, near[0], near[1], hop(near[0], "x", 1), block_b, near[2], near[3], hop(near[2], "y", 1)]
     sums = reduce_rows(pair_rows(same, other))
-    k, sums[1] = lax.optimization_barrier((k, sums[1]))
+    k, sums[1], near[1], near[3] = lax.optimization_barrier((k, sums[1], near[1], near[3]))
     fresh = fresh_states(place, owner_slot, old, states, k, v)
     fresh, w_all = lax.optimization_barrier((fresh, w_all))
     landed = lax.all_to_all(fresh, "req", split_axis=0, concat_axis=0, tiled=True)

time: 139 us -> 138 us (level)
  waiting for transfers between devices: 46.8 us -> 49 us
    all_to_all x1, waiting for transfers between devices: 13.9 us -> 15.3 us  [per_device(): lax.all_to_all(fresh, 'req', split_axis=0, concat_axis=0, tiled=True)]
  transfers between devices with their start and end apart: 30 -> 30, of which waited for: 17 -> 17; matrix products, arithmetic and copies ran while one was open for 5% -> 4% of each run, Pallas kernels for 21% -> 21%
where the time goes in v4:
time: 138 us
  waiting for transfers between devices  49 us (36%)
  starting transfers between devices  41.5 us (30%)
  Pallas kernels  36.4 us (26%)
  local copies, waits for them, and re-layouts  5.93 us (4%)
  other arithmetic  3.65 us (3%)
    all_to_all x1, waiting for transfers between devices, per_device(): lax.all_to_all(fresh, 'req', split_axis=0, concat_axis=0, tiled=True)  15.3 us
    ppermute x6, waiting for transfers between devices, reduce_rows(): lax.ppermute(pieces[s], 'mlp', along(-s))  15.2 us
    ppermute x12, starting transfers between devices, hop(): return lax.ppermute(v, 'req', pairs)  13.6 us
    ppermute x6, starting transfers between devices, reduce_rows(): lax.ppermute(pieces[s], 'mlp', along(-s))  10.1 us
    pallas_call x1, Pallas kernels, retention(): pl.pallas_call(body, out_shape=[sds((rows // 2, width), BF), sds((rows //...  10.1 us
    all_to_all x1, starting transfers between devices, per_device(): lax.all_to_all(fresh, 'req', split_axis=0, concat_axis=0, tiled=True)  8.58 us
    ppermute x12, waiting for transfers between devices, hop(): return lax.ppermute(v, 'req', pairs)  7.05 us
    pallas_call x1, Pallas kernels, ffn(): pl.pallas_call(functools.partial(ffn_kernel, rows_in=rows_in), out_shape=...  6.77 us
  transfers between devices with their start and end apart: 30, of which 17 were waited for; matrix products, arithmetic and copies ran while one was open for 4% of the time, Pallas kernels for 21%

profile of v4, /device:TPU:28, one launch (start us, length us, event | category | flops | bytes accessed | tf_op | source)
XLA Modules:
  0.0 137.7 jit_solution(16419541314070232713)
XLA Ops:
  0.6 0.1 collective-permute-start
  0.9 0.9 select_reduce_fusion.1
  1.9 0.6 reshape.159
  2.6 0.6 copy-done.11
  3.3 2.6 %prepare.1 = (bf16[128,768]{1,0:T(8,128)(2,1)}, bf16[128,768]{1,0:T(8,128)(2,1)}, bf16[4,64,2048]{2,1,0:T(8,128)(2,1)}) custom-call(bf16[128,512]{1,0:T(8,128)(2,1)} %refs_0_.2, bf16[128,512]{1,0:T(8,128)(2,1)} %refs_1_.1, bf16[512,128]{1,0:T(8,128)(2,1)} %refs_2_.2, bf16[32,2048]{1,0:T(8,128)(2,1)} %refs_0_.3, bf16[32,2048]{1,0:T(8,128)(2,1)} %copy-done.11), custom_call_target="tpu_custom_call" | custom-call | bytes 2097152 | tf_op jit(solution)/shard_map/prepare/pallas_call | solution.py:52
  5.8 0.3 collective-permute-start.1
  6.1 1.2 collective-permute-start.4
  7.3 0.5 multiply_cosine_fusion
  7.8 1.9 %collective-permute-start.2 = (bf16[128,768]{1,0:T(8,128)(2,1)}, bf16[128,768]{1,0:T(8,128)(2,1)S(1)}, u32[]{:S(2)}, u32[]{:S(2)}) collective-permute-start(bf16[128,768]{1,0:T(8,128)(2,1)} %get-tuple-element.44.refs_0_), channel_id=1, source_target_pairs={{0,24},{8,0},{16,8},{24,16},{32,56},{40,32},{48,40},{56,48},{64,88... | collective-permute-start | bytes 589832 | tf_op jit(solution)/shard_map/ppermute | solution.py:401
  9.7 0.8 collective-permute-start.5
  10.6 5.3 %all-to-all-start = ((bf16[4,64,2048]{2,1,0:T(8,128)(2,1)}), bf16[4,64,2048]{2,1,0:T(8,128)(2,1)S(1)}, u32[]{:S(2)}, u32[]{:S(2)}) async-start(bf16[4,64,2048]{2,1,0:T(8,128)(2,1)} %get-tuple-element.49), calls=%async_computation | async-start | bytes 2097152 | tf_op jit(solution)/shard_map/all_to_all | solution.py:466
  15.9 1.5 %collective-permute-start.3 = (bf16[128,768]{1,0:T(8,128)(2,1)S(1)}, bf16[128,768]{1,0:T(8,128)(2,1)S(1)}, u32[]{:S(2)}, u32[]{:S(2)}) collective-permute-start(bf16[128,768]{1,0:T(8,128)(2,1)S(1)} %collective-permute-done.1.refs_1_), channel_id=1, source_target_pairs={{0,8},{8,16},{16,24},{24,0},{32,40},{40,48},{48,56},{56,32},{64,72... | collective-permute-start | bytes 589832 | tf_op jit(solution)/shard_map/ppermute | solution.py:401
  17.4 1.2 collective-permute-start.6
  18.6 0.7 broadcast_in_dim.44
  19.3 0.1 broadcast_in_dim.45
  19.4 0.8 pad_maximum_fusion.refs_1_
  20.3 1.6 %collective-permute-done.3.refs_3_ = bf16[128,768]{1,0:T(8,128)(2,1)S(1)} collective-permute-done((bf16[128,768]{1,0:T(8,128)(2,1)S(1)}, bf16[128,768]{1,0:T(8,128)(2,1)S(1)}, u32[]{:S(2)}, u32[]{:S(2)}) %collective-permute-start.3) | collective-permute-done | bytes 196640 | tf_op jit(solution)/shard_map/ppermute | solution.py:401
  21.8 1.4 %collective-permute-done.6.refs_7_ = bf16[128,768]{1,0:T(8,128)(2,1)} collective-permute-done((bf16[128,768]{1,0:T(8,128)(2,1)S(1)}, bf16[128,768]{1,0:T(8,128)(2,1)}, u32[]{:S(2)}, u32[]{:S(2)}) %collective-permute-start.6) | collective-permute-done | bytes 196640 | tf_op jit(solution)/shard_map/ppermute | solution.py:401
  23.3 2.7 %join.1 = (bf16[512,768]{1,0:T(8,128)(2,1)}, bf16[512,768]{1,0:T(8,128)(2,1)}) custom-call(bf16[128,768]{1,0:T(8,128)(2,1)} %get-tuple-element.44.refs_0_, bf16[128,768]{1,0:T(8,128)(2,1)} %copy-done.6, bf16[128,768]{1,0:T(8,128)(2,1)} %copy-done.8, bf16[128,768]{1,0:T(8,128)(2,1)} %copy-done.10, bf16[128,768]{1,0:T(8,128)(2,1)} %get-tuple-element.45.refs_4_, ...), custom_call_target="tpu_custom_call" | custom-call | bytes 4194304 | tf_op jit(solution)/shard_map/join/pallas_call | solution.py:424
  26.0 2.1 %collective-permute-start.8 = (bf16[512,768]{1,0:T(8,128)(2,1)}, bf16[512,768]{1,0:T(8,128)(2,1)S(1)}, u32[]{:S(2)}, u32[]{:S(2)}) collective-permute-start(bf16[512,768]{1,0:T(8,128)(2,1)} %get-tuple-element.73.refs_12_), channel_id=1, source_target_pairs={{0,8},{8,16},{16,24},{24,0},{32,40},{40,48},{48,56},{56,32},{64,72... | collective-permute-start | bytes 2359304 | tf_op jit(solution)/shard_map/ppermute | solution.py:401
  28.1 1.2 collective-permute-start.7
  29.3 0.7 pad_add_fusion.place
  29.9 0.8 collective-permute-start.11
  30.8 1.0 copy-done.4
  31.7 10.1 %retention.1 = (bf16[128,2048]{1,0:T(8,128)(2,1)}, bf16[128,2048]{1,0:T(8,128)(2,1)}, bf16[256,256]{1,0:T(8,128)(2,1)}, bf16[256,512]{1,0:T(8,128)(2,1)}) custom-call(s32[4]{0:T(128)} %pad_add_fusion.place, f32[1]{0:T(128)} %bitcast.4.decay, bf16[4,64,2048]{2,1,0:T(8,128)(2,1)} %copy-done.4, f32[256,512]{1,0:T(8,128)} %pad_maximum_fusion.refs_1_, ...), custom_call_target="tpu_custom_call" | custom-call | flops 2147483648 | bytes 20971520 | tf_op jit(solution)/shard_map/retention/pallas_call | solution.py:222
  41.8 1.9 %collective-permute-done.8.refs_13_ = bf16[512,768]{1,0:T(8,128)(2,1)S(1)} collective-permute-done((bf16[512,768]{1,0:T(8,128)(2,1)}, bf16[512,768]{1,0:T(8,128)(2,1)S(1)}, u32[]{:S(2)}, u32[]{:S(2)}) %collective-permute-start.8) | collective-permute-done | bytes 786464 | tf_op jit(solution)/shard_map/ppermute | solution.py:401
  43.7 2.1 %collective-permute-done.7.refs_9_ = bf16[512,768]{1,0:T(8,128)(2,1)} collective-permute-done((bf16[512,768]{1,0:T(8,128)(2,1)}, bf16[512,768]{1,0:T(8,128)(2,1)}, u32[]{:S(2)}, u32[]{:S(2)}) %collective-permute-start.7) | collective-permute-done | bytes 786464 | tf_op jit(solution)/shard_map/ppermute | solution.py:401
  45.8 1.2 collective-permute-start.22
  47.0 1.4 %collective-permute-start.23 = (bf16[512,768]{1,0:T(8,128)(2,1)S(1)}, bf16[512,768]{1,0:T(8,128)(2,1)}, u32[]{:S(2)}, u32[]{:S(2)}) collective-permute-start(bf16[512,768]{1,0:T(8,128)(2,1)S(1)} %collective-permute-done.8.refs_13_), channel_id=1, source_target_pairs={{0,8},{8,16},{16,24},{24,0},{32,40},{40,48},{48,56},{56,32},{64,72... | collective-permute-start | bytes 2359304 | tf_op jit(solution)/shard_map/ppermute | solution.py:401
  48.4 2.1 %collective-permute-done.9.refs_1_ = bf16[128,2048]{1,0:T(8,128)(2,1)S(1)} collective-permute-done((bf16[128,2048]{1,0:T(8,128)(2,1)}, bf16[128,2048]{1,0:T(8,128)(2,1)S(1)}, u32[]{:S(2)}, u32[]{:S(2)}) %collective-permute-start.9) | collective-permute-done | bytes 524320 | tf_op jit(solution)/shard_map/ppermute | solution.py:444
  50.6 1.0 copy-done.1
  51.6 0.2 pair_sum.2
  51.8 2.9 %collective-permute-start.10 = (bf16[32,2048]{1,0:T(8,128)(2,1)S(1)}, bf16[32,2048]{1,0:T(8,128)(2,1)S(1)}, u32[]{:S(2)}, u32[]{:S(2)}) collective-permute-start(bf16[32,2048]{1,0:T(8,128)(2,1)S(1)} %get-tuple-element.59), channel_id=1, source_target_pairs={{0,6},{1,7},{2,0},{3,1},{4,2},{5,3},{6,4},{7,5},{8,14},{9,15},{10,... | collective-permute-start | bytes 393224 | tf_op jit(solution)/shard_map/ppermute | solution.py:448
  54.7 0.6 multiply_exponential_fusion.old
  55.3 2.5 %collective-permute-done.10.refs_2_ = bf16[32,2048]{1,0:T(8,128)(2,1)S(1)} collective-permute-done((bf16[32,2048]{1,0:T(8,128)(2,1)S(1)}, bf16[32,2048]{1,0:T(8,128)(2,1)S(1)}, u32[]{:S(2)}, u32[]{:S(2)}) %collective-permute-start.10) | collective-permute-done | bytes 131104 | tf_op jit(solution)/shard_map/ppermute | solution.py:448
  57.7 6.7 %fresh_states.1 = bf16[16,256,512]{2,1,0:T(8,128)(2,1)} custom-call(s32[4]{0:T(128)} %pad_add_fusion.place, s32[16]{0:T(128)} %owner.1, f32[16]{0:T(128)} %multiply_exponential_fusion.old, f32[16,256,512]{2,1,0:T(8,128)} %bitcast.10, bf16[256,256]{1,0:T(8,128)(2,1)} %get-tuple-element.65.k_h, bf16[256,512]{1,0:T(8,128)(2,1)} %get-tuple-element.66.v_h), custom_call_target="tpu_custom_call" | custom-call | flops 67108864 | bytes 12582912 | tf_op jit(solution)/shard_map/fresh_states/pallas_call | solution.py:273
  64.5 8.6 %all-to-all-start.1 = ((bf16[16,256,512]{2,1,0:T(8,128)(2,1)}), bf16[16,256,512]{2,1,0:T(8,128)(2,1)}, u32[]{:S(2)}, u32[]{:S(2)}) async-start(bf16[16,256,512]{2,1,0:T(8,128)(2,1)} %fresh_states.1), calls=%async_computation.1 | async-start | bytes 8388608 | tf_op jit(solution)/shard_map/all_to_all | solution.py:509
  73.1 2.8 %collective-permute-start.13 = (bf16[32,2048]{1,0:T(8,128)(2,1)S(1)}, bf16[32,2048]{1,0:T(8,128)(2,1)S(1)}, u32[]{:S(2)}, u32[]{:S(2)}) collective-permute-start(bf16[32,2048]{1,0:T(8,128)(2,1)S(1)} %get-tuple-element.61), channel_id=1, source_target_pairs={{0,4},{1,5},{2,6},{3,7},{4,0},{5,1},{6,2},{7,3},{8,12},{9,13},{10,... | collective-permute-start | bytes 393224 | tf_op jit(solution)/shard_map/ppermute | solution.py:448
  75.9 1.8 %collective-permute-start.14 = (bf16[32,2048]{1,0:T(8,128)(2,1)S(1)}, bf16[32,2048]{1,0:T(8,128)(2,1)S(1)}, u32[]{:S(2)}, u32[]{:S(2)}) collective-permute-start(bf16[32,2048]{1,0:T(8,128)(2,1)S(1)} %get-tuple-element.62), channel_id=1, source_target_pairs={{0,2},{1,3},{2,4},{3,5},{4,6},{5,7},{6,0},{7,1},{8,10},{9,11},{10,... | collective-permute-start | bytes 393224 | tf_op jit(solution)/shard_map/ppermute | solution.py:448
  77.7 2.9 %collective-permute-done.13.refs_3_ = bf16[32,2048]{1,0:T(8,128)(2,1)S(1)} collective-permute-done((bf16[32,2048]{1,0:T(8,128)(2,1)S(1)}, bf16[32,2048]{1,0:T(8,128)(2,1)S(1)}, u32[]{:S(2)}, u32[]{:S(2)}) %collective-permute-start.13) | collective-permute-done | bytes 131104 | tf_op jit(solution)/shard_map/ppermute | solution.py:448
  80.6 1.8 %collective-permute-done.14.refs_4_ = bf16[32,2048]{1,0:T(8,128)(2,1)S(1)} collective-permute-done((bf16[32,2048]{1,0:T(8,128)(2,1)S(1)}, bf16[32,2048]{1,0:T(8,128)(2,1)S(1)}, u32[]{:S(2)}, u32[]{:S(2)}) %collective-permute-start.14) | collective-permute-done | bytes 131104 | tf_op jit(solution)/shard_map/ppermute | solution.py:448
  82.4 1.2 residual_rows.1
  83.6 1.0 collective-permute-start.17
  84.5 1.7 %collective-permute-start.16 = (bf16[32,2048]{1,0:T(8,128)(2,1)S(1)}, bf16[32,2048]{1,0:T(8,128)(2,1)S(1)}, u32[]{:S(2)}, u32[]{:S(2)}) collective-permute-start(bf16[32,2048]{1,0:T(8,128)(2,1)S(1)} %get-tuple-element.64.refs_0_), channel_id=1, source_target_pairs={{0,4},{1,5},{2,6},{3,7},{4,0},{5,1},{6,2},{7,3},{8,12},{9,13},{10,... | collective-permute-start | bytes 393224 | tf_op jit(solution)/shard_map/ppermute | solution.py:439
  86.3 0.9 collective-permute-start.15
  87.1 2.4 %collective-permute-done.17.refs_3_ = bf16[32,2048]{1,0:T(8,128)(2,1)S(1)} collective-permute-done((bf16[32,2048]{1,0:T(8,128)(2,1)S(1)}, bf16[32,2048]{1,0:T(8,128)(2,1)S(1)}, u32[]{:S(2)}, u32[]{:S(2)}) %collective-permute-start.17) | collective-permute-done | bytes 131104 | tf_op jit(solution)/shard_map/ppermute | solution.py:439
  89.5 2.2 %collective-permute-done.16.refs_2_ = bf16[32,2048]{1,0:T(8,128)(2,1)S(1)} collective-permute-done((bf16[32,2048]{1,0:T(8,128)(2,1)S(1)}, bf16[32,2048]{1,0:T(8,128)(2,1)S(1)}, u32[]{:S(2)}, u32[]{:S(2)}) %collective-permute-start.16) | collective-permute-done | bytes 131104 | tf_op jit(solution)/shard_map/ppermute | solution.py:439
  91.8 1.3 collective-permute-done.15.refs_1_
  93.2 1.3 collective-permute-done.19.refs_5_
  94.5 0.6 copy-done.18
  95.2 6.8 %feed_forward.1 = (bf16[128,2048]{1,0:T(8,128)(2,1)}, bf16[128,2048]{1,0:T(8,128)(2,1)}) custom-call(s32[4]{0:T(128)} %pad_add_fusion.place, bf16[32,2048]{1,0:T(8,128)(2,1)} %copy-done.3, bf16[32,2048]{1,0:T(8,128)(2,1)} %copy-done.14, bf16[32,2048]{1,0:T(8,128)(2,1)} %copy-done.13, bf16[32,2048]{1,0:T(8,128)(2,1)} %copy-done.12, ...), custom_call_target="tpu_custom_call" | custom-call | flops 1610612736 | bytes 9437184 | tf_op jit(solution)/shard_map/feed_forward/pallas_call | solution.py:377
  101.9 0.2 collective-permute-start.24
  102.1 2.0 %collective-permute-done.24.refs_1_ = bf16[128,2048]{1,0:T(8,128)(2,1)S(1)} collective-permute-done((bf16[128,2048]{1,0:T(8,128)(2,1)}, bf16[128,2048]{1,0:T(8,128)(2,1)S(1)}, u32[]{:S(2)}, u32[]{:S(2)}) %collective-permute-start.24) | collective-permute-done | bytes 524320 | tf_op jit(solution)/shard_map/ppermute | solution.py:444
  104.1 1.0 copy-done.2
  105.2 0.2 pair_sum.3
  105.4 1.2 collective-permute-start.25
  106.6 1.2 collective-permute-start.26
  107.8 0.3 collective-permute-start.27
  108.1 3.7 %collective-permute-done.25.refs_2_ = bf16[32,2048]{1,0:T(8,128)(2,1)S(1)} collective-permute-done((bf16[32,2048]{1,0:T(8,128)(2,1)S(1)}, bf16[32,2048]{1,0:T(8,128)(2,1)S(1)}, u32[]{:S(2)}, u32[]{:S(2)}) %collective-permute-start.25) | collective-permute-done | bytes 131104 | tf_op jit(solution)/shard_map/ppermute | solution.py:448
  111.8 2.6 %collective-permute-done.26.refs_3_ = bf16[32,2048]{1,0:T(8,128)(2,1)S(1)} collective-permute-done((bf16[32,2048]{1,0:T(8,128)(2,1)S(1)}, bf16[32,2048]{1,0:T(8,128)(2,1)S(1)}, u32[]{:S(2)}, u32[]{:S(2)}) %collective-permute-start.26) | collective-permute-done | bytes 131104 | tf_op jit(solution)/shard_map/ppermute | solution.py:448
  114.4 1.7 %collective-permute-done.27.refs_4_ = bf16[32,2048]{1,0:T(8,128)(2,1)S(1)} collective-permute-done((bf16[32,2048]{1,0:T(8,128)(2,1)S(1)}, bf16[32,2048]{1,0:T(8,128)(2,1)S(1)}, u32[]{:S(2)}, u32[]{:S(2)}) %collective-permute-start.27) | collective-permute-done | bytes 131104 | tf_op jit(solution)/shard_map/ppermute | solution.py:448
  116.1 1.5 %final_rows.1 = bf16[32,2048]{1,0:T(8,128)(2,1)} custom-call(f32[32,2048]{1,0:T(8,128)S(1)} %get-tuple-element.63.refs_0_, bf16[32,2048]{1,0:T(8,128)(2,1)S(1)} %get-tuple-element.79.refs_1_, bf16[32,2048]{1,0:T(8,128)(2,1)S(1)} %collective-permute-done.25.refs_2_, bf16[32,2048]{1,0:T(8,128)(2,1)S(1)} %collective-permute-done.26.refs_3_, ...), custom_call_target="tpu_custom_call" | custom-call | bytes 917504 | tf_op jit(solution)/shard_map/final_rows/pallas_call | solution.py:52
  117.6 15.3 %all-to-all-done.1.x_h = bf16[16,256,512]{2,1,0:T(8,128)(2,1)} async-done(((bf16[16,256,512]{2,1,0:T(8,128)(2,1)}), bf16[16,256,512]{2,1,0:T(8,128)(2,1)}, u32[]{:S(2)}, u32[]{:S(2)}) %all-to-all-start.1) | async-done | bytes 4194336 | tf_op jit(solution)/shard_map/all_to_all | solution.py:509
  133.0 4.5 %widen.1 = f32[16,256,512]{2,1,0:T(8,128)} custom-call(bf16[16,256,512]{2,1,0:T(8,128)(2,1)} %all-to-all-done.1.x_h), custom_call_target="tpu_custom_call" | custom-call | flops 2097152 | bytes 12582912 | tf_op jit(solution)/shard_map/widen/pallas_call | solution.py:305
  (61 shorter events, 0.4 us)
Async XLA Ops:
  0.6 2.0 %collective-permute-start = (bf16[32,2048]{1,0:T(8,128)(2,1)}, bf16[32,2048]{1,0:T(8,128)(2,1)S(1)}, u32[]{:S(2)}, u32[]{:S(2)}) collective-permute-start(bf16[32,2048]{1,0:T(8,128)(2,1)} %refs_0_.3), channel_id=1, source_target_pairs={{0,1},{1,0},{2,3},{3,2},{4,5},{5,4},{6,7},{7,6},{8,9},{9,8},{10,11... | collective-permute-start | bytes 393224 | tf_op jit(solution)/shard_map/ppermute | solution.py:464
  2.6 0.7 copy-start.11
  5.8 10.0 %collective-permute-start.1 = (bf16[128,768]{1,0:T(8,128)(2,1)}, bf16[128,768]{1,0:T(8,128)(2,1)S(1)}, u32[]{:S(2)}, u32[]{:S(2)}) collective-permute-start(bf16[128,768]{1,0:T(8,128)(2,1)} %get-tuple-element.44.refs_0_), channel_id=1, source_target_pairs={{0,8},{8,16},{16,24},{24,0},{32,40},{40,48},{48,56},{56,32},{64,72... | collective-permute-start | bytes 589832 | tf_op jit(solution)/shard_map/ppermute | solution.py:401
  6.1 11.2 %collective-permute-start.4 = (bf16[128,768]{1,0:T(8,128)(2,1)}, bf16[128,768]{1,0:T(8,128)(2,1)S(1)}, u32[]{:S(2)}, u32[]{:S(2)}) collective-permute-start(bf16[128,768]{1,0:T(8,128)(2,1)} %get-tuple-element.45.refs_4_), channel_id=1, source_target_pairs={{0,32},{8,40},{16,48},{24,56},{32,64},{40,72},{48,80},{56,88},{64,... | collective-permute-start | bytes 589832 | tf_op jit(solution)/shard_map/ppermute | solution.py:401
  7.8 12.4 %collective-permute-start.2 = (bf16[128,768]{1,0:T(8,128)(2,1)}, bf16[128,768]{1,0:T(8,128)(2,1)S(1)}, u32[]{:S(2)}, u32[]{:S(2)}) collective-permute-start(bf16[128,768]{1,0:T(8,128)(2,1)} %get-tuple-element.44.refs_0_), channel_id=1, source_target_pairs={{0,24},{8,0},{16,8},{24,16},{32,56},{40,32},{48,40},{56,48},{64,88... | collective-permute-start | bytes 589832 | tf_op jit(solution)/shard_map/ppermute | solution.py:401
  9.7 10.5 %collective-permute-start.5 = (bf16[128,768]{1,0:T(8,128)(2,1)}, bf16[128,768]{1,0:T(8,128)(2,1)S(1)}, u32[]{:S(2)}, u32[]{:S(2)}) collective-permute-start(bf16[128,768]{1,0:T(8,128)(2,1)} %get-tuple-element.45.refs_4_), channel_id=1, source_target_pairs={{0,96},{8,104},{16,112},{24,120},{32,0},{40,8},{48,16},{56,24},{64... | collective-permute-start | bytes 589832 | tf_op jit(solution)/shard_map/ppermute | solution.py:401
  10.6 20.2 %all-to-all-start = ((bf16[4,64,2048]{2,1,0:T(8,128)(2,1)}), bf16[4,64,2048]{2,1,0:T(8,128)(2,1)S(1)}, u32[]{:S(2)}, u32[]{:S(2)}) async-start(bf16[4,64,2048]{2,1,0:T(8,128)(2,1)} %get-tuple-element.49), calls=%async_computation | async-start | bytes 2097152 | tf_op jit(solution)/shard_map/all_to_all | solution.py:466
  15.9 7.4 %copy-start.6 = (bf16[128,768]{1,0:T(8,128)(2,1)}, bf16[128,768]{1,0:T(8,128)(2,1)S(1)}, u32[]{:S(2)}) copy-start(bf16[128,768]{1,0:T(8,128)(2,1)S(1)} %collective-permute-done.1.refs_1_) | copy-start | bytes 589828
  15.9 6.0 %collective-permute-start.3 = (bf16[128,768]{1,0:T(8,128)(2,1)S(1)}, bf16[128,768]{1,0:T(8,128)(2,1)S(1)}, u32[]{:S(2)}, u32[]{:S(2)}) collective-permute-start(bf16[128,768]{1,0:T(8,128)(2,1)S(1)} %collective-permute-done.1.refs_1_), channel_id=1, source_target_pairs={{0,8},{8,16},{16,24},{24,0},{32,40},{40,48},{48,56},{56,32},{64,72... | collective-permute-start | bytes 589832 | tf_op jit(solution)/shard_map/ppermute | solution.py:401
  17.4 5.9 %copy-start.7 = (bf16[128,768]{1,0:T(8,128)(2,1)}, bf16[128,768]{1,0:T(8,128)(2,1)S(1)}, u32[]{:S(2)}) copy-start(bf16[128,768]{1,0:T(8,128)(2,1)S(1)} %collective-permute-done.4.refs_5_) | copy-start | bytes 589828
  17.4 5.9 %collective-permute-start.6 = (bf16[128,768]{1,0:T(8,128)(2,1)S(1)}, bf16[128,768]{1,0:T(8,128)(2,1)}, u32[]{:S(2)}, u32[]{:S(2)}) collective-permute-start(bf16[128,768]{1,0:T(8,128)(2,1)S(1)} %collective-permute-done.4.refs_5_), channel_id=1, source_target_pairs={{0,32},{8,40},{16,48},{24,56},{32,64},{40,72},{48,80},{56,88},{64,... | collective-permute-start | bytes 589832 | tf_op jit(solution)/shard_map/ppermute | solution.py:401
  20.2 3.0 %copy-start.8 = (bf16[128,768]{1,0:T(8,128)(2,1)}, bf16[128,768]{1,0:T(8,128)(2,1)S(1)}, u32[]{:S(2)}) copy-start(bf16[128,768]{1,0:T(8,128)(2,1)S(1)} %collective-permute-done.2.refs_2_) | copy-start | bytes 589828
  20.2 3.0 %copy-start.9 = (bf16[128,768]{1,0:T(8,128)(2,1)}, bf16[128,768]{1,0:T(8,128)(2,1)S(1)}, u32[]{:S(2)}) copy-start(bf16[128,768]{1,0:T(8,128)(2,1)S(1)} %collective-permute-done.5.refs_6_) | copy-start | bytes 589828
  21.8 1.4 %copy-start.10 = (bf16[128,768]{1,0:T(8,128)(2,1)}, bf16[128,768]{1,0:T(8,128)(2,1)S(1)}, u32[]{:S(2)}) copy-start(bf16[128,768]{1,0:T(8,128)(2,1)S(1)} %collective-permute-done.3.refs_3_) | copy-start | bytes 589828
  26.0 17.8 %collective-permute-start.8 = (bf16[512,768]{1,0:T(8,128)(2,1)}, bf16[512,768]{1,0:T(8,128)(2,1)S(1)}, u32[]{:S(2)}, u32[]{:S(2)}) collective-permute-start(bf16[512,768]{1,0:T(8,128)(2,1)} %get-tuple-element.73.refs_12_), channel_id=1, source_target_pairs={{0,8},{8,16},{16,24},{24,0},{32,40},{40,48},{48,56},{56,32},{64,72... | collective-permute-start | bytes 2359304 | tf_op jit(solution)/shard_map/ppermute | solution.py:401
  28.1 17.8 %collective-permute-start.7 = (bf16[512,768]{1,0:T(8,128)(2,1)}, bf16[512,768]{1,0:T(8,128)(2,1)}, u32[]{:S(2)}, u32[]{:S(2)}) collective-permute-start(bf16[512,768]{1,0:T(8,128)(2,1)} %get-tuple-element.69.refs_8_), channel_id=1, source_target_pairs={{0,32},{8,40},{16,48},{24,56},{32,64},{40,72},{48,80},{56,88},{64,... | collective-permute-start | bytes 2359304 | tf_op jit(solution)/shard_map/ppermute | solution.py:401
  29.9 25.4 %collective-permute-start.12 = (bf16[512,768]{1,0:T(8,128)(2,1)}, bf16[512,768]{1,0:T(8,128)(2,1)}, u32[]{:S(2)}, u32[]{:S(2)}) collective-permute-start(bf16[512,768]{1,0:T(8,128)(2,1)} %get-tuple-element.73.refs_12_), channel_id=1, source_target_pairs={{0,24},{8,0},{16,8},{24,16},{32,56},{40,32},{48,40},{56,48},{64,88... | collective-permute-start | bytes 2359304 | tf_op jit(solution)/shard_map/ppermute | solution.py:401
  29.9 25.4 %collective-permute-start.11 = (bf16[512,768]{1,0:T(8,128)(2,1)}, bf16[512,768]{1,0:T(8,128)(2,1)}, u32[]{:S(2)}, u32[]{:S(2)}) collective-permute-start(bf16[512,768]{1,0:T(8,128)(2,1)} %get-tuple-element.69.refs_8_), channel_id=1, source_target_pairs={{0,96},{8,104},{16,112},{24,120},{32,0},{40,8},{48,16},{56,24},{64... | collective-permute-start | bytes 2359304 | tf_op jit(solution)/shard_map/ppermute | solution.py:401
  30.8 1.0 copy-start.4
  31.7 23.0 %copy-start.19 = (s32[16]{0:T(128)S(1)}, s32[16]{0:T(128)}, u32[]{:S(2)}) copy-start(s32[16]{0:T(128)} %param.16) | copy-start | bytes 196
  43.7 20.7 %copy-start.5 = (bf16[512,768]{1,0:T(8,128)(2,1)}, bf16[512,768]{1,0:T(8,128)(2,1)S(1)}, u32[]{:S(2)}) copy-start(bf16[512,768]{1,0:T(8,128)(2,1)S(1)} %collective-permute-done.8.refs_13_) | copy-start | bytes 2359300
  45.8 18.6 %collective-permute-start.22 = (bf16[512,768]{1,0:T(8,128)(2,1)}, bf16[512,768]{1,0:T(8,128)(2,1)}, u32[]{:S(2)}, u32[]{:S(2)}) collective-permute-start(bf16[512,768]{1,0:T(8,128)(2,1)} %collective-permute-done.7.refs_9_), channel_id=1, source_target_pairs={{0,32},{8,40},{16,48},{24,56},{32,64},{40,72},{48,80},{56,88},{64,... | collective-permute-start | bytes 2359304 | tf_op jit(solution)/shard_map/ppermute | solution.py:401
  47.0 17.5 %collective-permute-start.23 = (bf16[512,768]{1,0:T(8,128)(2,1)S(1)}, bf16[512,768]{1,0:T(8,128)(2,1)}, u32[]{:S(2)}, u32[]{:S(2)}) collective-permute-start(bf16[512,768]{1,0:T(8,128)(2,1)S(1)} %collective-permute-done.8.refs_13_), channel_id=1, source_target_pairs={{0,8},{8,16},{16,24},{24,0},{32,40},{40,48},{48,56},{56,32},{64,72... | collective-permute-start | bytes 2359304 | tf_op jit(solution)/shard_map/ppermute | solution.py:401
  48.4 2.1 %collective-permute-start.9 = (bf16[128,2048]{1,0:T(8,128)(2,1)}, bf16[128,2048]{1,0:T(8,128)(2,1)S(1)}, u32[]{:S(2)}, u32[]{:S(2)}) collective-permute-start(bf16[128,2048]{1,0:T(8,128)(2,1)} %get-tuple-element.56), channel_id=1, source_target_pairs={{0,1},{1,0},{2,3},{3,2},{4,5},{5,4},{6,7},{7,6},{8,9},{9,8},{10,11... | collective-permute-start | bytes 1572872 | tf_op jit(solution)/shard_map/ppermute | solution.py:444
  50.6 1.0 copy-start.1
  51.8 5.9 %collective-permute-start.10 = (bf16[32,2048]{1,0:T(8,128)(2,1)S(1)}, bf16[32,2048]{1,0:T(8,128)(2,1)S(1)}, u32[]{:S(2)}, u32[]{:S(2)}) collective-permute-start(bf16[32,2048]{1,0:T(8,128)(2,1)S(1)} %get-tuple-element.59), channel_id=1, source_target_pairs={{0,6},{1,7},{2,0},{3,1},{4,2},{5,3},{6,4},{7,5},{8,14},{9,15},{10,... | collective-permute-start | bytes 393224 | tf_op jit(solution)/shard_map/ppermute | solution.py:448
  64.5 17.9 %copy-start = (bf16[32,2048]{1,0:T(8,128)(2,1)S(1)}, bf16[32,2048]{1,0:T(8,128)(2,1)}, u32[]{:S(2)}) copy-start(bf16[32,2048]{1,0:T(8,128)(2,1)} %refs_0_.3) | copy-start | bytes 393220
  64.5 68.4 %all-to-all-start.1 = ((bf16[16,256,512]{2,1,0:T(8,128)(2,1)}), bf16[16,256,512]{2,1,0:T(8,128)(2,1)}, u32[]{:S(2)}, u32[]{:S(2)}) async-start(bf16[16,256,512]{2,1,0:T(8,128)(2,1)} %fresh_states.1), calls=%async_computation.1 | async-start | bytes 8388608 | tf_op jit(solution)/shard_map/all_to_all | solution.py:509
  73.1 7.5 %collective-permute-start.13 = (bf16[32,2048]{1,0:T(8,128)(2,1)S(1)}, bf16[32,2048]{1,0:T(8,128)(2,1)S(1)}, u32[]{:S(2)}, u32[]{:S(2)}) collective-permute-start(bf16[32,2048]{1,0:T(8,128)(2,1)S(1)} %get-tuple-element.61), channel_id=1, source_target_pairs={{0,4},{1,5},{2,6},{3,7},{4,0},{5,1},{6,2},{7,3},{8,12},{9,13},{10,... | collective-permute-start | bytes 393224 | tf_op jit(solution)/shard_map/ppermute | solution.py:448
  75.9 6.5 %collective-permute-start.14 = (bf16[32,2048]{1,0:T(8,128)(2,1)S(1)}, bf16[32,2048]{1,0:T(8,128)(2,1)S(1)}, u32[]{:S(2)}, u32[]{:S(2)}) collective-permute-start(bf16[32,2048]{1,0:T(8,128)(2,1)S(1)} %get-tuple-element.62), channel_id=1, source_target_pairs={{0,2},{1,3},{2,4},{3,5},{4,6},{5,7},{6,0},{7,1},{8,10},{9,11},{10,... | collective-permute-start | bytes 393224 | tf_op jit(solution)/shard_map/ppermute | solution.py:448
  83.6 10.9 %copy-start.3 = (bf16[32,2048]{1,0:T(8,128)(2,1)}, bf16[32,2048]{1,0:T(8,128)(2,1)S(1)}, u32[]{:S(2)}) copy-start(bf16[32,2048]{1,0:T(8,128)(2,1)S(1)} %get-tuple-element.64.refs_0_) | copy-start | bytes 393220
  83.6 6.0 %collective-permute-start.17 = (bf16[32,2048]{1,0:T(8,128)(2,1)S(1)}, bf16[32,2048]{1,0:T(8,128)(2,1)S(1)}, u32[]{:S(2)}, u32[]{:S(2)}) collective-permute-start(bf16[32,2048]{1,0:T(8,128)(2,1)S(1)} %get-tuple-element.64.refs_0_), channel_id=1, source_target_pairs={{0,6},{1,7},{2,0},{3,1},{4,2},{5,3},{6,4},{7,5},{8,14},{9,15},{10,... | collective-permute-start | bytes 393224 | tf_op jit(solution)/shard_map/ppermute | solution.py:439
  84.5 7.2 %collective-permute-start.16 = (bf16[32,2048]{1,0:T(8,128)(2,1)S(1)}, bf16[32,2048]{1,0:T(8,128)(2,1)S(1)}, u32[]{:S(2)}, u32[]{:S(2)}) collective-permute-start(bf16[32,2048]{1,0:T(8,128)(2,1)S(1)} %get-tuple-element.64.refs_0_), channel_id=1, source_target_pairs={{0,4},{1,5},{2,6},{3,7},{4,0},{5,1},{6,2},{7,3},{8,12},{9,13},{10,... | collective-permute-start | bytes 393224 | tf_op jit(solution)/shard_map/ppermute | solution.py:439
  86.3 6.8 %collective-permute-start.15 = (bf16[32,2048]{1,0:T(8,128)(2,1)S(1)}, bf16[32,2048]{1,0:T(8,128)(2,1)S(1)}, u32[]{:S(2)}, u32[]{:S(2)}) collective-permute-start(bf16[32,2048]{1,0:T(8,128)(2,1)S(1)} %get-tuple-element.64.refs_0_), channel_id=1, source_target_pairs={{0,2},{1,3},{2,4},{3,5},{4,6},{5,7},{6,0},{7,1},{8,10},{9,11},{10,... | collective-permute-start | bytes 393224 | tf_op jit(solution)/shard_map/ppermute | solution.py:439
  87.1 6.0 %collective-permute-start.18 = (bf16[32,2048]{1,0:T(8,128)(2,1)S(1)}, bf16[32,2048]{1,0:T(8,128)(2,1)S(1)}, u32[]{:S(2)}, u32[]{:S(2)}) collective-permute-start(bf16[32,2048]{1,0:T(8,128)(2,1)S(1)} %get-tuple-element.64.refs_0_), channel_id=1, source_target_pairs={{0,1},{1,0},{2,3},{3,2},{4,5},{5,4},{6,7},{7,6},{8,9},{9,8},{10,11... | collective-permute-start | bytes 393224 | tf_op jit(solution)/shard_map/ppermute | solution.py:440
  89.5 4.9 %copy-start.12 = (bf16[32,2048]{1,0:T(8,128)(2,1)}, bf16[32,2048]{1,0:T(8,128)(2,1)S(1)}, u32[]{:S(2)}) copy-start(bf16[32,2048]{1,0:T(8,128)(2,1)S(1)} %collective-permute-done.17.refs_3_) | copy-start | bytes 393220
  89.5 3.6 %collective-permute-start.21 = (bf16[32,2048]{1,0:T(8,128)(2,1)S(1)}, bf16[32,2048]{1,0:T(8,128)(2,1)S(1)}, u32[]{:S(2)}, u32[]{:S(2)}) collective-permute-start(bf16[32,2048]{1,0:T(8,128)(2,1)S(1)} %collective-permute-done.17.refs_3_), channel_id=1, source_target_pairs={{0,1},{1,0},{2,3},{3,2},{4,5},{5,4},{6,7},{7,6},{8,9},{9,8},{10,11... | collective-permute-start | bytes 393224 | tf_op jit(solution)/shard_map/ppermute | solution.py:440
  91.8 2.7 %copy-start.13 = (bf16[32,2048]{1,0:T(8,128)(2,1)}, bf16[32,2048]{1,0:T(8,128)(2,1)S(1)}, u32[]{:S(2)}) copy-start(bf16[32,2048]{1,0:T(8,128)(2,1)S(1)} %collective-permute-done.16.refs_2_) | copy-start | bytes 393220
  91.8 1.4 %collective-permute-start.20 = (bf16[32,2048]{1,0:T(8,128)(2,1)S(1)}, bf16[32,2048]{1,0:T(8,128)(2,1)S(1)}, u32[]{:S(2)}, u32[]{:S(2)}) collective-permute-start(bf16[32,2048]{1,0:T(8,128)(2,1)S(1)} %collective-permute-done.16.refs_2_), channel_id=1, source_target_pairs={{0,1},{1,0},{2,3},{3,2},{4,5},{5,4},{6,7},{7,6},{8,9},{9,8},{10,11... | collective-permute-start | bytes 393224 | tf_op jit(solution)/shard_map/ppermute | solution.py:440
  93.1 1.4 copy-start.14
  93.1 1.3 collective-permute-start.19
  93.1 1.4 copy-start.15
  93.1 1.4 copy-start.16
  93.1 1.3 copy-start.17
  94.5 0.7 copy-start.18
  101.9 2.2 %collective-permute-start.24 = (bf16[128,2048]{1,0:T(8,128)(2,1)}, bf16[128,2048]{1,0:T(8,128)(2,1)S(1)}, u32[]{:S(2)}, u32[]{:S(2)}) collective-permute-start(bf16[128,2048]{1,0:T(8,128)(2,1)} %get-tuple-element.78), channel_id=1, source_target_pairs={{0,1},{1,0},{2,3},{3,2},{4,5},{5,4},{6,7},{7,6},{8,9},{9,8},{10,11... | collective-permute-start | bytes 1572872 | tf_op jit(solution)/shard_map/ppermute | solution.py:444
  104.1 1.0 copy-start.2
  105.4 6.4 %collective-permute-start.25 = (bf16[32,2048]{1,0:T(8,128)(2,1)S(1)}, bf16[32,2048]{1,0:T(8,128)(2,1)S(1)}, u32[]{:S(2)}, u32[]{:S(2)}) collective-permute-start(bf16[32,2048]{1,0:T(8,128)(2,1)S(1)} %get-tuple-element.80), channel_id=1, source_target_pairs={{0,6},{1,7},{2,0},{3,1},{4,2},{5,3},{6,4},{7,5},{8,14},{9,15},{10,... | collective-permute-start | bytes 393224 | tf_op jit(solution)/shard_map/ppermute | solution.py:448
  106.6 7.9 %collective-permute-start.26 = (bf16[32,2048]{1,0:T(8,128)(2,1)S(1)}, bf16[32,2048]{1,0:T(8,128)(2,1)S(1)}, u32[]{:S(2)}, u32[]{:S(2)}) collective-permute-start(bf16[32,2048]{1,0:T(8,128)(2,1)S(1)} %get-tuple-element.81), channel_id=1, source_target_pairs={{0,4},{1,5},{2,6},{3,7},{4,0},{5,1},{6,2},{7,3},{8,12},{9,13},{10,... | collective-permute-start | bytes 393224 | tf_op jit(solution)/shard_map/ppermute | solution.py:448
  107.8 8.3 %collective-permute-start.27 = (bf16[32,2048]{1,0:T(8,128)(2,1)S(1)}, bf16[32,2048]{1,0:T(8,128)(2,1)S(1)}, u32[]{:S(2)}, u32[]{:S(2)}) collective-permute-start(bf16[32,2048]{1,0:T(8,128)(2,1)S(1)} %get-tuple-element.82), channel_id=1, source_target_pairs={{0,2},{1,3},{2,4},{3,5},{4,6},{5,7},{6,0},{7,1},{8,10},{9,11},{10,... | collective-permute-start | bytes 393224 | tf_op jit(solution)/shard_map/ppermute | solution.py:448

commit v5 on v4

--- a/solution.py
+++ b/solution.py
@@ -301,6 +301,8 @@
 
 
 def widen(x):
+    shape = x.shape
+    x = x.reshape(2 * shape[0], shape[1] // 2, shape[2])
     n = x.shape[0]
     return pl.pallas_call(
         widen_kernel, in_specs=[ANY], out_specs=ANY,
@@ -311,7 +313,7 @@
         ],
         compiler_params=params(62),
         cost_estimate=cost(x.size, x.size * 6), name="widen",
-    )(x)
+    )(x).reshape(shape)
 
 
 def ring_order(me):

time: 138 us -> 138 us (level)
  no operation moved by 1% of the time
where the time goes in v5:
time: 138 us
  waiting for transfers between devices  49 us (36%)
  starting transfers between devices  41.5 us (30%)
  Pallas kernels  36.6 us (27%)
  local copies, waits for them, and re-layouts  5.93 us (4%)
  other arithmetic  3.65 us (3%)
    all_to_all x1, waiting for transfers between devices, per_device(): lax.all_to_all(fresh, 'req', split_axis=0, concat_axis=0, tiled=True)  15.3 us
    ppermute x6, waiting for transfers between devices, reduce_rows(): lax.ppermute(pieces[s], 'mlp', along(-s))  15.2 us
    ppermute x12, starting transfers between devices, hop(): return lax.ppermute(v, 'req', pairs)  13.6 us
    ppermute x6, starting transfers between devices, reduce_rows(): lax.ppermute(pieces[s], 'mlp', along(-s))  10.1 us
    pallas_call x1, Pallas kernels, retention(): pl.pallas_call(body, out_shape=[sds((rows // 2, width), BF), sds((rows //...  10.1 us
    all_to_all x1, starting transfers between devices, per_device(): lax.all_to_all(fresh, 'req', split_axis=0, concat_axis=0, tiled=True)  8.58 us
    ppermute x12, waiting for transfers between devices, hop(): return lax.ppermute(v, 'req', pairs)  7.05 us
    pallas_call x1, Pallas kernels, ffn(): pl.pallas_call(functools.partial(ffn_kernel, rows_in=rows_in), out_shape=...  6.77 us
  transfers between devices with their start and end apart: 30, of which 17 were waited for; matrix products, arithmetic and copies ran while one was open for 4% of the time, Pallas kernels for 21%

profile of v5, /device:TPU:28, one launch (start us, length us, event | category | flops | bytes accessed | tf_op | source)
XLA Modules:
  0.0 137.9 jit_solution(5193564925980077147)
XLA Ops:
  0.6 0.1 collective-permute-start
  0.9 0.9 select_reduce_fusion.1
  1.9 0.6 reshape.159
  2.6 0.6 copy-done.11
  3.3 2.6 %prepare.1 = (bf16[128,768]{1,0:T(8,128)(2,1)}, bf16[128,768]{1,0:T(8,128)(2,1)}, bf16[4,64,2048]{2,1,0:T(8,128)(2,1)}) custom-call(bf16[128,512]{1,0:T(8,128)(2,1)} %refs_0_.2, bf16[128,512]{1,0:T(8,128)(2,1)} %refs_1_.1, bf16[512,128]{1,0:T(8,128)(2,1)} %refs_2_.2, bf16[32,2048]{1,0:T(8,128)(2,1)} %refs_0_.3, bf16[32,2048]{1,0:T(8,128)(2,1)} %copy-done.11), custom_call_target="tpu_custom_call" | custom-call | bytes 2097152 | tf_op jit(solution)/shard_map/prepare/pallas_call | solution.py:52
  5.8 0.3 collective-permute-start.1
  6.1 1.2 collective-permute-start.4
  7.3 0.5 multiply_cosine_fusion
  7.8 1.9 %collective-permute-start.2 = (bf16[128,768]{1,0:T(8,128)(2,1)}, bf16[128,768]{1,0:T(8,128)(2,1)S(1)}, u32[]{:S(2)}, u32[]{:S(2)}) collective-permute-start(bf16[128,768]{1,0:T(8,128)(2,1)} %get-tuple-element.44.refs_0_), channel_id=1, source_target_pairs={{0,24},{8,0},{16,8},{24,16},{32,56},{40,32},{48,40},{56,48},{64,88... | collective-permute-start | bytes 589832 | tf_op jit(solution)/shard_map/ppermute | solution.py:403
  9.7 0.8 collective-permute-start.5
  10.6 5.3 %all-to-all-start = ((bf16[4,64,2048]{2,1,0:T(8,128)(2,1)}), bf16[4,64,2048]{2,1,0:T(8,128)(2,1)S(1)}, u32[]{:S(2)}, u32[]{:S(2)}) async-start(bf16[4,64,2048]{2,1,0:T(8,128)(2,1)} %get-tuple-element.49), calls=%async_computation | async-start | bytes 2097152 | tf_op jit(solution)/shard_map/all_to_all | solution.py:468
  15.9 1.5 %collective-permute-start.3 = (bf16[128,768]{1,0:T(8,128)(2,1)S(1)}, bf16[128,768]{1,0:T(8,128)(2,1)S(1)}, u32[]{:S(2)}, u32[]{:S(2)}) collective-permute-start(bf16[128,768]{1,0:T(8,128)(2,1)S(1)} %collective-permute-done.1.refs_1_), channel_id=1, source_target_pairs={{0,8},{8,16},{16,24},{24,0},{32,40},{40,48},{48,56},{56,32},{64,72... | collective-permute-start | bytes 589832 | tf_op jit(solution)/shard_map/ppermute | solution.py:403
  17.4 1.2 collective-permute-start.6
  18.6 0.7 broadcast_in_dim.44
  19.3 0.1 broadcast_in_dim.45
  19.4 0.8 pad_maximum_fusion.refs_1_
  20.3 1.6 %collective-permute-done.3.refs_3_ = bf16[128,768]{1,0:T(8,128)(2,1)S(1)} collective-permute-done((bf16[128,768]{1,0:T(8,128)(2,1)S(1)}, bf16[128,768]{1,0:T(8,128)(2,1)S(1)}, u32[]{:S(2)}, u32[]{:S(2)}) %collective-permute-start.3) | collective-permute-done | bytes 196640 | tf_op jit(solution)/shard_map/ppermute | solution.py:403
  21.8 1.4 %collective-permute-done.6.refs_7_ = bf16[128,768]{1,0:T(8,128)(2,1)} collective-permute-done((bf16[128,768]{1,0:T(8,128)(2,1)S(1)}, bf16[128,768]{1,0:T(8,128)(2,1)}, u32[]{:S(2)}, u32[]{:S(2)}) %collective-permute-start.6) | collective-permute-done | bytes 196640 | tf_op jit(solution)/shard_map/ppermute | solution.py:403
  23.3 2.7 %join.1 = (bf16[512,768]{1,0:T(8,128)(2,1)}, bf16[512,768]{1,0:T(8,128)(2,1)}) custom-call(bf16[128,768]{1,0:T(8,128)(2,1)} %get-tuple-element.44.refs_0_, bf16[128,768]{1,0:T(8,128)(2,1)} %copy-done.6, bf16[128,768]{1,0:T(8,128)(2,1)} %copy-done.8, bf16[128,768]{1,0:T(8,128)(2,1)} %copy-done.10, bf16[128,768]{1,0:T(8,128)(2,1)} %get-tuple-element.45.refs_4_, ...), custom_call_target="tpu_custom_call" | custom-call | bytes 4194304 | tf_op jit(solution)/shard_map/join/pallas_call | solution.py:426
  26.0 2.1 %collective-permute-start.8 = (bf16[512,768]{1,0:T(8,128)(2,1)}, bf16[512,768]{1,0:T(8,128)(2,1)S(1)}, u32[]{:S(2)}, u32[]{:S(2)}) collective-permute-start(bf16[512,768]{1,0:T(8,128)(2,1)} %get-tuple-element.73.refs_12_), channel_id=1, source_target_pairs={{0,8},{8,16},{16,24},{24,0},{32,40},{40,48},{48,56},{56,32},{64,72... | collective-permute-start | bytes 2359304 | tf_op jit(solution)/shard_map/ppermute | solution.py:403
  28.1 1.2 collective-permute-start.7
  29.3 0.7 pad_add_fusion.place
  29.9 0.8 collective-permute-start.11
  30.8 1.0 copy-done.4
  31.7 10.1 %retention.1 = (bf16[128,2048]{1,0:T(8,128)(2,1)}, bf16[128,2048]{1,0:T(8,128)(2,1)}, bf16[256,256]{1,0:T(8,128)(2,1)}, bf16[256,512]{1,0:T(8,128)(2,1)}) custom-call(s32[4]{0:T(128)} %pad_add_fusion.place, f32[1]{0:T(128)} %bitcast.4.decay, bf16[4,64,2048]{2,1,0:T(8,128)(2,1)} %copy-done.4, f32[256,512]{1,0:T(8,128)} %pad_maximum_fusion.refs_1_, ...), custom_call_target="tpu_custom_call" | custom-call | flops 2147483648 | bytes 20971520 | tf_op jit(solution)/shard_map/retention/pallas_call | solution.py:222
  41.8 1.9 %collective-permute-done.8.refs_13_ = bf16[512,768]{1,0:T(8,128)(2,1)S(1)} collective-permute-done((bf16[512,768]{1,0:T(8,128)(2,1)}, bf16[512,768]{1,0:T(8,128)(2,1)S(1)}, u32[]{:S(2)}, u32[]{:S(2)}) %collective-permute-start.8) | collective-permute-done | bytes 786464 | tf_op jit(solution)/shard_map/ppermute | solution.py:403
  43.7 2.1 %collective-permute-done.7.refs_9_ = bf16[512,768]{1,0:T(8,128)(2,1)} collective-permute-done((bf16[512,768]{1,0:T(8,128)(2,1)}, bf16[512,768]{1,0:T(8,128)(2,1)}, u32[]{:S(2)}, u32[]{:S(2)}) %collective-permute-start.7) | collective-permute-done | bytes 786464 | tf_op jit(solution)/shard_map/ppermute | solution.py:403
  45.8 1.2 collective-permute-start.22
  47.0 1.4 %collective-permute-start.23 = (bf16[512,768]{1,0:T(8,128)(2,1)S(1)}, bf16[512,768]{1,0:T(8,128)(2,1)}, u32[]{:S(2)}, u32[]{:S(2)}) collective-permute-start(bf16[512,768]{1,0:T(8,128)(2,1)S(1)} %collective-permute-done.8.refs_13_), channel_id=1, source_target_pairs={{0,8},{8,16},{16,24},{24,0},{32,40},{40,48},{48,56},{56,32},{64,72... | collective-permute-start | bytes 2359304 | tf_op jit(solution)/shard_map/ppermute | solution.py:403
  48.4 2.1 %collective-permute-done.9.refs_1_ = bf16[128,2048]{1,0:T(8,128)(2,1)S(1)} collective-permute-done((bf16[128,2048]{1,0:T(8,128)(2,1)}, bf16[128,2048]{1,0:T(8,128)(2,1)S(1)}, u32[]{:S(2)}, u32[]{:S(2)}) %collective-permute-start.9) | collective-permute-done | bytes 524320 | tf_op jit(solution)/shard_map/ppermute | solution.py:446
  50.6 1.0 copy-done.1
  51.6 0.2 pair_sum.2
  51.8 2.9 %collective-permute-start.10 = (bf16[32,2048]{1,0:T(8,128)(2,1)S(1)}, bf16[32,2048]{1,0:T(8,128)(2,1)S(1)}, u32[]{:S(2)}, u32[]{:S(2)}) collective-permute-start(bf16[32,2048]{1,0:T(8,128)(2,1)S(1)} %get-tuple-element.59), channel_id=1, source_target_pairs={{0,6},{1,7},{2,0},{3,1},{4,2},{5,3},{6,4},{7,5},{8,14},{9,15},{10,... | collective-permute-start | bytes 393224 | tf_op jit(solution)/shard_map/ppermute | solution.py:450
  54.7 0.6 multiply_exponential_fusion.old
  55.3 2.5 %collective-permute-done.10.refs_2_ = bf16[32,2048]{1,0:T(8,128)(2,1)S(1)} collective-permute-done((bf16[32,2048]{1,0:T(8,128)(2,1)S(1)}, bf16[32,2048]{1,0:T(8,128)(2,1)S(1)}, u32[]{:S(2)}, u32[]{:S(2)}) %collective-permute-start.10) | collective-permute-done | bytes 131104 | tf_op jit(solution)/shard_map/ppermute | solution.py:450
  57.7 6.7 %fresh_states.1 = bf16[16,256,512]{2,1,0:T(8,128)(2,1)} custom-call(s32[4]{0:T(128)} %pad_add_fusion.place, s32[16]{0:T(128)} %owner.1, f32[16]{0:T(128)} %multiply_exponential_fusion.old, f32[16,256,512]{2,1,0:T(8,128)} %bitcast.11, bf16[256,256]{1,0:T(8,128)(2,1)} %get-tuple-element.65.k_h, bf16[256,512]{1,0:T(8,128)(2,1)} %get-tuple-element.66.v_h), custom_call_target="tpu_custom_call" | custom-call | flops 67108864 | bytes 12582912 | tf_op jit(solution)/shard_map/fresh_states/pallas_call | solution.py:273
  64.5 8.6 %all-to-all-start.1 = ((bf16[16,256,512]{2,1,0:T(8,128)(2,1)}), bf16[16,256,512]{2,1,0:T(8,128)(2,1)}, u32[]{:S(2)}, u32[]{:S(2)}) async-start(bf16[16,256,512]{2,1,0:T(8,128)(2,1)} %fresh_states.1), calls=%async_computation.1 | async-start | bytes 8388608 | tf_op jit(solution)/shard_map/all_to_all | solution.py:511
  73.1 2.8 %collective-permute-start.13 = (bf16[32,2048]{1,0:T(8,128)(2,1)S(1)}, bf16[32,2048]{1,0:T(8,128)(2,1)S(1)}, u32[]{:S(2)}, u32[]{:S(2)}) collective-permute-start(bf16[32,2048]{1,0:T(8,128)(2,1)S(1)} %get-tuple-element.61), channel_id=1, source_target_pairs={{0,4},{1,5},{2,6},{3,7},{4,0},{5,1},{6,2},{7,3},{8,12},{9,13},{10,... | collective-permute-start | bytes 393224 | tf_op jit(solution)/shard_map/ppermute | solution.py:450
  75.9 1.8 %collective-permute-start.14 = (bf16[32,2048]{1,0:T(8,128)(2,1)S(1)}, bf16[32,2048]{1,0:T(8,128)(2,1)S(1)}, u32[]{:S(2)}, u32[]{:S(2)}) collective-permute-start(bf16[32,2048]{1,0:T(8,128)(2,1)S(1)} %get-tuple-element.62), channel_id=1, source_target_pairs={{0,2},{1,3},{2,4},{3,5},{4,6},{5,7},{6,0},{7,1},{8,10},{9,11},{10,... | collective-permute-start | bytes 393224 | tf_op jit(solution)/shard_map/ppermute | solution.py:450
  77.7 2.9 %collective-permute-done.13.refs_3_ = bf16[32,2048]{1,0:T(8,128)(2,1)S(1)} collective-permute-done((bf16[32,2048]{1,0:T(8,128)(2,1)S(1)}, bf16[32,2048]{1,0:T(8,128)(2,1)S(1)}, u32[]{:S(2)}, u32[]{:S(2)}) %collective-permute-start.13) | collective-permute-done | bytes 131104 | tf_op jit(solution)/shard_map/ppermute | solution.py:450
  80.6 1.8 %collective-permute-done.14.refs_4_ = bf16[32,2048]{1,0:T(8,128)(2,1)S(1)} collective-permute-done((bf16[32,2048]{1,0:T(8,128)(2,1)S(1)}, bf16[32,2048]{1,0:T(8,128)(2,1)S(1)}, u32[]{:S(2)}, u32[]{:S(2)}) %collective-permute-start.14) | collective-permute-done | bytes 131104 | tf_op jit(solution)/shard_map/ppermute | solution.py:450
  82.4 1.2 residual_rows.1
  83.6 1.0 collective-permute-start.17
  84.5 1.7 %collective-permute-start.16 = (bf16[32,2048]{1,0:T(8,128)(2,1)S(1)}, bf16[32,2048]{1,0:T(8,128)(2,1)S(1)}, u32[]{:S(2)}, u32[]{:S(2)}) collective-permute-start(bf16[32,2048]{1,0:T(8,128)(2,1)S(1)} %get-tuple-element.64.refs_0_), channel_id=1, source_target_pairs={{0,4},{1,5},{2,6},{3,7},{4,0},{5,1},{6,2},{7,3},{8,12},{9,13},{10,... | collective-permute-start | bytes 393224 | tf_op jit(solution)/shard_map/ppermute | solution.py:441
  86.3 0.9 collective-permute-start.15
  87.1 2.4 %collective-permute-done.17.refs_3_ = bf16[32,2048]{1,0:T(8,128)(2,1)S(1)} collective-permute-done((bf16[32,2048]{1,0:T(8,128)(2,1)S(1)}, bf16[32,2048]{1,0:T(8,128)(2,1)S(1)}, u32[]{:S(2)}, u32[]{:S(2)}) %collective-permute-start.17) | collective-permute-done | bytes 131104 | tf_op jit(solution)/shard_map/ppermute | solution.py:441
  89.5 2.2 %collective-permute-done.16.refs_2_ = bf16[32,2048]{1,0:T(8,128)(2,1)S(1)} collective-permute-done((bf16[32,2048]{1,0:T(8,128)(2,1)S(1)}, bf16[32,2048]{1,0:T(8,128)(2,1)S(1)}, u32[]{:S(2)}, u32[]{:S(2)}) %collective-permute-start.16) | collective-permute-done | bytes 131104 | tf_op jit(solution)/shard_map/ppermute | solution.py:441
  91.8 1.3 collective-permute-done.15.refs_1_
  93.2 1.3 collective-permute-done.19.refs_5_
  94.5 0.6 copy-done.18
  95.2 6.8 %feed_forward.1 = (bf16[128,2048]{1,0:T(8,128)(2,1)}, bf16[128,2048]{1,0:T(8,128)(2,1)}) custom-call(s32[4]{0:T(128)} %pad_add_fusion.place, bf16[32,2048]{1,0:T(8,128)(2,1)} %copy-done.3, bf16[32,2048]{1,0:T(8,128)(2,1)} %copy-done.14, bf16[32,2048]{1,0:T(8,128)(2,1)} %copy-done.13, bf16[32,2048]{1,0:T(8,128)(2,1)} %copy-done.12, ...), custom_call_target="tpu_custom_call" | custom-call | flops 1610612736 | bytes 9437184 | tf_op jit(solution)/shard_map/feed_forward/pallas_call | solution.py:379
  101.9 0.2 collective-permute-start.24
  102.1 2.0 %collective-permute-done.24.refs_1_ = bf16[128,2048]{1,0:T(8,128)(2,1)S(1)} collective-permute-done((bf16[128,2048]{1,0:T(8,128)(2,1)}, bf16[128,2048]{1,0:T(8,128)(2,1)S(1)}, u32[]{:S(2)}, u32[]{:S(2)}) %collective-permute-start.24) | collective-permute-done | bytes 524320 | tf_op jit(solution)/shard_map/ppermute | solution.py:446
  104.1 1.0 copy-done.2
  105.2 0.2 pair_sum.3
  105.4 1.2 collective-permute-start.25
  106.6 1.2 collective-permute-start.26
  107.8 0.3 collective-permute-start.27
  108.1 3.7 %collective-permute-done.25.refs_2_ = bf16[32,2048]{1,0:T(8,128)(2,1)S(1)} collective-permute-done((bf16[32,2048]{1,0:T(8,128)(2,1)S(1)}, bf16[32,2048]{1,0:T(8,128)(2,1)S(1)}, u32[]{:S(2)}, u32[]{:S(2)}) %collective-permute-start.25) | collective-permute-done | bytes 131104 | tf_op jit(solution)/shard_map/ppermute | solution.py:450
  111.8 2.6 %collective-permute-done.26.refs_3_ = bf16[32,2048]{1,0:T(8,128)(2,1)S(1)} collective-permute-done((bf16[32,2048]{1,0:T(8,128)(2,1)S(1)}, bf16[32,2048]{1,0:T(8,128)(2,1)S(1)}, u32[]{:S(2)}, u32[]{:S(2)}) %collective-permute-start.26) | collective-permute-done | bytes 131104 | tf_op jit(solution)/shard_map/ppermute | solution.py:450
  114.4 1.7 %collective-permute-done.27.refs_4_ = bf16[32,2048]{1,0:T(8,128)(2,1)S(1)} collective-permute-done((bf16[32,2048]{1,0:T(8,128)(2,1)S(1)}, bf16[32,2048]{1,0:T(8,128)(2,1)S(1)}, u32[]{:S(2)}, u32[]{:S(2)}) %collective-permute-start.27) | collective-permute-done | bytes 131104 | tf_op jit(solution)/shard_map/ppermute | solution.py:450
  116.1 1.5 %final_rows.1 = bf16[32,2048]{1,0:T(8,128)(2,1)} custom-call(f32[32,2048]{1,0:T(8,128)S(1)} %get-tuple-element.63.refs_0_, bf16[32,2048]{1,0:T(8,128)(2,1)S(1)} %get-tuple-element.79.refs_1_, bf16[32,2048]{1,0:T(8,128)(2,1)S(1)} %collective-permute-done.25.refs_2_, bf16[32,2048]{1,0:T(8,128)(2,1)S(1)} %collective-permute-done.26.refs_3_, ...), custom_call_target="tpu_custom_call" | custom-call | bytes 917504 | tf_op jit(solution)/shard_map/final_rows/pallas_call | solution.py:52
  117.6 15.3 %all-to-all-done.1 = bf16[16,256,512]{2,1,0:T(8,128)(2,1)} async-done(((bf16[16,256,512]{2,1,0:T(8,128)(2,1)}), bf16[16,256,512]{2,1,0:T(8,128)(2,1)}, u32[]{:S(2)}, u32[]{:S(2)}) %all-to-all-start.1) | async-done | bytes 4194336 | tf_op jit(solution)/shard_map/all_to_all | solution.py:511
  133.0 4.7 %widen.1 = f32[32,128,512]{2,1,0:T(8,128)} custom-call(bf16[32,128,512]{2,1,0:T(8,128)(2,1)} %bitcast.6.x_h), custom_call_target="tpu_custom_call" | custom-call | flops 2097152 | bytes 12582912 | tf_op jit(solution)/shard_map/widen/pallas_call | solution.py:307
  (61 shorter events, 0.4 us)
Async XLA Ops:
  0.6 2.0 %collective-permute-start = (bf16[32,2048]{1,0:T(8,128)(2,1)}, bf16[32,2048]{1,0:T(8,128)(2,1)S(1)}, u32[]{:S(2)}, u32[]{:S(2)}) collective-permute-start(bf16[32,2048]{1,0:T(8,128)(2,1)} %refs_0_.3), channel_id=1, source_target_pairs={{0,1},{1,0},{2,3},{3,2},{4,5},{5,4},{6,7},{7,6},{8,9},{9,8},{10,11... | collective-permute-start | bytes 393224 | tf_op jit(solution)/shard_map/ppermute | solution.py:466
  2.6 0.7 copy-start.11
  5.8 10.0 %collective-permute-start.1 = (bf16[128,768]{1,0:T(8,128)(2,1)}, bf16[128,768]{1,0:T(8,128)(2,1)S(1)}, u32[]{:S(2)}, u32[]{:S(2)}) collective-permute-start(bf16[128,768]{1,0:T(8,128)(2,1)} %get-tuple-element.44.refs_0_), channel_id=1, source_target_pairs={{0,8},{8,16},{16,24},{24,0},{32,40},{40,48},{48,56},{56,32},{64,72... | collective-permute-start | bytes 589832 | tf_op jit(solution)/shard_map/ppermute | solution.py:403
  6.1 11.2 %collective-permute-start.4 = (bf16[128,768]{1,0:T(8,128)(2,1)}, bf16[128,768]{1,0:T(8,128)(2,1)S(1)}, u32[]{:S(2)}, u32[]{:S(2)}) collective-permute-start(bf16[128,768]{1,0:T(8,128)(2,1)} %get-tuple-element.45.refs_4_), channel_id=1, source_target_pairs={{0,32},{8,40},{16,48},{24,56},{32,64},{40,72},{48,80},{56,88},{64,... | collective-permute-start | bytes 589832 | tf_op jit(solution)/shard_map/ppermute | solution.py:403
  7.8 12.4 %collective-permute-start.2 = (bf16[128,768]{1,0:T(8,128)(2,1)}, bf16[128,768]{1,0:T(8,128)(2,1)S(1)}, u32[]{:S(2)}, u32[]{:S(2)}) collective-permute-start(bf16[128,768]{1,0:T(8,128)(2,1)} %get-tuple-element.44.refs_0_), channel_id=1, source_target_pairs={{0,24},{8,0},{16,8},{24,16},{32,56},{40,32},{48,40},{56,48},{64,88... | collective-permute-start | bytes 589832 | tf_op jit(solution)/shard_map/ppermute | solution.py:403
  9.7 10.5 %collective-permute-start.5 = (bf16[128,768]{1,0:T(8,128)(2,1)}, bf16[128,768]{1,0:T(8,128)(2,1)S(1)}, u32[]{:S(2)}, u32[]{:S(2)}) collective-permute-start(bf16[128,768]{1,0:T(8,128)(2,1)} %get-tuple-element.45.refs_4_), channel_id=1, source_target_pairs={{0,96},{8,104},{16,112},{24,120},{32,0},{40,8},{48,16},{56,24},{64... | collective-permute-start | bytes 589832 | tf_op jit(solution)/shard_map/ppermute | solution.py:403
  10.6 20.2 %all-to-all-start = ((bf16[4,64,2048]{2,1,0:T(8,128)(2,1)}), bf16[4,64,2048]{2,1,0:T(8,128)(2,1)S(1)}, u32[]{:S(2)}, u32[]{:S(2)}) async-start(bf16[4,64,2048]{2,1,0:T(8,128)(2,1)} %get-tuple-element.49), calls=%async_computation | async-start | bytes 2097152 | tf_op jit(solution)/shard_map/all_to_all | solution.py:468
  15.9 7.4 %copy-start.6 = (bf16[128,768]{1,0:T(8,128)(2,1)}, bf16[128,768]{1,0:T(8,128)(2,1)S(1)}, u32[]{:S(2)}) copy-start(bf16[128,768]{1,0:T(8,128)(2,1)S(1)} %collective-permute-done.1.refs_1_) | copy-start | bytes 589828
  15.9 6.0 %collective-permute-start.3 = (bf16[128,768]{1,0:T(8,128)(2,1)S(1)}, bf16[128,768]{1,0:T(8,128)(2,1)S(1)}, u32[]{:S(2)}, u32[]{:S(2)}) collective-permute-start(bf16[128,768]{1,0:T(8,128)(2,1)S(1)} %collective-permute-done.1.refs_1_), channel_id=1, source_target_pairs={{0,8},{8,16},{16,24},{24,0},{32,40},{40,48},{48,56},{56,32},{64,72... | collective-permute-start | bytes 589832 | tf_op jit(solution)/shard_map/ppermute | solution.py:403
  17.4 5.9 %copy-start.7 = (bf16[128,768]{1,0:T(8,128)(2,1)}, bf16[128,768]{1,0:T(8,128)(2,1)S(1)}, u32[]{:S(2)}) copy-start(bf16[128,768]{1,0:T(8,128)(2,1)S(1)} %collective-permute-done.4.refs_5_) | copy-start | bytes 589828
  17.4 5.9 %collective-permute-start.6 = (bf16[128,768]{1,0:T(8,128)(2,1)S(1)}, bf16[128,768]{1,0:T(8,128)(2,1)}, u32[]{:S(2)}, u32[]{:S(2)}) collective-permute-start(bf16[128,768]{1,0:T(8,128)(2,1)S(1)} %collective-permute-done.4.refs_5_), channel_id=1, source_target_pairs={{0,32},{8,40},{16,48},{24,56},{32,64},{40,72},{48,80},{56,88},{64,... | collective-permute-start | bytes 589832 | tf_op jit(solution)/shard_map/ppermute | solution.py:403
  20.2 3.0 %copy-start.8 = (bf16[128,768]{1,0:T(8,128)(2,1)}, bf16[128,768]{1,0:T(8,128)(2,1)S(1)}, u32[]{:S(2)}) copy-start(bf16[128,768]{1,0:T(8,128)(2,1)S(1)} %collective-permute-done.2.refs_2_) | copy-start | bytes 589828
  20.2 3.0 %copy-start.9 = (bf16[128,768]{1,0:T(8,128)(2,1)}, bf16[128,768]{1,0:T(8,128)(2,1)S(1)}, u32[]{:S(2)}) copy-start(bf16[128,768]{1,0:T(8,128)(2,1)S(1)} %collective-permute-done.5.refs_6_) | copy-start | bytes 589828
  21.8 1.4 %copy-start.10 = (bf16[128,768]{1,0:T(8,128)(2,1)}, bf16[128,768]{1,0:T(8,128)(2,1)S(1)}, u32[]{:S(2)}) copy-start(bf16[128,768]{1,0:T(8,128)(2,1)S(1)} %collective-permute-done.3.refs_3_) | copy-start | bytes 589828
  26.0 17.8 %collective-permute-start.8 = (bf16[512,768]{1,0:T(8,128)(2,1)}, bf16[512,768]{1,0:T(8,128)(2,1)S(1)}, u32[]{:S(2)}, u32[]{:S(2)}) collective-permute-start(bf16[512,768]{1,0:T(8,128)(2,1)} %get-tuple-element.73.refs_12_), channel_id=1, source_target_pairs={{0,8},{8,16},{16,24},{24,0},{32,40},{40,48},{48,56},{56,32},{64,72... | collective-permute-start | bytes 2359304 | tf_op jit(solution)/shard_map/ppermute | solution.py:403
  28.1 17.8 %collective-permute-start.7 = (bf16[512,768]{1,0:T(8,128)(2,1)}, bf16[512,768]{1,0:T(8,128)(2,1)}, u32[]{:S(2)}, u32[]{:S(2)}) collective-permute-start(bf16[512,768]{1,0:T(8,128)(2,1)} %get-tuple-element.69.refs_8_), channel_id=1, source_target_pairs={{0,32},{8,40},{16,48},{24,56},{32,64},{40,72},{48,80},{56,88},{64,... | collective-permute-start | bytes 2359304 | tf_op jit(solution)/shard_map/ppermute | solution.py:403
  29.9 25.4 %collective-permute-start.12 = (bf16[512,768]{1,0:T(8,128)(2,1)}, bf16[512,768]{1,0:T(8,128)(2,1)}, u32[]{:S(2)}, u32[]{:S(2)}) collective-permute-start(bf16[512,768]{1,0:T(8,128)(2,1)} %get-tuple-element.73.refs_12_), channel_id=1, source_target_pairs={{0,24},{8,0},{16,8},{24,16},{32,56},{40,32},{48,40},{56,48},{64,88... | collective-permute-start | bytes 2359304 | tf_op jit(solution)/shard_map/ppermute | solution.py:403
  29.9 25.4 %collective-permute-start.11 = (bf16[512,768]{1,0:T(8,128)(2,1)}, bf16[512,768]{1,0:T(8,128)(2,1)}, u32[]{:S(2)}, u32[]{:S(2)}) collective-permute-start(bf16[512,768]{1,0:T(8,128)(2,1)} %get-tuple-element.69.refs_8_), channel_id=1, source_target_pairs={{0,96},{8,104},{16,112},{24,120},{32,0},{40,8},{48,16},{56,24},{64... | collective-permute-start | bytes 2359304 | tf_op jit(solution)/shard_map/ppermute | solution.py:403
  30.8 1.0 copy-start.4
  31.7 23.0 %copy-start.19 = (s32[16]{0:T(128)S(1)}, s32[16]{0:T(128)}, u32[]{:S(2)}) copy-start(s32[16]{0:T(128)} %param.16) | copy-start | bytes 196
  43.7 20.7 %copy-start.5 = (bf16[512,768]{1,0:T(8,128)(2,1)}, bf16[512,768]{1,0:T(8,128)(2,1)S(1)}, u32[]{:S(2)}) copy-start(bf16[512,768]{1,0:T(8,128)(2,1)S(1)} %collective-permute-done.8.refs_13_) | copy-start | bytes 2359300
  45.8 18.6 %collective-permute-start.22 = (bf16[512,768]{1,0:T(8,128)(2,1)}, bf16[512,768]{1,0:T(8,128)(2,1)}, u32[]{:S(2)}, u32[]{:S(2)}) collective-permute-start(bf16[512,768]{1,0:T(8,128)(2,1)} %collective-permute-done.7.refs_9_), channel_id=1, source_target_pairs={{0,32},{8,40},{16,48},{24,56},{32,64},{40,72},{48,80},{56,88},{64,... | collective-permute-start | bytes 2359304 | tf_op jit(solution)/shard_map/ppermute | solution.py:403
  47.0 17.5 %collective-permute-start.23 = (bf16[512,768]{1,0:T(8,128)(2,1)S(1)}, bf16[512,768]{1,0:T(8,128)(2,1)}, u32[]{:S(2)}, u32[]{:S(2)}) collective-permute-start(bf16[512,768]{1,0:T(8,128)(2,1)S(1)} %collective-permute-done.8.refs_13_), channel_id=1, source_target_pairs={{0,8},{8,16},{16,24},{24,0},{32,40},{40,48},{48,56},{56,32},{64,72... | collective-permute-start | bytes 2359304 | tf_op jit(solution)/shard_map/ppermute | solution.py:403
  48.4 2.1 %collective-permute-start.9 = (bf16[128,2048]{1,0:T(8,128)(2,1)}, bf16[128,2048]{1,0:T(8,128)(2,1)S(1)}, u32[]{:S(2)}, u32[]{:S(2)}) collective-permute-start(bf16[128,2048]{1,0:T(8,128)(2,1)} %get-tuple-element.56), channel_id=1, source_target_pairs={{0,1},{1,0},{2,3},{3,2},{4,5},{5,4},{6,7},{7,6},{8,9},{9,8},{10,11... | collective-permute-start | bytes 1572872 | tf_op jit(solution)/shard_map/ppermute | solution.py:446
  50.6 1.0 copy-start.1
  51.8 5.9 %collective-permute-start.10 = (bf16[32,2048]{1,0:T(8,128)(2,1)S(1)}, bf16[32,2048]{1,0:T(8,128)(2,1)S(1)}, u32[]{:S(2)}, u32[]{:S(2)}) collective-permute-start(bf16[32,2048]{1,0:T(8,128)(2,1)S(1)} %get-tuple-element.59), channel_id=1, source_target_pairs={{0,6},{1,7},{2,0},{3,1},{4,2},{5,3},{6,4},{7,5},{8,14},{9,15},{10,... | collective-permute-start | bytes 393224 | tf_op jit(solution)/shard_map/ppermute | solution.py:450
  64.5 17.9 %copy-start = (bf16[32,2048]{1,0:T(8,128)(2,1)S(1)}, bf16[32,2048]{1,0:T(8,128)(2,1)}, u32[]{:S(2)}) copy-start(bf16[32,2048]{1,0:T(8,128)(2,1)} %refs_0_.3) | copy-start | bytes 393220
  64.5 68.4 %all-to-all-start.1 = ((bf16[16,256,512]{2,1,0:T(8,128)(2,1)}), bf16[16,256,512]{2,1,0:T(8,128)(2,1)}, u32[]{:S(2)}, u32[]{:S(2)}) async-start(bf16[16,256,512]{2,1,0:T(8,128)(2,1)} %fresh_states.1), calls=%async_computation.1 | async-start | bytes 8388608 | tf_op jit(solution)/shard_map/all_to_all | solution.py:511
  73.1 7.5 %collective-permute-start.13 = (bf16[32,2048]{1,0:T(8,128)(2,1)S(1)}, bf16[32,2048]{1,0:T(8,128)(2,1)S(1)}, u32[]{:S(2)}, u32[]{:S(2)}) collective-permute-start(bf16[32,2048]{1,0:T(8,128)(2,1)S(1)} %get-tuple-element.61), channel_id=1, source_target_pairs={{0,4},{1,5},{2,6},{3,7},{4,0},{5,1},{6,2},{7,3},{8,12},{9,13},{10,... | collective-permute-start | bytes 393224 | tf_op jit(solution)/shard_map/ppermute | solution.py:450
  75.9 6.5 %collective-permute-start.14 = (bf16[32,2048]{1,0:T(8,128)(2,1)S(1)}, bf16[32,2048]{1,0:T(8,128)(2,1)S(1)}, u32[]{:S(2)}, u32[]{:S(2)}) collective-permute-start(bf16[32,2048]{1,0:T(8,128)(2,1)S(1)} %get-tuple-element.62), channel_id=1, source_target_pairs={{0,2},{1,3},{2,4},{3,5},{4,6},{5,7},{6,0},{7,1},{8,10},{9,11},{10,... | collective-permute-start | bytes 393224 | tf_op jit(solution)/shard_map/ppermute | solution.py:450
  83.6 10.9 %copy-start.3 = (bf16[32,2048]{1,0:T(8,128)(2,1)}, bf16[32,2048]{1,0:T(8,128)(2,1)S(1)}, u32[]{:S(2)}) copy-start(bf16[32,2048]{1,0:T(8,128)(2,1)S(1)} %get-tuple-element.64.refs_0_) | copy-start | bytes 393220
  83.6 6.0 %collective-permute-start.17 = (bf16[32,2048]{1,0:T(8,128)(2,1)S(1)}, bf16[32,2048]{1,0:T(8,128)(2,1)S(1)}, u32[]{:S(2)}, u32[]{:S(2)}) collective-permute-start(bf16[32,2048]{1,0:T(8,128)(2,1)S(1)} %get-tuple-element.64.refs_0_), channel_id=1, source_target_pairs={{0,6},{1,7},{2,0},{3,1},{4,2},{5,3},{6,4},{7,5},{8,14},{9,15},{10,... | collective-permute-start | bytes 393224 | tf_op jit(solution)/shard_map/ppermute | solution.py:441
  84.5 7.2 %collective-permute-start.16 = (bf16[32,2048]{1,0:T(8,128)(2,1)S(1)}, bf16[32,2048]{1,0:T(8,128)(2,1)S(1)}, u32[]{:S(2)}, u32[]{:S(2)}) collective-permute-start(bf16[32,2048]{1,0:T(8,128)(2,1)S(1)} %get-tuple-element.64.refs_0_), channel_id=1, source_target_pairs={{0,4},{1,5},{2,6},{3,7},{4,0},{5,1},{6,2},{7,3},{8,12},{9,13},{10,... | collective-permute-start | bytes 393224 | tf_op jit(solution)/shard_map/ppermute | solution.py:441
  86.3 6.8 %collective-permute-start.15 = (bf16[32,2048]{1,0:T(8,128)(2,1)S(1)}, bf16[32,2048]{1,0:T(8,128)(2,1)S(1)}, u32[]{:S(2)}, u32[]{:S(2)}) collective-permute-start(bf16[32,2048]{1,0:T(8,128)(2,1)S(1)} %get-tuple-element.64.refs_0_), channel_id=1, source_target_pairs={{0,2},{1,3},{2,4},{3,5},{4,6},{5,7},{6,0},{7,1},{8,10},{9,11},{10,... | collective-permute-start | bytes 393224 | tf_op jit(solution)/shard_map/ppermute | solution.py:441
  87.1 6.0 %collective-permute-start.18 = (bf16[32,2048]{1,0:T(8,128)(2,1)S(1)}, bf16[32,2048]{1,0:T(8,128)(2,1)S(1)}, u32[]{:S(2)}, u32[]{:S(2)}) collective-permute-start(bf16[32,2048]{1,0:T(8,128)(2,1)S(1)} %get-tuple-element.64.refs_0_), channel_id=1, source_target_pairs={{0,1},{1,0},{2,3},{3,2},{4,5},{5,4},{6,7},{7,6},{8,9},{9,8},{10,11... | collective-permute-start | bytes 393224 | tf_op jit(solution)/shard_map/ppermute | solution.py:442
  89.5 4.9 %copy-start.12 = (bf16[32,2048]{1,0:T(8,128)(2,1)}, bf16[32,2048]{1,0:T(8,128)(2,1)S(1)}, u32[]{:S(2)}) copy-start(bf16[32,2048]{1,0:T(8,128)(2,1)S(1)} %collective-permute-done.17.refs_3_) | copy-start | bytes 393220
  89.5 3.6 %collective-permute-start.21 = (bf16[32,2048]{1,0:T(8,128)(2,1)S(1)}, bf16[32,2048]{1,0:T(8,128)(2,1)S(1)}, u32[]{:S(2)}, u32[]{:S(2)}) collective-permute-start(bf16[32,2048]{1,0:T(8,128)(2,1)S(1)} %collective-permute-done.17.refs_3_), channel_id=1, source_target_pairs={{0,1},{1,0},{2,3},{3,2},{4,5},{5,4},{6,7},{7,6},{8,9},{9,8},{10,11... | collective-permute-start | bytes 393224 | tf_op jit(solution)/shard_map/ppermute | solution.py:442
  91.8 2.7 %copy-start.13 = (bf16[32,2048]{1,0:T(8,128)(2,1)}, bf16[32,2048]{1,0:T(8,128)(2,1)S(1)}, u32[]{:S(2)}) copy-start(bf16[32,2048]{1,0:T(8,128)(2,1)S(1)} %collective-permute-done.16.refs_2_) | copy-start | bytes 393220
  91.8 1.4 %collective-permute-start.20 = (bf16[32,2048]{1,0:T(8,128)(2,1)S(1)}, bf16[32,2048]{1,0:T(8,128)(2,1)S(1)}, u32[]{:S(2)}, u32[]{:S(2)}) collective-permute-start(bf16[32,2048]{1,0:T(8,128)(2,1)S(1)} %collective-permute-done.16.refs_2_), channel_id=1, source_target_pairs={{0,1},{1,0},{2,3},{3,2},{4,5},{5,4},{6,7},{7,6},{8,9},{9,8},{10,11... | collective-permute-start | bytes 393224 | tf_op jit(solution)/shard_map/ppermute | solution.py:442
  93.1 1.4 copy-start.14
  93.1 1.3 collective-permute-start.19
  93.1 1.4 copy-start.15
  93.1 1.4 copy-start.16
  93.1 1.3 copy-start.17
  94.5 0.7 copy-start.18
  101.9 2.2 %collective-permute-start.24 = (bf16[128,2048]{1,0:T(8,128)(2,1)}, bf16[128,2048]{1,0:T(8,128)(2,1)S(1)}, u32[]{:S(2)}, u32[]{:S(2)}) collective-permute-start(bf16[128,2048]{1,0:T(8,128)(2,1)} %get-tuple-element.78), channel_id=1, source_target_pairs={{0,1},{1,0},{2,3},{3,2},{4,5},{5,4},{6,7},{7,6},{8,9},{9,8},{10,11... | collective-permute-start | bytes 1572872 | tf_op jit(solution)/shard_map/ppermute | solution.py:446
  104.1 1.0 copy-start.2
  105.4 6.4 %collective-permute-start.25 = (bf16[32,2048]{1,0:T(8,128)(2,1)S(1)}, bf16[32,2048]{1,0:T(8,128)(2,1)S(1)}, u32[]{:S(2)}, u32[]{:S(2)}) collective-permute-start(bf16[32,2048]{1,0:T(8,128)(2,1)S(1)} %get-tuple-element.80), channel_id=1, source_target_pairs={{0,6},{1,7},{2,0},{3,1},{4,2},{5,3},{6,4},{7,5},{8,14},{9,15},{10,... | collective-permute-start | bytes 393224 | tf_op jit(solution)/shard_map/ppermute | solution.py:450
  106.6 7.9 %collective-permute-start.26 = (bf16[32,2048]{1,0:T(8,128)(2,1)S(1)}, bf16[32,2048]{1,0:T(8,128)(2,1)S(1)}, u32[]{:S(2)}, u32[]{:S(2)}) collective-permute-start(bf16[32,2048]{1,0:T(8,128)(2,1)S(1)} %get-tuple-element.81), channel_id=1, source_target_pairs={{0,4},{1,5},{2,6},{3,7},{4,0},{5,1},{6,2},{7,3},{8,12},{9,13},{10,... | collective-permute-start | bytes 393224 | tf_op jit(solution)/shard_map/ppermute | solution.py:450
  107.8 8.3 %collective-permute-start.27 = (bf16[32,2048]{1,0:T(8,128)(2,1)S(1)}, bf16[32,2048]{1,0:T(8,128)(2,1)S(1)}, u32[]{:S(2)}, u32[]{:S(2)}) collective-permute-start(bf16[32,2048]{1,0:T(8,128)(2,1)S(1)} %get-tuple-element.82), channel_id=1, source_target_pairs={{0,2},{1,3},{2,4},{3,5},{4,6},{5,7},{6,0},{7,1},{8,10},{9,11},{10,... | collective-permute-start | bytes 393224 | tf_op jit(solution)/shard_map/ppermute | solution.py:450

commit v6 on v4

--- a/solution.py
+++ b/solution.py
@@ -503,7 +503,7 @@
     near[0], near[2], (same, other, k, v) = lax.optimization_barrier((near[0], near[2], (same, other, k, v)))
     w_all = [block_a, near[0], near[1], hop(near[0], "x", 1), block_b, near[2], near[3], hop(near[2], "y", 1)]
     sums = reduce_rows(pair_rows(same, other))
-    k, sums[1], near[1], near[3] = lax.optimization_barrier((k, sums[1], near[1], near[3]))
+    k, near[1], near[3] = lax.optimization_barrier((k, near[1], near[3]))
     fresh = fresh_states(place, owner_slot, old, states, k, v)
     fresh, w_all = lax.optimization_barrier((fresh, w_all))
     landed = lax.all_to_all(fresh, "req", split_axis=0, concat_axis=0, tiled=True)

time: 138 us -> 128 us (0.928)
  waiting for transfers between devices: 49 us -> 44 us
  starting transfers between devices: 41.5 us -> 36.7 us
    all_to_all x1, waiting for transfers between devices: 15.3 us -> 0.01 us  [per_device(): lax.all_to_all(fresh, 'req', split_axis=0, concat_axis=0, tiled=True)]
    ppermute x12, waiting for transfers between devices: 7.05 us -> 14.6 us  [hop(): return lax.ppermute(v, 'req', pairs)]
    ppermute x6, starting transfers between devices: 10.1 us -> 6.6 us  [reduce_rows(): lax.ppermute(pieces[s], 'mlp', along(-s))]
    ppermute x3, waiting for transfers between devices: 5.97 us -> 7.85 us  [gather_rows(): mine = [x] + [lax.ppermute(x, 'mlp', along(s)) for s in (1, 2, 3)]]
    ppermute x3, starting transfers between devices: 3.54 us -> 2.13 us  [gather_rows(): mine = [x] + [lax.ppermute(x, 'mlp', along(s)) for s in (1, 2, 3)]]
    unnamed x40 -> x44, local copies, waits for them, and re-layouts: 4.41 us -> 3.39 us
  transfers between devices with their start and end apart: 30 -> 30, of which waited for: 17 -> 18; matrix products, arithmetic and copies ran while one was open for 4% -> 4% of each run, Pallas kernels for 21% -> 23%
where the time goes in v6:
time: 128 us; the launch traced here: 127 us
  waiting for transfers between devices  44 us (34%)
  starting transfers between devices  36.7 us (29%)
  Pallas kernels  36.4 us (28%)
  local copies, waits for them, and re-layouts  4.98 us (4%)
  other arithmetic  3.65 us (3%)
    ppermute x6, waiting for transfers between devices, reduce_rows(): lax.ppermute(pieces[s], 'mlp', along(-s))  16.4 us
    ppermute x12, waiting for transfers between devices, hop(): return lax.ppermute(v, 'req', pairs)  14.6 us
    ppermute x12, starting transfers between devices, hop(): return lax.ppermute(v, 'req', pairs)  13.6 us
    pallas_call x1, Pallas kernels, retention(): pl.pallas_call(body, out_shape=[sds((rows // 2, width), BF), sds((rows //...  10.1 us
    all_to_all x1, starting transfers between devices, per_device(): lax.all_to_all(fresh, 'req', split_axis=0, concat_axis=0, tiled=True)  8.58 us
    ppermute x3, waiting for transfers between devices, gather_rows(): mine = [x] + [lax.ppermute(x, 'mlp', along(s)) for s in (1, 2, 3)]  7.85 us
    pallas_call x1, Pallas kernels, ffn(): pl.pallas_call(functools.partial(ffn_kernel, rows_in=rows_in), out_shape=...  6.77 us
    pallas_call x1, Pallas kernels, fresh_states(): pl.pallas_call(fresh_kernel, in_specs=[SM] * 3 + [ANY] * 3, out_specs=ANY...  6.73 us
  transfers between devices with their start and end apart: 30, of which 18 were waited for; matrix products, arithmetic and copies ran while one was open for 4% of the time, Pallas kernels for 23%

profile of v6, /device:TPU:28, one launch (start us, length us, event | category | flops | bytes accessed | tf_op | source)
XLA Modules:
  0.0 127.0 jit_solution(636358758414905872)
XLA Ops:
  0.6 0.1 collective-permute-start
  0.9 0.9 select_reduce_fusion.1
  1.9 0.7 reshape.159
  2.6 0.6 copy-done.12
  3.3 2.6 %prepare.1 = (bf16[128,768]{1,0:T(8,128)(2,1)}, bf16[128,768]{1,0:T(8,128)(2,1)}, bf16[4,64,2048]{2,1,0:T(8,128)(2,1)}) custom-call(bf16[128,512]{1,0:T(8,128)(2,1)} %refs_0_.2, bf16[128,512]{1,0:T(8,128)(2,1)} %refs_1_.1, bf16[512,128]{1,0:T(8,128)(2,1)} %refs_2_.2, bf16[32,2048]{1,0:T(8,128)(2,1)} %refs_0_.3, bf16[32,2048]{1,0:T(8,128)(2,1)} %copy-done.12), custom_call_target="tpu_custom_call" | custom-call | bytes 2097152 | tf_op jit(solution)/shard_map/prepare/pallas_call | solution.py:52
  5.9 0.3 collective-permute-start.1
  6.1 1.2 collective-permute-start.4
  7.3 0.5 multiply_cosine_fusion
  7.9 1.9 %collective-permute-start.2 = (bf16[128,768]{1,0:T(8,128)(2,1)}, bf16[128,768]{1,0:T(8,128)(2,1)S(1)}, u32[]{:S(2)}, u32[]{:S(2)}) collective-permute-start(bf16[128,768]{1,0:T(8,128)(2,1)} %get-tuple-element.43.refs_0_), channel_id=1, source_target_pairs={{0,24},{8,0},{16,8},{24,16},{32,56},{40,32},{48,40},{56,48},{64,88... | collective-permute-start | bytes 589832 | tf_op jit(solution)/shard_map/ppermute | solution.py:401
  9.8 0.8 collective-permute-start.5
  10.6 5.3 %all-to-all-start = ((bf16[4,64,2048]{2,1,0:T(8,128)(2,1)}), bf16[4,64,2048]{2,1,0:T(8,128)(2,1)S(1)}, u32[]{:S(2)}, u32[]{:S(2)}) async-start(bf16[4,64,2048]{2,1,0:T(8,128)(2,1)} %get-tuple-element.48), calls=%async_computation | async-start | bytes 2097152 | tf_op jit(solution)/shard_map/all_to_all | solution.py:466
  15.9 1.5 %collective-permute-start.3 = (bf16[128,768]{1,0:T(8,128)(2,1)S(1)}, bf16[128,768]{1,0:T(8,128)(2,1)S(1)}, u32[]{:S(2)}, u32[]{:S(2)}) collective-permute-start(bf16[128,768]{1,0:T(8,128)(2,1)S(1)} %collective-permute-done.1.refs_1_), channel_id=1, source_target_pairs={{0,8},{8,16},{16,24},{24,0},{32,40},{40,48},{48,56},{56,32},{64,72... | collective-permute-start | bytes 589832 | tf_op jit(solution)/shard_map/ppermute | solution.py:401
  17.4 1.2 collective-permute-start.6
  18.6 0.8 broadcast_in_dim.44
  19.4 0.1 broadcast_in_dim.45
  19.5 0.8 pad_maximum_fusion.refs_1_
  20.3 1.5 %collective-permute-done.3.refs_3_ = bf16[128,768]{1,0:T(8,128)(2,1)S(1)} collective-permute-done((bf16[128,768]{1,0:T(8,128)(2,1)S(1)}, bf16[128,768]{1,0:T(8,128)(2,1)S(1)}, u32[]{:S(2)}, u32[]{:S(2)}) %collective-permute-start.3) | collective-permute-done | bytes 196640 | tf_op jit(solution)/shard_map/ppermute | solution.py:401
  21.9 1.4 %collective-permute-done.6.refs_7_ = bf16[128,768]{1,0:T(8,128)(2,1)} collective-permute-done((bf16[128,768]{1,0:T(8,128)(2,1)S(1)}, bf16[128,768]{1,0:T(8,128)(2,1)}, u32[]{:S(2)}, u32[]{:S(2)}) %collective-permute-start.6) | collective-permute-done | bytes 196640 | tf_op jit(solution)/shard_map/ppermute | solution.py:401
  23.3 2.7 %join.1 = (bf16[512,768]{1,0:T(8,128)(2,1)}, bf16[512,768]{1,0:T(8,128)(2,1)}) custom-call(bf16[128,768]{1,0:T(8,128)(2,1)} %get-tuple-element.43.refs_0_, bf16[128,768]{1,0:T(8,128)(2,1)} %copy-done.7, bf16[128,768]{1,0:T(8,128)(2,1)} %copy-done.9, bf16[128,768]{1,0:T(8,128)(2,1)} %copy-done.11, bf16[128,768]{1,0:T(8,128)(2,1)} %get-tuple-element.44.refs_4_, ...), custom_call_target="tpu_custom_call" | custom-call | bytes 4194304 | tf_op jit(solution)/shard_map/join/pallas_call | solution.py:424
  26.0 2.1 %collective-permute-start.8 = (bf16[512,768]{1,0:T(8,128)(2,1)}, bf16[512,768]{1,0:T(8,128)(2,1)S(1)}, u32[]{:S(2)}, u32[]{:S(2)}) collective-permute-start(bf16[512,768]{1,0:T(8,128)(2,1)} %get-tuple-element.71.refs_12_), channel_id=1, source_target_pairs={{0,8},{8,16},{16,24},{24,0},{32,40},{40,48},{48,56},{56,32},{64,72... | collective-permute-start | bytes 2359304 | tf_op jit(solution)/shard_map/ppermute | solution.py:401
  28.1 1.2 collective-permute-start.7
  29.3 0.6 pad_add_fusion.place
  30.0 0.8 collective-permute-start.20
  30.8 1.0 copy-done.4
  31.8 10.1 %retention.1 = (bf16[128,2048]{1,0:T(8,128)(2,1)}, bf16[128,2048]{1,0:T(8,128)(2,1)}, bf16[256,256]{1,0:T(8,128)(2,1)}, bf16[256,512]{1,0:T(8,128)(2,1)}) custom-call(s32[4]{0:T(128)} %pad_add_fusion.place, f32[1]{0:T(128)} %bitcast.4.decay, bf16[4,64,2048]{2,1,0:T(8,128)(2,1)} %copy-done.4, f32[256,512]{1,0:T(8,128)} %pad_maximum_fusion.refs_1_, ...), custom_call_target="tpu_custom_call" | custom-call | flops 2147483648 | bytes 20971520 | tf_op jit(solution)/shard_map/retention/pallas_call | solution.py:222
  41.8 1.9 %collective-permute-done.8.refs_13_ = bf16[512,768]{1,0:T(8,128)(2,1)S(1)} collective-permute-done((bf16[512,768]{1,0:T(8,128)(2,1)}, bf16[512,768]{1,0:T(8,128)(2,1)S(1)}, u32[]{:S(2)}, u32[]{:S(2)}) %collective-permute-start.8) | collective-permute-done | bytes 786464 | tf_op jit(solution)/shard_map/ppermute | solution.py:401
  43.8 2.1 %collective-permute-done.7.refs_9_ = bf16[512,768]{1,0:T(8,128)(2,1)} collective-permute-done((bf16[512,768]{1,0:T(8,128)(2,1)}, bf16[512,768]{1,0:T(8,128)(2,1)}, u32[]{:S(2)}, u32[]{:S(2)}) %collective-permute-start.7) | collective-permute-done | bytes 786464 | tf_op jit(solution)/shard_map/ppermute | solution.py:401
  45.9 1.2 collective-permute-start.22
  47.1 1.4 %collective-permute-start.23 = (bf16[512,768]{1,0:T(8,128)(2,1)S(1)}, bf16[512,768]{1,0:T(8,128)(2,1)}, u32[]{:S(2)}, u32[]{:S(2)}) collective-permute-start(bf16[512,768]{1,0:T(8,128)(2,1)S(1)} %collective-permute-done.8.refs_13_), channel_id=1, source_target_pairs={{0,8},{8,16},{16,24},{24,0},{32,40},{40,48},{48,56},{56,32},{64,72... | collective-permute-start | bytes 2359304 | tf_op jit(solution)/shard_map/ppermute | solution.py:401
  48.5 0.6 multiply_exponential_fusion.old
  49.1 6.7 %fresh_states.1 = bf16[16,256,512]{2,1,0:T(8,128)(2,1)} custom-call(s32[4]{0:T(128)} %pad_add_fusion.place, s32[16]{0:T(128)} %owner.1, f32[16]{0:T(128)} %multiply_exponential_fusion.old, f32[16,256,512]{2,1,0:T(8,128)} %bitcast.10, bf16[256,256]{1,0:T(8,128)(2,1)} %get-tuple-element.63.k_h, bf16[256,512]{1,0:T(8,128)(2,1)} %get-tuple-element.64.v_h), custom_call_target="tpu_custom_call" | custom-call | flops 67108864 | bytes 12582912 | tf_op jit(solution)/shard_map/fresh_states/pallas_call | solution.py:273
  55.9 6.8 %collective-permute-done.22.refs_11_ = bf16[512,768]{1,0:T(8,128)(2,1)S(1)} collective-permute-done((bf16[512,768]{1,0:T(8,128)(2,1)}, bf16[512,768]{1,0:T(8,128)(2,1)S(1)}, u32[]{:S(2)}, u32[]{:S(2)}) %collective-permute-start.22) | collective-permute-done | bytes 786464 | tf_op jit(solution)/shard_map/ppermute | solution.py:401
  62.7 0.8 collective-permute-done.23.refs_15_
  63.5 8.6 %all-to-all-start.1 = ((bf16[16,256,512]{2,1,0:T(8,128)(2,1)}), bf16[16,256,512]{2,1,0:T(8,128)(2,1)}, u32[]{:S(2)}, u32[]{:S(2)}) async-start(bf16[16,256,512]{2,1,0:T(8,128)(2,1)} %fresh_states.1), calls=%async_computation.1 | async-start | bytes 8388608 | tf_op jit(solution)/shard_map/all_to_all | solution.py:509
  72.1 1.9 %collective-permute-done.9.refs_1_ = bf16[128,2048]{1,0:T(8,128)(2,1)S(1)} collective-permute-done((bf16[128,2048]{1,0:T(8,128)(2,1)S(1)}, bf16[128,2048]{1,0:T(8,128)(2,1)S(1)}, u32[]{:S(2)}, u32[]{:S(2)}) %collective-permute-start.9) | collective-permute-done | bytes 524320 | tf_op jit(solution)/shard_map/ppermute | solution.py:444
  74.0 0.2 pair_sum.2
  74.3 2.4 %collective-permute-start.10 = (bf16[32,2048]{1,0:T(8,128)(2,1)S(1)}, bf16[32,2048]{1,0:T(8,128)(2,1)S(1)}, u32[]{:S(2)}, u32[]{:S(2)}) collective-permute-start(bf16[32,2048]{1,0:T(8,128)(2,1)S(1)} %get-tuple-element.57), channel_id=1, source_target_pairs={{0,6},{1,7},{2,0},{3,1},{4,2},{5,3},{6,4},{7,5},{8,14},{9,15},{10,... | collective-permute-start | bytes 393224 | tf_op jit(solution)/shard_map/ppermute | solution.py:448
  76.7 0.6 collective-permute-start.11
  77.3 0.9 collective-permute-start.12
  78.2 4.4 %collective-permute-done.10.refs_2_ = bf16[32,2048]{1,0:T(8,128)(2,1)S(1)} collective-permute-done((bf16[32,2048]{1,0:T(8,128)(2,1)S(1)}, bf16[32,2048]{1,0:T(8,128)(2,1)S(1)}, u32[]{:S(2)}, u32[]{:S(2)}) %collective-permute-start.10) | collective-permute-done | bytes 131104 | tf_op jit(solution)/shard_map/ppermute | solution.py:448
  82.6 2.0 %collective-permute-done.11.refs_3_ = bf16[32,2048]{1,0:T(8,128)(2,1)S(1)} collective-permute-done((bf16[32,2048]{1,0:T(8,128)(2,1)S(1)}, bf16[32,2048]{1,0:T(8,128)(2,1)S(1)}, u32[]{:S(2)}, u32[]{:S(2)}) %collective-permute-start.11) | collective-permute-done | bytes 131104 | tf_op jit(solution)/shard_map/ppermute | solution.py:448
  84.6 1.7 %collective-permute-done.12.refs_4_ = bf16[32,2048]{1,0:T(8,128)(2,1)S(1)} collective-permute-done((bf16[32,2048]{1,0:T(8,128)(2,1)S(1)}, bf16[32,2048]{1,0:T(8,128)(2,1)S(1)}, u32[]{:S(2)}, u32[]{:S(2)}) %collective-permute-start.12) | collective-permute-done | bytes 131104 | tf_op jit(solution)/shard_map/ppermute | solution.py:448
  86.3 1.2 residual_rows.1
  87.4 0.6 collective-permute-start.15
  88.1 0.6 collective-permute-start.14
  88.7 0.9 collective-permute-start.13
  89.6 4.3 %collective-permute-done.15.refs_3_ = bf16[32,2048]{1,0:T(8,128)(2,1)S(1)} collective-permute-done((bf16[32,2048]{1,0:T(8,128)(2,1)S(1)}, bf16[32,2048]{1,0:T(8,128)(2,1)S(1)}, u32[]{:S(2)}, u32[]{:S(2)}) %collective-permute-start.15) | collective-permute-done | bytes 131104 | tf_op jit(solution)/shard_map/ppermute | solution.py:439
  93.9 1.6 %collective-permute-done.14.refs_2_ = bf16[32,2048]{1,0:T(8,128)(2,1)S(1)} collective-permute-done((bf16[32,2048]{1,0:T(8,128)(2,1)S(1)}, bf16[32,2048]{1,0:T(8,128)(2,1)S(1)}, u32[]{:S(2)}, u32[]{:S(2)}) %collective-permute-start.14) | collective-permute-done | bytes 131104 | tf_op jit(solution)/shard_map/ppermute | solution.py:439
  95.5 1.9 %collective-permute-done.13.refs_1_ = bf16[32,2048]{1,0:T(8,128)(2,1)S(1)} collective-permute-done((bf16[32,2048]{1,0:T(8,128)(2,1)S(1)}, bf16[32,2048]{1,0:T(8,128)(2,1)S(1)}, u32[]{:S(2)}, u32[]{:S(2)}) %collective-permute-start.13) | collective-permute-done | bytes 131104 | tf_op jit(solution)/shard_map/ppermute | solution.py:439
  97.4 0.1 collective-permute-start.17
  97.6 1.2 collective-permute-done.17.refs_5_
  98.8 0.6 copy-done.19
  99.5 6.8 %feed_forward.1 = (bf16[128,2048]{1,0:T(8,128)(2,1)}, bf16[128,2048]{1,0:T(8,128)(2,1)}) custom-call(s32[4]{0:T(128)} %pad_add_fusion.place, bf16[32,2048]{1,0:T(8,128)(2,1)} %copy-done.3, bf16[32,2048]{1,0:T(8,128)(2,1)} %copy-done.15, bf16[32,2048]{1,0:T(8,128)(2,1)} %copy-done.14, bf16[32,2048]{1,0:T(8,128)(2,1)} %copy-done.13, ...), custom_call_target="tpu_custom_call" | custom-call | flops 1610612736 | bytes 9437184 | tf_op jit(solution)/shard_map/feed_forward/pallas_call | solution.py:377
  106.3 0.2 collective-permute-start.24
  106.5 2.0 %collective-permute-done.24.refs_1_ = bf16[128,2048]{1,0:T(8,128)(2,1)S(1)} collective-permute-done((bf16[128,2048]{1,0:T(8,128)(2,1)}, bf16[128,2048]{1,0:T(8,128)(2,1)S(1)}, u32[]{:S(2)}, u32[]{:S(2)}) %collective-permute-start.24) | collective-permute-done | bytes 524320 | tf_op jit(solution)/shard_map/ppermute | solution.py:444
  108.5 1.0 copy-done.2
  109.5 0.2 pair_sum.3
  109.7 1.7 %collective-permute-start.25 = (bf16[32,2048]{1,0:T(8,128)(2,1)S(1)}, bf16[32,2048]{1,0:T(8,128)(2,1)S(1)}, u32[]{:S(2)}, u32[]{:S(2)}) collective-permute-start(bf16[32,2048]{1,0:T(8,128)(2,1)S(1)} %get-tuple-element.78), channel_id=1, source_target_pairs={{0,6},{1,7},{2,0},{3,1},{4,2},{5,3},{6,4},{7,5},{8,14},{9,15},{10,... | collective-permute-start | bytes 393224 | tf_op jit(solution)/shard_map/ppermute | solution.py:448
  111.5 0.9 collective-permute-start.27
  112.4 3.7 %collective-permute-done.25.refs_2_ = bf16[32,2048]{1,0:T(8,128)(2,1)S(1)} collective-permute-done((bf16[32,2048]{1,0:T(8,128)(2,1)S(1)}, bf16[32,2048]{1,0:T(8,128)(2,1)S(1)}, u32[]{:S(2)}, u32[]{:S(2)}) %collective-permute-start.25) | collective-permute-done | bytes 131104 | tf_op jit(solution)/shard_map/ppermute | solution.py:448
  116.1 3.2 %collective-permute-done.26.refs_3_ = bf16[32,2048]{1,0:T(8,128)(2,1)S(1)} collective-permute-done((bf16[32,2048]{1,0:T(8,128)(2,1)S(1)}, bf16[32,2048]{1,0:T(8,128)(2,1)S(1)}, u32[]{:S(2)}, u32[]{:S(2)}) %collective-permute-start.26) | collective-permute-done | bytes 131104 | tf_op jit(solution)/shard_map/ppermute | solution.py:448
  119.4 1.4 %collective-permute-done.27.refs_4_ = bf16[32,2048]{1,0:T(8,128)(2,1)S(1)} collective-permute-done((bf16[32,2048]{1,0:T(8,128)(2,1)S(1)}, bf16[32,2048]{1,0:T(8,128)(2,1)S(1)}, u32[]{:S(2)}, u32[]{:S(2)}) %collective-permute-start.27) | collective-permute-done | bytes 131104 | tf_op jit(solution)/shard_map/ppermute | solution.py:448
  120.8 1.5 %final_rows.1 = bf16[32,2048]{1,0:T(8,128)(2,1)} custom-call(f32[32,2048]{1,0:T(8,128)S(1)} %get-tuple-element.60.refs_0_, bf16[32,2048]{1,0:T(8,128)(2,1)S(1)} %get-tuple-element.77.refs_1_, bf16[32,2048]{1,0:T(8,128)(2,1)S(1)} %collective-permute-done.25.refs_2_, bf16[32,2048]{1,0:T(8,128)(2,1)S(1)} %collective-permute-done.26.refs_3_, ...), custom_call_target="tpu_custom_call" | custom-call | bytes 917504 | tf_op jit(solution)/shard_map/final_rows/pallas_call | solution.py:52
  122.3 4.5 %widen.1 = f32[16,256,512]{2,1,0:T(8,128)} custom-call(bf16[16,256,512]{2,1,0:T(8,128)(2,1)} %all-to-all-done.1.x_h), custom_call_target="tpu_custom_call" | custom-call | flops 2097152 | bytes 12582912 | tf_op jit(solution)/shard_map/widen/pallas_call | solution.py:305
  (65 shorter events, 0.5 us)
Async XLA Ops:
  0.6 2.0 %collective-permute-start = (bf16[32,2048]{1,0:T(8,128)(2,1)}, bf16[32,2048]{1,0:T(8,128)(2,1)S(1)}, u32[]{:S(2)}, u32[]{:S(2)}) collective-permute-start(bf16[32,2048]{1,0:T(8,128)(2,1)} %refs_0_.3), channel_id=1, source_target_pairs={{0,1},{1,0},{2,3},{3,2},{4,5},{5,4},{6,7},{7,6},{8,9},{9,8},{10,11... | collective-permute-start | bytes 393224 | tf_op jit(solution)/shard_map/ppermute | solution.py:464
  2.6 0.7 copy-start.12
  5.9 10.0 %collective-permute-start.1 = (bf16[128,768]{1,0:T(8,128)(2,1)}, bf16[128,768]{1,0:T(8,128)(2,1)S(1)}, u32[]{:S(2)}, u32[]{:S(2)}) collective-permute-start(bf16[128,768]{1,0:T(8,128)(2,1)} %get-tuple-element.43.refs_0_), channel_id=1, source_target_pairs={{0,8},{8,16},{16,24},{24,0},{32,40},{40,48},{48,56},{56,32},{64,72... | collective-permute-start | bytes 589832 | tf_op jit(solution)/shard_map/ppermute | solution.py:401
  6.1 11.2 %collective-permute-start.4 = (bf16[128,768]{1,0:T(8,128)(2,1)}, bf16[128,768]{1,0:T(8,128)(2,1)S(1)}, u32[]{:S(2)}, u32[]{:S(2)}) collective-permute-start(bf16[128,768]{1,0:T(8,128)(2,1)} %get-tuple-element.44.refs_4_), channel_id=1, source_target_pairs={{0,32},{8,40},{16,48},{24,56},{32,64},{40,72},{48,80},{56,88},{64,... | collective-permute-start | bytes 589832 | tf_op jit(solution)/shard_map/ppermute | solution.py:401
  7.9 12.4 %collective-permute-start.2 = (bf16[128,768]{1,0:T(8,128)(2,1)}, bf16[128,768]{1,0:T(8,128)(2,1)S(1)}, u32[]{:S(2)}, u32[]{:S(2)}) collective-permute-start(bf16[128,768]{1,0:T(8,128)(2,1)} %get-tuple-element.43.refs_0_), channel_id=1, source_target_pairs={{0,24},{8,0},{16,8},{24,16},{32,56},{40,32},{48,40},{56,48},{64,88... | collective-permute-start | bytes 589832 | tf_op jit(solution)/shard_map/ppermute | solution.py:401
  9.8 10.6 %collective-permute-start.5 = (bf16[128,768]{1,0:T(8,128)(2,1)}, bf16[128,768]{1,0:T(8,128)(2,1)S(1)}, u32[]{:S(2)}, u32[]{:S(2)}) collective-permute-start(bf16[128,768]{1,0:T(8,128)(2,1)} %get-tuple-element.44.refs_4_), channel_id=1, source_target_pairs={{0,96},{8,104},{16,112},{24,120},{32,0},{40,8},{48,16},{56,24},{64... | collective-permute-start | bytes 589832 | tf_op jit(solution)/shard_map/ppermute | solution.py:401
  10.6 20.2 %all-to-all-start = ((bf16[4,64,2048]{2,1,0:T(8,128)(2,1)}), bf16[4,64,2048]{2,1,0:T(8,128)(2,1)S(1)}, u32[]{:S(2)}, u32[]{:S(2)}) async-start(bf16[4,64,2048]{2,1,0:T(8,128)(2,1)} %get-tuple-element.48), calls=%async_computation | async-start | bytes 2097152 | tf_op jit(solution)/shard_map/all_to_all | solution.py:466
  15.9 7.4 %copy-start.7 = (bf16[128,768]{1,0:T(8,128)(2,1)}, bf16[128,768]{1,0:T(8,128)(2,1)S(1)}, u32[]{:S(2)}) copy-start(bf16[128,768]{1,0:T(8,128)(2,1)S(1)} %collective-permute-done.1.refs_1_) | copy-start | bytes 589828
  15.9 6.0 %collective-permute-start.3 = (bf16[128,768]{1,0:T(8,128)(2,1)S(1)}, bf16[128,768]{1,0:T(8,128)(2,1)S(1)}, u32[]{:S(2)}, u32[]{:S(2)}) collective-permute-start(bf16[128,768]{1,0:T(8,128)(2,1)S(1)} %collective-permute-done.1.refs_1_), channel_id=1, source_target_pairs={{0,8},{8,16},{16,24},{24,0},{32,40},{40,48},{48,56},{56,32},{64,72... | collective-permute-start | bytes 589832 | tf_op jit(solution)/shard_map/ppermute | solution.py:401
  17.4 5.9 %copy-start.8 = (bf16[128,768]{1,0:T(8,128)(2,1)}, bf16[128,768]{1,0:T(8,128)(2,1)S(1)}, u32[]{:S(2)}) copy-start(bf16[128,768]{1,0:T(8,128)(2,1)S(1)} %collective-permute-done.4.refs_5_) | copy-start | bytes 589828
  17.4 5.9 %collective-permute-start.6 = (bf16[128,768]{1,0:T(8,128)(2,1)S(1)}, bf16[128,768]{1,0:T(8,128)(2,1)}, u32[]{:S(2)}, u32[]{:S(2)}) collective-permute-start(bf16[128,768]{1,0:T(8,128)(2,1)S(1)} %collective-permute-done.4.refs_5_), channel_id=1, source_target_pairs={{0,32},{8,40},{16,48},{24,56},{32,64},{40,72},{48,80},{56,88},{64,... | collective-permute-start | bytes 589832 | tf_op jit(solution)/shard_map/ppermute | solution.py:401
  20.3 3.0 %copy-start.9 = (bf16[128,768]{1,0:T(8,128)(2,1)}, bf16[128,768]{1,0:T(8,128)(2,1)S(1)}, u32[]{:S(2)}) copy-start(bf16[128,768]{1,0:T(8,128)(2,1)S(1)} %collective-permute-done.2.refs_2_) | copy-start | bytes 589828
  20.3 3.0 %copy-start.10 = (bf16[128,768]{1,0:T(8,128)(2,1)}, bf16[128,768]{1,0:T(8,128)(2,1)S(1)}, u32[]{:S(2)}) copy-start(bf16[128,768]{1,0:T(8,128)(2,1)S(1)} %collective-permute-done.5.refs_6_) | copy-start | bytes 589828
  21.9 1.4 %copy-start.11 = (bf16[128,768]{1,0:T(8,128)(2,1)}, bf16[128,768]{1,0:T(8,128)(2,1)S(1)}, u32[]{:S(2)}) copy-start(bf16[128,768]{1,0:T(8,128)(2,1)S(1)} %collective-permute-done.3.refs_3_) | copy-start | bytes 589828
  26.0 17.8 %collective-permute-start.8 = (bf16[512,768]{1,0:T(8,128)(2,1)}, bf16[512,768]{1,0:T(8,128)(2,1)S(1)}, u32[]{:S(2)}, u32[]{:S(2)}) collective-permute-start(bf16[512,768]{1,0:T(8,128)(2,1)} %get-tuple-element.71.refs_12_), channel_id=1, source_target_pairs={{0,8},{8,16},{16,24},{24,0},{32,40},{40,48},{48,56},{56,32},{64,72... | collective-permute-start | bytes 2359304 | tf_op jit(solution)/shard_map/ppermute | solution.py:401
  28.1 17.8 %collective-permute-start.7 = (bf16[512,768]{1,0:T(8,128)(2,1)}, bf16[512,768]{1,0:T(8,128)(2,1)}, u32[]{:S(2)}, u32[]{:S(2)}) collective-permute-start(bf16[512,768]{1,0:T(8,128)(2,1)} %get-tuple-element.67.refs_8_), channel_id=1, source_target_pairs={{0,32},{8,40},{16,48},{24,56},{32,64},{40,72},{48,80},{56,88},{64,... | collective-permute-start | bytes 2359304 | tf_op jit(solution)/shard_map/ppermute | solution.py:401
  29.9 19.1 %collective-permute-start.21 = (bf16[512,768]{1,0:T(8,128)(2,1)}, bf16[512,768]{1,0:T(8,128)(2,1)}, u32[]{:S(2)}, u32[]{:S(2)}) collective-permute-start(bf16[512,768]{1,0:T(8,128)(2,1)} %get-tuple-element.71.refs_12_), channel_id=1, source_target_pairs={{0,24},{8,0},{16,8},{24,16},{32,56},{40,32},{48,40},{56,48},{64,88... | collective-permute-start | bytes 2359304 | tf_op jit(solution)/shard_map/ppermute | solution.py:401
  30.0 19.1 %collective-permute-start.20 = (bf16[512,768]{1,0:T(8,128)(2,1)}, bf16[512,768]{1,0:T(8,128)(2,1)}, u32[]{:S(2)}, u32[]{:S(2)}) collective-permute-start(bf16[512,768]{1,0:T(8,128)(2,1)} %get-tuple-element.67.refs_8_), channel_id=1, source_target_pairs={{0,96},{8,104},{16,112},{24,120},{32,0},{40,8},{48,16},{56,24},{64... | collective-permute-start | bytes 2359304 | tf_op jit(solution)/shard_map/ppermute | solution.py:401
  30.8 1.0 copy-start.4
  31.8 16.7 %copy-start.20 = (s32[16]{0:T(128)S(1)}, s32[16]{0:T(128)}, u32[]{:S(2)}) copy-start(s32[16]{0:T(128)} %param.16) | copy-start | bytes 196
  43.8 12.1 %copy-start.5 = (bf16[512,768]{1,0:T(8,128)(2,1)}, bf16[512,768]{1,0:T(8,128)(2,1)S(1)}, u32[]{:S(2)}) copy-start(bf16[512,768]{1,0:T(8,128)(2,1)S(1)} %collective-permute-done.8.refs_13_) | copy-start | bytes 2359300
  45.9 16.8 %collective-permute-start.22 = (bf16[512,768]{1,0:T(8,128)(2,1)}, bf16[512,768]{1,0:T(8,128)(2,1)S(1)}, u32[]{:S(2)}, u32[]{:S(2)}) collective-permute-start(bf16[512,768]{1,0:T(8,128)(2,1)} %collective-permute-done.7.refs_9_), channel_id=1, source_target_pairs={{0,32},{8,40},{16,48},{24,56},{32,64},{40,72},{48,80},{56,88},{64,... | collective-permute-start | bytes 2359304 | tf_op jit(solution)/shard_map/ppermute | solution.py:401
  47.1 16.4 %collective-permute-start.23 = (bf16[512,768]{1,0:T(8,128)(2,1)S(1)}, bf16[512,768]{1,0:T(8,128)(2,1)}, u32[]{:S(2)}, u32[]{:S(2)}) collective-permute-start(bf16[512,768]{1,0:T(8,128)(2,1)S(1)} %collective-permute-done.8.refs_13_), channel_id=1, source_target_pairs={{0,8},{8,16},{16,24},{24,0},{32,40},{40,48},{48,56},{56,32},{64,72... | collective-permute-start | bytes 2359304 | tf_op jit(solution)/shard_map/ppermute | solution.py:401
  55.8 16.2 %copy-start.21 = (bf16[128,2048]{1,0:T(8,128)(2,1)S(1)}, bf16[128,2048]{1,0:T(8,128)(2,1)}, u32[]{:S(2)}) copy-start(bf16[128,2048]{1,0:T(8,128)(2,1)} %get-tuple-element.55) | copy-start | bytes 1572868
  55.8 18.2 %copy-start.1 = (bf16[128,2048]{1,0:T(8,128)(2,1)S(1)}, bf16[128,2048]{1,0:T(8,128)(2,1)}, u32[]{:S(2)}) copy-start(bf16[128,2048]{1,0:T(8,128)(2,1)} %get-tuple-element.54.refs_0_) | copy-start | bytes 1572868
  55.8 30.4 %copy-start = (bf16[32,2048]{1,0:T(8,128)(2,1)S(1)}, bf16[32,2048]{1,0:T(8,128)(2,1)}, u32[]{:S(2)}) copy-start(bf16[32,2048]{1,0:T(8,128)(2,1)} %refs_0_.3) | copy-start | bytes 393220
  62.7 11.6 %copy-start.6 = (bf16[512,768]{1,0:T(8,128)(2,1)}, bf16[512,768]{1,0:T(8,128)(2,1)S(1)}, u32[]{:S(2)}) copy-start(bf16[512,768]{1,0:T(8,128)(2,1)S(1)} %collective-permute-done.22.refs_11_) | copy-start | bytes 2359300
  63.5 58.8 %all-to-all-start.1 = ((bf16[16,256,512]{2,1,0:T(8,128)(2,1)}), bf16[16,256,512]{2,1,0:T(8,128)(2,1)}, u32[]{:S(2)}, u32[]{:S(2)}) async-start(bf16[16,256,512]{2,1,0:T(8,128)(2,1)} %fresh_states.1), calls=%async_computation.1 | async-start | bytes 8388608 | tf_op jit(solution)/shard_map/all_to_all | solution.py:509
  72.1 2.0 %collective-permute-start.9 = (bf16[128,2048]{1,0:T(8,128)(2,1)S(1)}, bf16[128,2048]{1,0:T(8,128)(2,1)S(1)}, u32[]{:S(2)}, u32[]{:S(2)}) collective-permute-start(bf16[128,2048]{1,0:T(8,128)(2,1)S(1)} %copy-done.21), channel_id=1, source_target_pairs={{0,1},{1,0},{2,3},{3,2},{4,5},{5,4},{6,7},{7,6},{8,9},{9,8},{10,11... | collective-permute-start | bytes 1572872 | tf_op jit(solution)/shard_map/ppermute | solution.py:444
  74.3 8.3 %collective-permute-start.10 = (bf16[32,2048]{1,0:T(8,128)(2,1)S(1)}, bf16[32,2048]{1,0:T(8,128)(2,1)S(1)}, u32[]{:S(2)}, u32[]{:S(2)}) collective-permute-start(bf16[32,2048]{1,0:T(8,128)(2,1)S(1)} %get-tuple-element.57), channel_id=1, source_target_pairs={{0,6},{1,7},{2,0},{3,1},{4,2},{5,3},{6,4},{7,5},{8,14},{9,15},{10,... | collective-permute-start | bytes 393224 | tf_op jit(solution)/shard_map/ppermute | solution.py:448
  76.7 7.9 %collective-permute-start.11 = (bf16[32,2048]{1,0:T(8,128)(2,1)S(1)}, bf16[32,2048]{1,0:T(8,128)(2,1)S(1)}, u32[]{:S(2)}, u32[]{:S(2)}) collective-permute-start(bf16[32,2048]{1,0:T(8,128)(2,1)S(1)} %get-tuple-element.58), channel_id=1, source_target_pairs={{0,4},{1,5},{2,6},{3,7},{4,0},{5,1},{6,2},{7,3},{8,12},{9,13},{10,... | collective-permute-start | bytes 393224 | tf_op jit(solution)/shard_map/ppermute | solution.py:448
  77.3 8.9 %collective-permute-start.12 = (bf16[32,2048]{1,0:T(8,128)(2,1)S(1)}, bf16[32,2048]{1,0:T(8,128)(2,1)S(1)}, u32[]{:S(2)}, u32[]{:S(2)}) collective-permute-start(bf16[32,2048]{1,0:T(8,128)(2,1)S(1)} %get-tuple-element.59), channel_id=1, source_target_pairs={{0,2},{1,3},{2,4},{3,5},{4,6},{5,7},{6,0},{7,1},{8,10},{9,11},{10,... | collective-permute-start | bytes 393224 | tf_op jit(solution)/shard_map/ppermute | solution.py:448
  87.4 11.4 %copy-start.3 = (bf16[32,2048]{1,0:T(8,128)(2,1)}, bf16[32,2048]{1,0:T(8,128)(2,1)S(1)}, u32[]{:S(2)}) copy-start(bf16[32,2048]{1,0:T(8,128)(2,1)S(1)} %get-tuple-element.61.refs_0_) | copy-start | bytes 393220
  87.4 6.4 %collective-permute-start.15 = (bf16[32,2048]{1,0:T(8,128)(2,1)S(1)}, bf16[32,2048]{1,0:T(8,128)(2,1)S(1)}, u32[]{:S(2)}, u32[]{:S(2)}) collective-permute-start(bf16[32,2048]{1,0:T(8,128)(2,1)S(1)} %get-tuple-element.61.refs_0_), channel_id=1, source_target_pairs={{0,6},{1,7},{2,0},{3,1},{4,2},{5,3},{6,4},{7,5},{8,14},{9,15},{10,... | collective-permute-start | bytes 393224 | tf_op jit(solution)/shard_map/ppermute | solution.py:439
  88.1 7.4 %collective-permute-start.14 = (bf16[32,2048]{1,0:T(8,128)(2,1)S(1)}, bf16[32,2048]{1,0:T(8,128)(2,1)S(1)}, u32[]{:S(2)}, u32[]{:S(2)}) collective-permute-start(bf16[32,2048]{1,0:T(8,128)(2,1)S(1)} %get-tuple-element.61.refs_0_), channel_id=1, source_target_pairs={{0,4},{1,5},{2,6},{3,7},{4,0},{5,1},{6,2},{7,3},{8,12},{9,13},{10,... | collective-permute-start | bytes 393224 | tf_op jit(solution)/shard_map/ppermute | solution.py:439
  88.7 8.7 %collective-permute-start.13 = (bf16[32,2048]{1,0:T(8,128)(2,1)S(1)}, bf16[32,2048]{1,0:T(8,128)(2,1)S(1)}, u32[]{:S(2)}, u32[]{:S(2)}) collective-permute-start(bf16[32,2048]{1,0:T(8,128)(2,1)S(1)} %get-tuple-element.61.refs_0_), channel_id=1, source_target_pairs={{0,2},{1,3},{2,4},{3,5},{4,6},{5,7},{6,0},{7,1},{8,10},{9,11},{10,... | collective-permute-start | bytes 393224 | tf_op jit(solution)/shard_map/ppermute | solution.py:439
  89.6 8.0 %collective-permute-start.16 = (bf16[32,2048]{1,0:T(8,128)(2,1)S(1)}, bf16[32,2048]{1,0:T(8,128)(2,1)S(1)}, u32[]{:S(2)}, u32[]{:S(2)}) collective-permute-start(bf16[32,2048]{1,0:T(8,128)(2,1)S(1)} %get-tuple-element.61.refs_0_), channel_id=1, source_target_pairs={{0,1},{1,0},{2,3},{3,2},{4,5},{5,4},{6,7},{7,6},{8,9},{9,8},{10,11... | collective-permute-start | bytes 393224 | tf_op jit(solution)/shard_map/ppermute | solution.py:440
  93.8 4.9 %copy-start.13 = (bf16[32,2048]{1,0:T(8,128)(2,1)}, bf16[32,2048]{1,0:T(8,128)(2,1)S(1)}, u32[]{:S(2)}) copy-start(bf16[32,2048]{1,0:T(8,128)(2,1)S(1)} %collective-permute-done.15.refs_3_) | copy-start | bytes 393220
  93.8 3.7 %collective-permute-start.19 = (bf16[32,2048]{1,0:T(8,128)(2,1)S(1)}, bf16[32,2048]{1,0:T(8,128)(2,1)S(1)}, u32[]{:S(2)}, u32[]{:S(2)}) collective-permute-start(bf16[32,2048]{1,0:T(8,128)(2,1)S(1)} %collective-permute-done.15.refs_3_), channel_id=1, source_target_pairs={{0,1},{1,0},{2,3},{3,2},{4,5},{5,4},{6,7},{7,6},{8,9},{9,8},{10,11... | collective-permute-start | bytes 393224 | tf_op jit(solution)/shard_map/ppermute | solution.py:440
  95.5 3.3 %copy-start.14 = (bf16[32,2048]{1,0:T(8,128)(2,1)}, bf16[32,2048]{1,0:T(8,128)(2,1)S(1)}, u32[]{:S(2)}) copy-start(bf16[32,2048]{1,0:T(8,128)(2,1)S(1)} %collective-permute-done.14.refs_2_) | copy-start | bytes 393220
  95.5 2.1 %collective-permute-start.18 = (bf16[32,2048]{1,0:T(8,128)(2,1)S(1)}, bf16[32,2048]{1,0:T(8,128)(2,1)S(1)}, u32[]{:S(2)}, u32[]{:S(2)}) collective-permute-start(bf16[32,2048]{1,0:T(8,128)(2,1)S(1)} %collective-permute-done.14.refs_2_), channel_id=1, source_target_pairs={{0,1},{1,0},{2,3},{3,2},{4,5},{5,4},{6,7},{7,6},{8,9},{9,8},{10,11... | collective-permute-start | bytes 393224 | tf_op jit(solution)/shard_map/ppermute | solution.py:440
  97.4 1.4 %copy-start.15 = (bf16[32,2048]{1,0:T(8,128)(2,1)}, bf16[32,2048]{1,0:T(8,128)(2,1)S(1)}, u32[]{:S(2)}) copy-start(bf16[32,2048]{1,0:T(8,128)(2,1)S(1)} %collective-permute-done.13.refs_1_) | copy-start | bytes 393220
  97.4 1.3 %collective-permute-start.17 = (bf16[32,2048]{1,0:T(8,128)(2,1)S(1)}, bf16[32,2048]{1,0:T(8,128)(2,1)S(1)}, u32[]{:S(2)}, u32[]{:S(2)}) collective-permute-start(bf16[32,2048]{1,0:T(8,128)(2,1)S(1)} %collective-permute-done.13.refs_1_), channel_id=1, source_target_pairs={{0,1},{1,0},{2,3},{3,2},{4,5},{5,4},{6,7},{7,6},{8,9},{9,8},{10,11... | collective-permute-start | bytes 393224 | tf_op jit(solution)/shard_map/ppermute | solution.py:440
  97.6 1.2 copy-start.16
  97.6 1.2 copy-start.17
  97.6 1.2 copy-start.18
  98.8 0.7 copy-start.19
  106.3 2.2 %collective-permute-start.24 = (bf16[128,2048]{1,0:T(8,128)(2,1)}, bf16[128,2048]{1,0:T(8,128)(2,1)S(1)}, u32[]{:S(2)}, u32[]{:S(2)}) collective-permute-start(bf16[128,2048]{1,0:T(8,128)(2,1)} %get-tuple-element.76), channel_id=1, source_target_pairs={{0,1},{1,0},{2,3},{3,2},{4,5},{5,4},{6,7},{7,6},{8,9},{9,8},{10,11... | collective-permute-start | bytes 1572872 | tf_op jit(solution)/shard_map/ppermute | solution.py:444
  108.5 1.0 copy-start.2
  109.7 6.4 %collective-permute-start.25 = (bf16[32,2048]{1,0:T(8,128)(2,1)S(1)}, bf16[32,2048]{1,0:T(8,128)(2,1)S(1)}, u32[]{:S(2)}, u32[]{:S(2)}) collective-permute-start(bf16[32,2048]{1,0:T(8,128)(2,1)S(1)} %get-tuple-element.78), channel_id=1, source_target_pairs={{0,6},{1,7},{2,0},{3,1},{4,2},{5,3},{6,4},{7,5},{8,14},{9,15},{10,... | collective-permute-start | bytes 393224 | tf_op jit(solution)/shard_map/ppermute | solution.py:448
  111.5 7.9 %collective-permute-start.26 = (bf16[32,2048]{1,0:T(8,128)(2,1)S(1)}, bf16[32,2048]{1,0:T(8,128)(2,1)S(1)}, u32[]{:S(2)}, u32[]{:S(2)}) collective-permute-start(bf16[32,2048]{1,0:T(8,128)(2,1)S(1)} %get-tuple-element.79), channel_id=1, source_target_pairs={{0,4},{1,5},{2,6},{3,7},{4,0},{5,1},{6,2},{7,3},{8,12},{9,13},{10,... | collective-permute-start | bytes 393224 | tf_op jit(solution)/shard_map/ppermute | solution.py:448
  111.5 9.3 %collective-permute-start.27 = (bf16[32,2048]{1,0:T(8,128)(2,1)S(1)}, bf16[32,2048]{1,0:T(8,128)(2,1)S(1)}, u32[]{:S(2)}, u32[]{:S(2)}) collective-permute-start(bf16[32,2048]{1,0:T(8,128)(2,1)S(1)} %get-tuple-element.80), channel_id=1, source_target_pairs={{0,2},{1,3},{2,4},{3,5},{4,6},{5,7},{6,0},{7,1},{8,10},{9,11},{10,... | collective-permute-start | bytes 393224 | tf_op jit(solution)/shard_map/ppermute | solution.py:448
